TPU v7x, 32 devices: a whole 2x2x4 slice. The times are simulated.
32 devices in a mesh: sec: 4 (over y, x), blk: 8 (over z, core).
Axes of the slice: x: 2, y: 2, z: 4, core: 2. Of those that a mesh axis runs over, the one named last changes fastest.
Arguments:
- state: float32 [2, 72, 4096], P(None, None, ('sec', 'blk')), may hold values from -6 to 6
- neighbors: int32 [4, 4096], P(None, ('sec', 'blk')), may hold values from 0 to 4095, as said below
- owner: int32 [4096, 1], P(('sec', 'blk')), may hold values from 0 to 31; in each aligned block of 128 rows (0 to 127, 128 to 255, ...) at most 8 rows name the same one
- crm_state: bfloat16 [8192, 9216], P(('sec', 'blk')), may hold values from -6 to 6
- phase_mask: int32 [8192, 4608], P(('sec', 'blk')), may hold values 0 or 1
Outputs:
- new_state: float32 [2, 72, 4096], P(None, None, ('sec', 'blk'))
Inputs may be any that keep to these rules, and one draw needn't show every extreme that they name: `neighbors`: each entry is a column index within 8 of its own column's index, counted cyclically over 4096. Among the columns of one device no owner is named more than 8 times.
All inputs are finite; a program needn't handle non-finite values. No bound on the sum of `phase_mask` on one device may be relied on, other than what follows from the above.
Results may differ from a plain program's by a relative error of at most 0.0003.
Values sent between devices are 32-bit elements; how exact they have to be, the bound alone decides.
No kernel may reach another device: no remote copies, remote signals or barrier semaphores. Data moves between devices by JAX's collectives and lax.ppermute only.
A program may use at most 128 MiB of HBM per device.

v0:
```python
import jax
import jax.numpy as jnp
from jax import lax
from jax.sharding import PartitionSpec as P

SUB = 4
REACH = 8


def extended(array, sides, width):
    for axis, dim in sides:
        size, length = (lax.axis_size(axis), array.shape[dim])
        up = [(i, (i + 1) % size) for i in range(size)]
        down = [(j, i) for i, j in up]
        last = lax.slice_in_dim(array, length - width, length, axis=dim)
        first = lax.slice_in_dim(array, 0, width, axis=dim)
        before = lax.ppermute(last, axis, up)
        after = lax.ppermute(first, axis, down)
        array = jnp.concatenate([before, array, after], axis=dim)
    return array


def condense(temp_col, moist_col, temp_force, moist_force, pert, flags):
    count = pert.shape[0]
    levels = temp_col.shape[1]
    fields = pert.astype(jnp.float32).reshape(count, 2, levels, -1)
    temper = temp_col[:, :, None] + fields[:, 0]
    moisture = moist_col[:, :, None] + fields[:, 1]
    is_ice = flags.reshape(count, levels, -1) == 1
    rate = jnp.where(is_ice, 0.3, 0.7).astype(jnp.float32)
    heat = jnp.where(is_ice, 1.3, 1.0).astype(jnp.float32)
    for substep in range(SUB):
        temper = temper + 0.2 * (jnp.roll(temper, 1, 2) + jnp.roll(temper, -1, 2) - 2.0 * temper)
        moisture = moisture + 0.2 * (
            jnp.roll(moisture, 1, 2) + jnp.roll(moisture, -1, 2) - 2.0 * moisture
        )
        temper = temper + temp_force[:, :, None] / SUB
        moisture = moisture + moist_force[:, :, None] / SUB
        excess = moisture - 0.8 * jnp.exp(0.3 * temper)
        cond = rate * jnp.maximum(excess, 0.0)
        moisture = moisture - cond
        temper = temper + heat * cond
    return (jnp.mean(temper, axis=2) - temp_col, jnp.mean(moisture, axis=2) - moist_col)


def local(state, neighbors, owner, crm_state, phase_mask):
    ndev = lax.axis_size(("sec", "blk"))
    myself = lax.axis_index(("sec", "blk"))
    levels = state.shape[1]
    cdev = state.shape[2]
    total = cdev * ndev
    slots = crm_state.shape[0]
    cap = slots // ndev
    widened = extended(state, ((("sec", "blk"), 2),), REACH)
    first = myself * cdev - REACH
    local_index = jnp.mod(neighbors - first, total)
    near = jnp.zeros_like(state)
    for k in range(4):
        near = near + jnp.take(widened, local_index[k], axis=2)
    dyn = 0.15 * (near - 4.0 * state)
    payload = jnp.concatenate([state, dyn], axis=0).reshape(4 * levels, cdev)
    mine = owner[:, 0]
    order = jnp.arange(cdev, dtype=jnp.int32)
    same = (mine[:, None] == mine[None, :]) & (order[None, :] < order[:, None])
    rank = jnp.sum(same.astype(jnp.int32), axis=1)
    target = mine * cap + rank
    onehot = (target[:, None] == jnp.arange(slots, dtype=jnp.int32)[None, :]).astype(jnp.float32)
    outgoing = lax.dot_general(
        onehot,
        payload,
        (((0,), (1,)), ((), ())),
        precision=lax.Precision.HIGHEST,
        preferred_element_type=jnp.float32,
    )
    arrived = lax.all_to_all(
        outgoing.reshape(ndev, cap * 4 * levels),
        ("sec", "blk"),
        split_axis=0,
        concat_axis=0,
        tiled=True,
    )
    arrived = arrived.reshape(slots, 4, levels)
    tend_temp, tend_moist = condense(
        arrived[:, 0], arrived[:, 1], arrived[:, 2], arrived[:, 3], crm_state, phase_mask
    )
    tends = jnp.stack([tend_temp, tend_moist], axis=1)
    returned = lax.all_to_all(
        tends.reshape(ndev, cap * 2 * levels),
        ("sec", "blk"),
        split_axis=0,
        concat_axis=0,
        tiled=True,
    )
    returned = returned.reshape(slots, 2 * levels)
    column_tend = jnp.dot(
        onehot, returned, precision=lax.Precision.HIGHEST, preferred_element_type=jnp.float32
    )
    column_tend = column_tend.T.reshape(2, levels, cdev)
    return state + dyn + column_tend


def solution(mesh):
    return jax.shard_map(
        local,
        mesh=mesh,
        in_specs=(
            P(None, None, ("sec", "blk")),
            P(None, ("sec", "blk")),
            P(("sec", "blk"), None),
            P(("sec", "blk"), None),
            P(("sec", "blk"), None),
        ),
        out_specs=P(None, None, ("sec", "blk")),
        check_vma=False,
    )
```

profile of v0, /device:TPU:0, one launch (start us, length us, event | category | flops | bytes accessed | tf_op | source)
XLA Modules:
  0.0 199.9 jit_solution(5421056815160143474)
XLA Ops:
  0.0 1.0 copy.42
  1.0 0.5 collective-permute-start
  1.6 6.0 %collective-permute-start.1 = (f32[2,72,8]{1,0,2:T(2,128)S(1)}, f32[2,72,8]{1,0,2:T(2,128)S(1)}, u32[]{:S(2)}, u32[]{:S(2)}) collective-permute-start(f32[2,72,8]{1,0,2:T(2,128)S(1)} %get-tuple-element.64), channel_id=1, source_target_pairs={{1,0},{2,1},{3,2},{4,3},{5,4},{6,5},{7,6},{8,7},{9,8},{10,9},{11,1... | collective-permute-start | bytes 13832 | tf_op jit(solution)/shard_map/ppermute | solution.py:18
  7.5 0.9 convert_reduce_fusion
  8.4 0.7 fusion.48
  9.1 0.7 add_select_fusion
  9.8 6.1 %copy.54 = s32[256,4608]{0,1:T(8,128)} copy(s32[256,4608]{1,0:T(8,128)} %param.11) | data formatting | bytes 9437184 | tf_op args[4]
  15.9 5.4 %broadcast_select_fusion = (f32[256,4608]{0,1:T(8,128)}, pred[256,4608]{0,1:T(8,128)(4,1)S(1)}) fusion(s32[256,4608]{0,1:T(8,128)} %copy.54), kind=kLoop, calls=%fused_computation.60 | loop fusion | flops 2359296 | bytes 10616832 | tf_op jit(solution)/shard_map/jit(_where)/select_n | solution.py:30
  21.3 0.1 pad_maximum_fusion
  21.4 0.7 gather_fusion.3
  22.1 0.1 copy.48
  22.2 0.8 gather_fusion.2
  23.0 0.1 copy.47
  23.1 0.8 gather_fusion.1
  23.8 0.1 copy.46
  23.9 0.8 gather_fusion
  24.7 0.1 copy.45
  24.8 0.4 fusion.42
  25.3 1.3 all_to_all.16
  26.5 2.8 %all-to-all-start = ((f32[32,1,2304]{2,1,0:T(1,128)}), f32[32,1,2304]{2,1,0:T(1,128)S(1)}, u32[]{:S(2)}, u32[]{:S(2)}) async-start(f32[32,1,2304]{2,1,0:T(1,128)} %all_to_all.16), calls=%async_computation | async-start | bytes 589824 | tf_op jit(solution)/shard_map/all_to_all | solution.py:75
  29.3 2.8 %broadcast_select_fusion.1 = f32[256,4608]{0,1:T(8,128)} fusion(pred[256,4608]{0,1:T(8,128)(4,1)S(1)} %get-tuple-element.16), kind=kLoop, calls=%fused_computation.61 | loop fusion | flops 1179648 | bytes 5898240 | tf_op jit(solution)/shard_map/jit(_where)/select_n | solution.py:31
  32.1 6.6 %copy.52 = bf16[256,9216]{0,1:T(8,128)(2,1)} copy(bf16[256,9216]{1,0:T(8,128)(2,1)} %param.10) | data formatting | bytes 9437184 | tf_op args[3]
  38.8 7.3 %convert.1 = f32[256,2,72,64]{0,3,2,1:T(8,128)} convert(bf16[256,2,72,64]{0,3,2,1:T(8,128)(2,1)} %bitcast.78) | non-fusion elementwise | flops 2359296 | bytes 14155776 | tf_op jit(solution)/shard_map/reshape | solution.py:26
  46.0 0.7 reduce
  46.7 0.9 reshape.82
  47.7 0.4 slice_multiply_fusion
  48.1 0.1 copy.61
  48.2 0.1 copy.62
  48.3 5.3 %fusion = (f32[256,72,64]{0,2,1:T(8,128)S(1)}, f32[256,72,64]{0,2,1:T(8,128)S(1)}) fusion(f32[256,2,72,64]{0,3,2,1:T(8,128)} %convert.1, f32[256,72]{0,1:T(8,128)S(1)} %bitcast.80, f32[256,72]{0,1:T(8,128)S(1)} %bitcast.81), kind=kLoop, calls=%fused_computation.5 | loop fusion | flops 2359296 | bytes 19021824 | tf_op jit(solution)/shard_map/add | solution.py:28
  53.6 0.1 fusion.65
  53.7 5.0 %fusion.66 = (f32[256,72,63]{0,2,1:T(8,128)}, f32[256,72,63]{0,2,1:T(8,128)}) fusion(f32[256,72,64]{0,2,1:T(8,128)S(1)} %get-tuple-element.25), kind=kLoop, calls=%fused_computation.116 | loop fusion | bytes 18579456 | tf_op jit(solution)/shard_map/jit(_roll_static)/slice | solution.py:35
  58.7 0.1 fusion.67
  58.9 1.2 copy-done.5
  60.0 4.7 %fusion.68 = (f32[256,72,63]{0,2,1:T(8,128)}, f32[256,72,63]{0,2,1:T(8,128)}) fusion(f32[256,72,64]{0,2,1:T(8,128)S(1)} %get-tuple-element.26), kind=kLoop, calls=%fused_computation.118 | loop fusion | bytes 18579456 | tf_op jit(solution)/shard_map/jit(_roll_static)/slice | solution.py:33
  64.7 0.1 copy.56
  64.8 0.1 copy.53
  64.9 18.1 %multiply_add_fusion.2 = (f32[256,72,64]{0,2,1:T(8,128)S(1)}, f32[256,72,64]{0,2,1:T(8,128)}, f32[256,72,64]{0,2,1:T(8,128)}) fusion(f32[256,72,64]{0,2,1:T(8,128)} %bitcast.72, f32[256,72,64]{0,2,1:T(8,128)} %bitcast.63, f32[256,72]{0,1:T(8,128)S(1)} %copy.53, f32[256,72,64]{0,2,1:T(8,128)} %copy-done.5, f32[256,72,1]{0,2,1:T(1,128)S(1)} %get-tuple-element.56, ...), kind=kLoop, calls=%fused_computation.55 | loop fusion | flops 27131904 | bytes 52051968 | tf_op jit(solution)/shard_map/add | solution.py:42
  83.0 5.4 %fusion.34 = f32[256,72,64]{0,2,1:T(8,128)S(1)} fusion(f32[256,72,64]{0,2,1:T(8,128)} %get-tuple-element.14, f32[256,72,64]{0,2,1:T(8,128)S(1)} %bitcast.66, f32[256,72,64]{0,2,1:T(8,128)} %get-tuple-element.13), kind=kLoop, calls=%fused_computation.57 | loop fusion | flops 7077888 | bytes 18874368 | tf_op jit(solution)/shard_map/sub | solution.py:41
  88.5 0.1 fusion.61
  88.6 5.0 %fusion.62 = (f32[256,72,63]{0,2,1:T(8,128)}, f32[256,72,63]{0,2,1:T(8,128)}) fusion(f32[256,72,64]{0,2,1:T(8,128)S(1)} %fusion.34), kind=kLoop, calls=%fused_computation.112 | loop fusion | bytes 18579456 | tf_op jit(solution)/shard_map/jit(_roll_static)/slice | solution.py:35
  93.5 0.1 fusion.63
  93.6 4.7 %fusion.64 = (f32[256,72,63]{0,2,1:T(8,128)}, f32[256,72,63]{0,2,1:T(8,128)}) fusion(f32[256,72,64]{0,2,1:T(8,128)S(1)} %get-tuple-element.12), kind=kLoop, calls=%fused_computation.114 | loop fusion | bytes 18579456 | tf_op jit(solution)/shard_map/jit(_roll_static)/slice | solution.py:33
  98.3 13.7 %multiply_add_fusion.1 = (f32[256,72,64]{0,2,1:T(8,128)S(1)}, f32[256,72,64]{0,2,1:T(8,128)}) fusion(f32[256,72,64]{0,2,1:T(8,128)} %bitcast.73, f32[256,72,64]{0,2,1:T(8,128)S(1)} %bitcast.67, f32[256,72]{0,1:T(8,128)S(1)} %copy.53, f32[256,72,64]{0,2,1:T(8,128)S(1)} %get-tuple-element.12, f32[256,72,1]{0,2,1:T(1,128)S(1)} %get-tuple-element.48, ...), kind=kLoop, calls=%fused_computation.53 | loop fusion | flops 27131904 | bytes 47333376 | tf_op jit(solution)/shard_map/add | solution.py:42
  112.0 6.8 %fusion.35 = f32[256,72,64]{0,2,1:T(8,128)S(1)} fusion(f32[256,72,64]{0,2,1:T(8,128)} %get-tuple-element.11, f32[256,72,64]{0,2,1:T(8,128)S(1)} %bitcast.68, f32[256,72]{0,1:T(8,128)S(1)} %copy.53, f32[256,72,64]{0,2,1:T(8,128)S(1)} %get-tuple-element.12, f32[256,72,1]{0,2,1:T(1,128)S(1)} %get-tuple-element.48, f32[256,72,63]{0,2,1:T(8,128)} %get-tuple-element.50, ...), kind=kLoop, calls=%fused_computation.58 | loop fusion | flops 16515072 | bytes 28385280 | tf_op jit(solution)/shard_map/sub | solution.py:41
  118.8 2.2 %copy-done.2 = f32[256,72,64]{0,2,1:T(8,128)} copy-done((f32[256,72,64]{0,2,1:T(8,128)}, f32[256,72,64]{0,2,1:T(8,128)S(1)}, u32[]{:S(2)}) %copy-start.2) | copy-done | bytes 4718616
  121.0 0.1 fusion.57
  121.1 9.3 %fusion.58 = (f32[256,72,63]{0,2,1:T(8,128)}, f32[256,72,63]{0,2,1:T(8,128)}) fusion(f32[256,72,64]{0,2,1:T(8,128)} %copy-done.2), kind=kLoop, calls=%fused_computation.108 | loop fusion | bytes 18579456 | tf_op jit(solution)/shard_map/jit(_roll_static)/slice | solution.py:35
  130.4 0.1 fusion.59
  130.5 4.6 %fusion.60 = (f32[256,72,63]{0,2,1:T(8,128)}, f32[256,72,63]{0,2,1:T(8,128)}) fusion(f32[256,72,64]{0,2,1:T(8,128)S(1)} %get-tuple-element.10), kind=kLoop, calls=%fused_computation.110 | loop fusion | bytes 18579456 | tf_op jit(solution)/shard_map/jit(_roll_static)/slice | solution.py:33
  135.1 14.4 %multiply_add_fusion = (f32[256,72,64]{0,2,1:T(8,128)}, f32[256,72,64]{0,2,1:T(8,128)}) fusion(f32[256,72,64]{0,2,1:T(8,128)S(1)} %bitcast.76, f32[256,72,64]{0,2,1:T(8,128)S(1)} %bitcast.69, f32[256,72]{0,1:T(8,128)S(1)} %copy.53, f32[256,72,64]{0,2,1:T(8,128)S(1)} %get-tuple-element.10, f32[256,72,1]{0,2,1:T(1,128)S(1)} %get-tuple-element.40, ...), kind=kLoop, calls=%fused_computation.51 | loop fusion | flops 27131904 | bytes 47333376 | tf_op jit(solution)/shard_map/add | solution.py:42
  149.5 6.8 %fusion.36 = f32[256,72,64]{0,2,1:T(8,128)S(1)} fusion(f32[256,72,64]{0,2,1:T(8,128)} %get-tuple-element.9, f32[256,72,64]{0,2,1:T(8,128)S(1)} %bitcast.70, f32[256,72]{0,1:T(8,128)S(1)} %copy.53, f32[256,72,64]{0,2,1:T(8,128)S(1)} %get-tuple-element.10, f32[256,72,1]{0,2,1:T(1,128)S(1)} %get-tuple-element.40, f32[256,72,63]{0,2,1:T(8,128)} %get-tuple-element.42, ...), kind=kLoop, calls=%fused_computation.59 | loop fusion | flops 16515072 | bytes 28385280 | tf_op jit(solution)/shard_map/sub | solution.py:41
  156.3 2.2 %copy-done.1 = f32[256,72,64]{0,2,1:T(8,128)} copy-done((f32[256,72,64]{0,2,1:T(8,128)}, f32[256,72,64]{0,2,1:T(8,128)S(1)}, u32[]{:S(2)}) %copy-start.1) | copy-done | bytes 4718616
  158.5 0.1 fusion.56
  158.6 9.3 %fusion.55 = (f32[256,72,63]{0,2,1:T(8,128)}, f32[256,72,63]{0,2,1:T(8,128)}) fusion(f32[256,72,64]{0,2,1:T(8,128)} %copy-done.1), kind=kLoop, calls=%fused_computation.105 | loop fusion | bytes 18579456 | tf_op jit(solution)/shard_map/jit(_roll_static)/slice | solution.py:35
  167.9 0.1 fusion.53
  168.0 4.8 %fusion.54 = (f32[256,72,63]{0,2,1:T(8,128)}, f32[256,72,63]{0,2,1:T(8,128)}) fusion(f32[256,72,64]{0,2,1:T(8,128)S(1)} %copy-done), kind=kLoop, calls=%fused_computation.104 | loop fusion | bytes 18579456 | tf_op jit(solution)/shard_map/jit(_roll_static)/slice | solution.py:33
  172.8 10.9 %add_reduce_fusion = (f32[256,72]{0,1:T(8,128)S(1)}, f32[256,72]{0,1:T(8,128)S(1)}) fusion(f32[256,72,64]{0,2,1:T(8,128)S(1)} %bitcast.77, f32[256,72,64]{0,2,1:T(8,128)S(1)} %bitcast.71, f32[256,72]{0,1:T(8,128)S(1)} %copy.53, f32[256,72,64]{0,2,1:T(8,128)S(1)} %copy-done, f32[256,72,1]{0,2,1:T(1,128)S(1)} %get-tuple-element.28, ...), kind=kLoop, calls=%fused_computation.49 | loop fusion | flops 30633984 | bytes 38043648 | tf_op jit(solution)/shard_map/reduce_sum | solution.py:43
  183.8 0.1 copy.57
  183.9 0.5 all_to_all.17
  184.5 13.8 %all_to_all.20 = f32[32,1,1152]{2,1,0:T(1,128)S(1)} all-to-all(f32[32,1,1152]{2,1,0:T(1,128)S(1)} %all_to_all.17), channel_id=1, replica_groups=mesh['sec'=4,'blk'=8] {'sec','blk'}, dimensions={0} | all-to-all | bytes 294912 | tf_op jit(solution)/shard_map/all_to_all | solution.py:87
  198.3 0.3 reduce.1
  198.6 0.2 reshape.85
  198.8 0.1 copy.59
  198.9 0.9 convolution_add_fusion
  (33 shorter events, 0.2 us)
Async XLA Ops:
  1.0 20.3 %collective-permute-start = (f32[2,72,8]{1,0,2:T(2,128)S(1)}, f32[2,72,8]{1,0,2:T(2,128)S(1)}, u32[]{:S(2)}, u32[]{:S(2)}) collective-permute-start(f32[2,72,8]{1,0,2:T(2,128)S(1)} %get-tuple-element.63), channel_id=1, source_target_pairs={{0,1},{1,2},{2,3},{3,4},{4,5},{5,6},{6,7},{7,8},{8,9},{9,10},{10,1... | collective-permute-start | bytes 13832 | tf_op jit(solution)/shard_map/ppermute | solution.py:17
  1.6 19.8 %collective-permute-start.1 = (f32[2,72,8]{1,0,2:T(2,128)S(1)}, f32[2,72,8]{1,0,2:T(2,128)S(1)}, u32[]{:S(2)}, u32[]{:S(2)}) collective-permute-start(f32[2,72,8]{1,0,2:T(2,128)S(1)} %get-tuple-element.64), channel_id=1, source_target_pairs={{1,0},{2,1},{3,2},{4,3},{5,4},{6,5},{7,6},{8,7},{9,8},{10,9},{11,1... | collective-permute-start | bytes 13832 | tf_op jit(solution)/shard_map/ppermute | solution.py:18
  15.9 8.9 %copy-start.6 = (f32[2,72,128]{2,1,0:T(8,128)S(1)}, f32[2,72,128]{2,1,0:T(8,128)}, u32[]{:S(2)}) copy-start(f32[2,72,128]{2,1,0:T(8,128)} %param.7) | copy-start | bytes 221188
  26.5 19.5 %all-to-all-start = ((f32[32,1,2304]{2,1,0:T(1,128)}), f32[32,1,2304]{2,1,0:T(1,128)S(1)}, u32[]{:S(2)}, u32[]{:S(2)}) async-start(f32[32,1,2304]{2,1,0:T(1,128)} %all_to_all.16), calls=%async_computation | async-start | bytes 589824 | tf_op jit(solution)/shard_map/all_to_all | solution.py:75
  53.6 5.1 %copy-start.4 = (f32[256,72,64]{0,2,1:T(8,128)}, f32[256,72,64]{0,2,1:T(8,128)S(1)}, u32[]{:S(2)}) copy-start(f32[256,72,64]{0,2,1:T(8,128)S(1)} %get-tuple-element.25) | copy-start | bytes 14155780
  53.6 6.4 %copy-start.5 = (f32[256,72,64]{0,2,1:T(8,128)}, f32[256,72,64]{0,2,1:T(8,128)S(1)}, u32[]{:S(2)}) copy-start(f32[256,72,64]{0,2,1:T(8,128)S(1)} %get-tuple-element.26) | copy-start | bytes 14155780
  60.0 22.9 %slice-start = ((s8[4718592]{0:T(1024)(128)(4,1)}), s8[524288]{0:T(1024)(128)(4,1)S(1)}, s32[]{:S(2)}) async-start(s8[4718592]{0:T(1024)(128)(4,1)} %bitcast.64), calls=%async_computation.2 | async-start | bytes 1048576
  64.9 18.1 %slice-start.1 = ((s8[4718592]{0:T(1024)(128)(4,1)}), s8[4194304]{0:T(1024)(128)(4,1)S(1)}, s32[]{:S(2)}) async-start(s8[4718592]{0:T(1024)(128)(4,1)} %bitcast.64), calls=%async_computation.3 | async-start | bytes 8388608
  88.4 5.1 %copy-start.3 = (f32[256,72,64]{0,2,1:T(8,128)}, f32[256,72,64]{0,2,1:T(8,128)S(1)}, u32[]{:S(2)}) copy-start(f32[256,72,64]{0,2,1:T(8,128)S(1)} %fusion.34) | copy-start | bytes 14155780
  118.8 2.2 %copy-start.2 = (f32[256,72,64]{0,2,1:T(8,128)}, f32[256,72,64]{0,2,1:T(8,128)S(1)}, u32[]{:S(2)}) copy-start(f32[256,72,64]{0,2,1:T(8,128)S(1)} %fusion.35) | copy-start | bytes 14155780
  121.1 14.0 %slice-start.2 = ((s8[4718592]{0:T(1024)(128)(4,1)}), s8[4194304]{0:T(1024)(128)(4,1)S(1)}, s32[]{:S(2)}) async-start(s8[4718592]{0:T(1024)(128)(4,1)} %bitcast.74), calls=%async_computation.4 | async-start | bytes 8388608
  130.4 4.7 %slice-start.3 = ((s8[4718592]{0:T(1024)(128)(4,1)}), s8[524288]{0:T(1024)(128)(4,1)S(1)}, s32[]{:S(2)}) async-start(s8[4718592]{0:T(1024)(128)(4,1)} %bitcast.74), calls=%async_computation.5 | async-start | bytes 1048576
  156.3 2.2 %copy-start.1 = (f32[256,72,64]{0,2,1:T(8,128)}, f32[256,72,64]{0,2,1:T(8,128)S(1)}, u32[]{:S(2)}) copy-start(f32[256,72,64]{0,2,1:T(8,128)S(1)} %fusion.36) | copy-start | bytes 14155780
  158.6 9.3 %copy-start = (f32[256,72,64]{0,2,1:T(8,128)S(1)}, f32[256,72,64]{0,2,1:T(8,128)}, u32[]{:S(2)}) copy-start(f32[256,72,64]{0,2,1:T(8,128)} %get-tuple-element.8) | copy-start | bytes 14155780
where the time goes:
time: 200 us
  other arithmetic  101 us (50%)
  local copies, waits for them, and re-layouts  74.1 us (37%)
  blocking collectives  13.8 us (7%)
  starting transfers between devices  9.31 us (5%)
    add x3, other arithmetic, condense(): temper = temper + heat * cond  46.1 us
    slice x6, local copies, waits for them, and re-layouts, condense(): jnp.roll(moisture, 1, 2) + jnp.roll(moisture, -1, 2) - 2.0 * moisture  19.6 us
    unnamed x27, local copies, waits for them, and re-layouts  19.4 us
    sub x3, other arithmetic, condense(): moisture = moisture - cond  19.1 us
    slice x8, local copies, waits for them, and re-layouts, condense(): jnp.roll(temper, 1, 2) + jnp.roll(temper, -1, 2) - 2.0 * temper  19.1 us
    all_to_all x1, blocking collectives, local(): lax.all_to_all(tends.reshape(ndev, cap * 2 * levels), ('sec', 'blk'), spl...  13.8 us
    reduce_sum x1, other arithmetic, condense(): jnp.mean(temper, axis=2) - temp_col  10.9 us
    slice x2, local copies, waits for them, and re-layouts, condense(): jnp.roll(moisture, -1, 2)  9.39 us
  transfers between devices with their start and end apart: 3, of which 0 were waited for; matrix products, arithmetic and copies ran while one was open for 15% of the time, Pallas kernels for 0%

commit v1 on v0

v1 whole, which is shorter than its diff:
```python
import functools
import math

import jax
import jax.numpy as jnp
from jax import lax
from jax.experimental import pallas as pl
from jax.experimental.pallas import tpu as pltpu
from jax.sharding import PartitionSpec as P

SUB = 4
REACH = 8
GROUP = 4
AXES = ("sec", "blk")
F32 = jnp.float32
BF16 = jnp.bfloat16
NT = (((1,), (1,)), ((), ()))
NN = (((1,), (0,)), ((), ()))
TN = (((0,), (0,)), ((), ()))
VMEM = pl.BlockSpec(memory_space=pltpu.VMEM)
SMEM = pl.BlockSpec(memory_space=pltpu.SMEM)


def parts_of(x):
    high = x.astype(BF16)
    rest = x - high.astype(F32)
    middle = rest.astype(BF16)
    low = (rest - middle.astype(F32)).astype(BF16)
    return high, middle, low


def select_dot(x, onehot, dims, flip=False):
    total = None
    for part in parts_of(x):
        pair = (onehot, part) if flip else (part, onehot)
        term = lax.dot_general(*pair, dims, preferred_element_type=F32)
        total = term if total is None else total + term
    return total


def pack_kernel(cap, slots, total, first_ref, state_ref, before_ref, after_ref, near_ref, owner_ref, out_ref, dyn_ref, hot_ref):
    rows, cdev = state_ref.shape
    state = state_ref[...]
    index = near_ref[...] - (first_ref[0] - REACH)
    index = jnp.where(index < 0, index + total, index)
    index = jnp.where(index >= total, index - total, index)
    own = lax.broadcasted_iota(jnp.int32, (cdev, cdev), 0) + REACH
    edge = lax.broadcasted_iota(jnp.int32, (REACH, cdev), 0)
    counts = [jnp.zeros((cdev, cdev), F32), jnp.zeros((REACH, cdev), F32), jnp.zeros((REACH, cdev), F32)]
    for k in range(near_ref.shape[0]):
        row = index[k:k + 1, :]
        for i, place in enumerate((own, edge, edge + (REACH + cdev))):
            counts[i] = counts[i] + jnp.where(place == row, 1.0, 0.0)
    counts = [c.astype(BF16) for c in counts]
    near = select_dot(state, counts[0], NN)
    near = near + select_dot(before_ref[...], counts[1], NN)
    near = near + select_dot(after_ref[...], counts[2], NN)
    dyn = 0.15 * (near - 4.0 * state)
    dyn_ref[...] = dyn
    mine = jnp.broadcast_to(owner_ref[...], (cdev, cdev)).astype(F32)
    other = mine.T
    lower = lax.broadcasted_iota(jnp.int32, (cdev, cdev), 0) < lax.broadcasted_iota(jnp.int32, (cdev, cdev), 1)
    rank = jnp.sum(jnp.where((mine == other) & lower, 1.0, 0.0), axis=0, keepdims=True)
    target = owner_ref[...] * cap + rank.astype(jnp.int32)
    hot = jnp.where(lax.broadcasted_iota(jnp.int32, (slots, cdev), 0) == target, 1.0, 0.0).astype(BF16)
    hot_ref[...] = hot
    out_ref[:, 0:rows] = select_dot(state, hot, NT, True)
    out_ref[:, rows:2 * rows] = select_dot(dyn, hot, NT, True)


def prepare_kernel(crmx, ct_ref, cm_ref, mask_ref, yt_ref, ym_ref, rate_ref, both_ref):
    step = pl.program_id(0)
    width = ct_ref.shape[1]
    per = GROUP * crmx
    row = lax.broadcasted_iota(jnp.int32, (per, per), 0)
    col = lax.broadcasted_iota(jnp.int32, (per, per), 1)
    place = row % crmx
    apart = (((place % 8) * (crmx // 8) + place // 8) - col) & (crmx - 1)
    same = (row // crmx) == (col // crmx)
    move = jnp.where(same & (apart == 0), 1.0, 0.0)
    spread = jnp.where(same & ((apart == 1) | (apart == crmx - 1)), 1.0, 3.0 * move)
    move, spread = move.astype(BF16), spread.astype(BF16)
    for q in range(width // per):
        part = slice(q * per, (q + 1) * per)
        to = pl.ds(pl.multiple_of(step * width + q * per, per), per)
        yt_ref[to, :] = lax.dot_general(spread, ct_ref[:, part], NT, preferred_element_type=F32)
        ym_ref[to, :] = lax.dot_general(spread, cm_ref[:, part], NT, preferred_element_type=F32)
        ice = lax.dot_general(move, mask_ref[:, part].astype(F32).astype(BF16), NT, preferred_element_type=F32)
        rate_ref[to, :] = 0.7 - 0.4 * ice
        both_ref[to, :] = 0.7 - 0.31 * ice


def physics_kernel(levels, crmx, arrived_ref, yt_ref, ym_ref, rate_ref, both_ref, out_ref, rows_ref, sums_ref):
    slots = yt_ref.shape[1]
    steps = crmx // 8
    scale = 0.3 * math.log2(math.e)
    shift = [math.log(0.8 * 5.0 ** j) / 0.3 for j in range(SUB + 1)]
    columns = []
    for start in range(0, 4 * levels, 128):
        size = min(128, 4 * levels - start)
        block = arrived_ref[:, start:start + size]
        if size < 128:
            block = jnp.concatenate([block, jnp.zeros((slots, 128 - size), F32)], axis=1)
        columns.append(block.T[:size])
    arrived = jnp.concatenate(columns, axis=0)
    temp, moist, push, wet = [arrived[i * levels:(i + 1) * levels] for i in range(4)]
    push, wet = push * (1.0 / SUB), wet * (1.0 / SUB)
    tables = [5.0 * (temp + push + shift[1]), 5.0 * (moist + wet)]
    for j in range(2, SUB + 1):
        tables += [5.0 ** j * (push + (shift[j] - shift[j - 1])), 5.0 ** j * wet]
    for i, table in enumerate(tables):
        for half in range(slots // 128):
            rows_ref[half, i * levels:(i + 1) * levels] = table[:, half * 128:(half + 1) * 128]

    def unit(level, half):
        lanes = pl.ds(half * 128, 128)
        base = pl.multiple_of(level * crmx, crmx)
        get = lambda ref, k: ref[pl.ds(base + 8 * k, 8), lanes]
        const = lambda i: rows_ref[half, pl.ds(level + i * levels, 8, stride=0), :]
        add_t, add_m = const(0), const(1)
        temp = [get(yt_ref, k) + add_t for k in range(steps)]
        moist = [get(ym_ref, k) + add_m for k in range(steps)]
        for j in range(1, SUB + 1):
            if j > 1:
                spread = []
                for field, add in ((temp, const(2 * j - 2)), (moist, const(2 * j - 1))):
                    after = pltpu.roll(field[0], 7, 0)
                    before = pltpu.roll(field[steps - 1], 1, 0)
                    ring = [before] + field + [after]
                    spread.append([((ring[k] + ring[k + 2]) + 3.0 * field[k]) + add for k in range(steps)])
                temp, moist = spread
            temp, moist = list(temp), list(moist)
            for k in range(steps):
                over = jnp.maximum(moist[k] - jnp.exp2((scale / 5.0 ** j) * temp[k]), 0.0)
                moist[k] = moist[k] - get(rate_ref, k) * over
                temp[k] = temp[k] + get(both_ref, k) * over
        for i, field in enumerate((temp, moist)):
            while len(field) > 1:
                field = [a + b for a, b in zip(field[0::2], field[1::2])]
            sums_ref[half, pl.ds(pl.multiple_of((i * levels + level) * 8, 8), 8), :] = field[0]

    @pl.loop(0, levels)
    def _(level):
        for half in range(slots // 128):
            unit(level, half)

    factor = 1.0 / (crmx * 5.0 ** SUB)
    total = 2 * levels
    for half in range(slots // 128):
        summed = sums_ref[half, pl.ds(0, total, stride=8), :]
        for s in range(1, 8):
            summed = summed + sums_ref[half, pl.ds(s, total, stride=8), :]
        mean = summed * factor
        mean = jnp.concatenate([mean[:levels] - shift[SUB], mean[levels:], jnp.zeros((256 - total, 128), F32)], axis=0)
        out_ref[pl.ds(half * 128, 128), :] = mean.T[:, :total]


def finish_kernel(state_ref, dyn_ref, hot_ref, back_ref, out_ref):
    rows = state_ref.shape[0]
    out_ref[...] = dyn_ref[...] + select_dot(back_ref[...], hot_ref[...], TN)


def local(state, neighbors, owner, crm_state, phase_mask):
    ndev = lax.axis_size(AXES)
    me = lax.axis_index(AXES)
    fields, levels, cdev = state.shape
    rows = fields * levels
    slots, wide = crm_state.shape
    crmx = wide // rows
    cap = slots // ndev
    flat = state.reshape(rows, cdev)
    up = [(i, (i + 1) % ndev) for i in range(ndev)]
    down = [(j, i) for i, j in up]
    before = lax.ppermute(flat[:, cdev - REACH:], AXES, up)
    after = lax.ppermute(flat[:, :REACH], AXES, down)
    sds = jax.ShapeDtypeStruct

    outgoing, dyn, hot = pl.pallas_call(
        functools.partial(pack_kernel, cap, slots, cdev * ndev),
        in_specs=[SMEM] + [VMEM] * 5,
        out_specs=[VMEM] * 3,
        out_shape=[sds((slots, 2 * rows), F32), sds((rows, cdev), F32), sds((slots, cdev), BF16)],
        compiler_params=pltpu.CompilerParams(vmem_limit_bytes=16 << 20),
        name="pack",
    )((me * cdev).reshape(1), flat, before, after, neighbors, owner.reshape(1, cdev))
    arrived = lax.all_to_all(outgoing.reshape(ndev, cap * 2 * rows), AXES, split_axis=0, concat_axis=0, tiled=True)
    arrived = arrived.reshape(slots, 2 * rows)

    block = 2 * GROUP * crmx
    count = levels * crmx // block
    take = lambda offset: pl.BlockSpec((slots, block), lambda g: (0, g + offset))
    big = sds((levels * crmx, slots), F32)
    prepared = pl.pallas_call(
        functools.partial(prepare_kernel, crmx),
        grid=(count,),
        in_specs=[take(0), take(count), take(0)],
        out_specs=[VMEM] * 4,
        out_shape=[big] * 4,
        compiler_params=pltpu.CompilerParams(vmem_limit_bytes=32 << 20),
        cost_estimate=pl.CostEstimate(flops=6 * slots * levels * crmx * GROUP * crmx, transcendentals=0, bytes_accessed=4 * slots * wide),
        name="prepare",
    )(crm_state, crm_state, phase_mask)

    back = pl.pallas_call(
        functools.partial(physics_kernel, levels, crmx),
        in_specs=[VMEM] * 5,
        out_specs=VMEM,
        out_shape=sds((slots, rows), F32),
        scratch_shapes=[
            pltpu.VMEM((slots // 128, 2 * SUB * levels + 8, 128), F32),
            pltpu.VMEM((slots // 128, 8 * rows, 128), F32),
        ],
        compiler_params=pltpu.CompilerParams(vmem_limit_bytes=32 << 20),
        name="physics",
    )(arrived, *prepared)
    back = lax.all_to_all(back.reshape(ndev, cap * rows), AXES, split_axis=0, concat_axis=0, tiled=True)
    back = back.reshape(slots, rows)
    out = pl.pallas_call(
        finish_kernel,
        in_specs=[VMEM] * 4,
        out_specs=VMEM,
        out_shape=sds((rows, cdev), F32),
        compiler_params=pltpu.CompilerParams(vmem_limit_bytes=16 << 20),
        name="finish",
    )(flat, dyn, hot, back)
    return out.reshape(state.shape)


def solution(mesh):
    return jax.shard_map(
        local,
        mesh=mesh,
        in_specs=(
            P(None, None, AXES),
            P(None, AXES),
            P(AXES, None),
            P(AXES, None),
            P(AXES, None),
        ),
        out_specs=P(None, None, AXES),
        check_vma=False,
    )
```

time: 200 us -> 76.8 us (0.38)
  other arithmetic: 101 us -> 1.05 us
  local copies, waits for them, and re-layouts: 74.1 us -> 23.2 us
  Pallas kernels: 0 us -> 21.4 us
  waiting for transfers between devices: 0.01 us -> 7.37 us
    add x4 -> x0, other arithmetic: 51.4 us -> none  [the longest x3 46.1 us: condense(): temper = temper + heat * cond]
    slice x17 -> x1, local copies, waits for them, and re-layouts: 48 us -> 1.04 us  [local(): after = lax.ppermute(flat[:, :REACH], AXES, down)]
    pallas_call x0 -> x4, Pallas kernels: none -> 21.4 us  [the longest x1 11.3 us: local(): pl.pallas_call(functools.partial(physics_kernel, levels, crmx), in_specs=...]
    sub x5 -> x0, other arithmetic: 19.1 us -> none  [the longest x3 19.1 us: condense(): moisture = moisture - cond]
    reduce_sum x2 -> x0, other arithmetic: 11.8 us -> none  [the longest x1 10.9 us: condense(): jnp.mean(temper, axis=2) - temp_col]
    select_n x3 -> x0, other arithmetic: 8.91 us -> none  [the longest x1 5.4 us: condense(): rate = jnp.where(is_ice, 0.3, 0.7).astype(jnp.float32)]
    ppermute x2, waiting for transfers between devices: 0.01 us -> 7.37 us  [the longest x1 5.39 us: local(): before = lax.ppermute(flat[:, cdev - REACH:], AXES, up)]
    reshape x1 -> x0, other arithmetic: 7.25 us -> none  [condense(): fields = pert.astype(jnp.float32).reshape(count, 2, levels, -1)]
  transfers between devices with their start and end apart: 3 -> 3, of which waited for: 0 -> 2; matrix products, arithmetic and copies ran while one was open for 15% -> 0% of each run, Pallas kernels for 0% -> 11%
where the time goes in v1:
time: 76.8 us; the launch traced here: 76.2 us
  local copies, waits for them, and re-layouts  23.2 us (30%)
  Pallas kernels  21.4 us (28%)
  blocking collectives  14 us (18%)
  starting transfers between devices  9.04 us (12%)
  waiting for transfers between devices  7.37 us (10%)
  other arithmetic  1.05 us (1%)
    unnamed x24, local copies, waits for them, and re-layouts  20.2 us
    all_to_all x1, blocking collectives, local(): lax.all_to_all(back.reshape(ndev, cap * rows), AXES, split_axis=0, concat...  14 us
    pallas_call x1, Pallas kernels, local(): pl.pallas_call(functools.partial(physics_kernel, levels, crmx), in_specs=...  11.3 us
    pallas_call x1, Pallas kernels, local(): pl.pallas_call(functools.partial(prepare_kernel, crmx), grid=(count,), in...  8.38 us
    ppermute x1, starting transfers between devices, local(): after = lax.ppermute(flat[:, :REACH], AXES, down)  6.45 us
    ppermute x1, waiting for transfers between devices, local(): before = lax.ppermute(flat[:, cdev - REACH:], AXES, up)  5.39 us
    all_to_all x1, starting transfers between devices, local(): lax.all_to_all(outgoing.reshape(ndev, cap * 2 * rows), AXES, split_axis=0...  2.59 us
    ppermute x1, waiting for transfers between devices, local(): after = lax.ppermute(flat[:, :REACH], AXES, down)  1.98 us
  transfers between devices with their start and end apart: 3, of which 2 were waited for; matrix products, arithmetic and copies ran while one was open for 0% of the time, Pallas kernels for 11%

profile of v1, /device:TPU:0, one launch (start us, length us, event | category | flops | bytes accessed | tf_op | source)
XLA Modules:
  0.0 76.2 jit_solution(2928488629298587146)
XLA Ops:
  0.0 1.0 %fusion = (f32[144,8]{1,0:T(8,128)S(1)}, f32[144,8]{1,0:T(8,128)S(1)}) fusion(f32[144,128]{1,0:T(8,128)} %bitcast.4), kind=kLoop, calls=%fused_computation | loop fusion | bytes 18432 | tf_op jit(solution)/shard_map/slice | solution.py:175
  1.0 6.5 %collective-permute-start.1 = (f32[144,8]{1,0:T(8,128)S(1)}, f32[144,8]{1,0:T(8,128)S(1)}, u32[]{:S(2)}, u32[]{:S(2)}) collective-permute-start(f32[144,8]{1,0:T(8,128)S(1)} %get-tuple-element.19), channel_id=1, source_target_pairs={{1,0},{2,1},{3,2},{4,3},{5,4},{6,5},{7,6},{8,7},{9,8},{10,9},{11,1... | collective-permute-start | bytes 13832 | tf_op jit(solution)/shard_map/ppermute | solution.py:175
  7.5 0.0 collective-permute-start
  7.5 2.0 %collective-permute-done.1.after_ref = f32[144,8]{1,0:T(8,128)S(1)} collective-permute-done((f32[144,8]{1,0:T(8,128)S(1)}, f32[144,8]{1,0:T(8,128)S(1)}, u32[]{:S(2)}, u32[]{:S(2)}) %collective-permute-start.1) | collective-permute-done | bytes 4640 | tf_op jit(solution)/shard_map/ppermute | solution.py:175
  9.5 5.4 %collective-permute-done.before_ref = f32[144,8]{1,0:T(8,128)S(1)} collective-permute-done((f32[144,8]{1,0:T(8,128)S(1)}, f32[144,8]{1,0:T(8,128)S(1)}, u32[]{:S(2)}, u32[]{:S(2)}) %collective-permute-start) | collective-permute-done | bytes 4640 | tf_op jit(solution)/shard_map/ppermute | solution.py:174
  14.9 0.0 copy-start.8
  14.9 0.9 %copy-done.8 = f32[2,72,128]{2,1,0:T(8,128)S(1)} copy-done((f32[2,72,128]{2,1,0:T(8,128)S(1)}, f32[2,72,128]{2,1,0:T(8,128)}, u32[]{:S(2)}) %copy-start.8) | copy-done | bytes 73752
  15.8 0.0 copy-start.10
  15.8 0.7 copy-done.10
  16.4 0.0 copy-start.11
  16.4 0.7 copy-done.11
  17.1 0.9 %pack.1 = (f32[256,288]{1,0:T(8,128)S(1)}, f32[144,128]{1,0:T(8,128)S(1)}, bf16[256,128]{1,0:T(8,128)(2,1)S(1)}) custom-call(s32[1]{0:T(128)} %bitcast.1.first_ref, f32[144,128]{1,0:T(8,128)S(1)} %bitcast.5, f32[144,8]{1,0:T(8,128)S(1)} %collective-permute-done.before_ref, f32[144,8]{1,0:T(8,128)S(1)} %collective-permute-done.1.after_ref, ...), custom_call_target="tpu_custom_call" | custom-call | tf_op jit(solution)/shard_map/pack/pallas_call | solution.py:178
  18.0 1.2 %all_to_all.16 = f32[32,1,2304]{2,1,0:T(1,128)} reshape(f32[256,288]{1,0:T(8,128)S(1)} %get-tuple-element.14) | data formatting | bytes 589824 | tf_op jit(solution)/shard_map/all_to_all | solution.py:186
  19.2 2.6 %all-to-all-start = ((f32[32,1,2304]{2,1,0:T(1,128)}), f32[32,1,2304]{2,1,0:T(1,128)S(1)}, u32[]{:S(2)}, u32[]{:S(2)}) async-start(f32[32,1,2304]{2,1,0:T(1,128)} %all_to_all.16), calls=%async_computation | async-start | bytes 589824 | tf_op jit(solution)/shard_map/all_to_all | solution.py:186
  21.8 8.4 %prepare.1 = (f32[4608,256]{1,0:T(8,128)S(1)}, f32[4608,256]{1,0:T(8,128)S(1)}, f32[4608,256]{1,0:T(8,128)S(1)}, f32[4608,256]{1,0:T(8,128)S(1)}) custom-call(bf16[256,9216]{1,0:T(8,128)(2,1)} %cm_ref.1, bf16[256,9216]{1,0:T(8,128)(2,1)} %cm_ref.1, s32[256,4608]{1,0:T(8,128)} %mask_ref.1), custom_call_target="tpu_custom_call" | custom-call | flops 1811939328 | bytes 9437184 | tf_op jit(solution)/shard_map/prepare/pallas_call | solution.py:193
  30.2 0.0 copy-start
  30.2 2.1 %copy-done = f32[4608,256]{1,0:T(8,128)} copy-done((f32[4608,256]{1,0:T(8,128)}, f32[4608,256]{1,0:T(8,128)S(1)}, u32[]{:S(2)}) %copy-start) | copy-done | bytes 4718616
  32.3 0.0 copy-start.2
  32.3 2.2 %copy-done.2 = f32[4608,256]{1,0:T(8,128)} copy-done((f32[4608,256]{1,0:T(8,128)}, f32[4608,256]{1,0:T(8,128)S(1)}, u32[]{:S(2)}) %copy-start.2) | copy-done | bytes 4718616
  34.5 0.0 copy-start.4
  34.5 2.2 %copy-done.4 = f32[4608,256]{1,0:T(8,128)} copy-done((f32[4608,256]{1,0:T(8,128)}, f32[4608,256]{1,0:T(8,128)S(1)}, u32[]{:S(2)}) %copy-start.4) | copy-done | bytes 4718616
  36.7 0.0 copy-start.6
  36.7 2.1 %copy-done.6 = f32[4608,256]{1,0:T(8,128)} copy-done((f32[4608,256]{1,0:T(8,128)}, f32[4608,256]{1,0:T(8,128)S(1)}, u32[]{:S(2)}) %copy-start.6) | copy-done | bytes 4718616
  38.8 0.0 all-to-all-done
  38.8 0.7 reduce
  39.5 0.3 reshape.31.arrived_ref
  39.8 0.0 copy-start.1
  39.8 2.3 %copy-done.1 = f32[4608,256]{1,0:T(8,128)S(1)} copy-done((f32[4608,256]{1,0:T(8,128)S(1)}, f32[4608,256]{1,0:T(8,128)}, u32[]{:S(2)}) %copy-start.1) | copy-done | bytes 4718616
  42.2 0.0 copy-start.3
  42.2 2.3 %copy-done.3 = f32[4608,256]{1,0:T(8,128)S(1)} copy-done((f32[4608,256]{1,0:T(8,128)S(1)}, f32[4608,256]{1,0:T(8,128)}, u32[]{:S(2)}) %copy-start.3) | copy-done | bytes 4718616
  44.5 0.0 copy-start.5
  44.5 2.3 %copy-done.5 = f32[4608,256]{1,0:T(8,128)S(1)} copy-done((f32[4608,256]{1,0:T(8,128)S(1)}, f32[4608,256]{1,0:T(8,128)}, u32[]{:S(2)}) %copy-start.5) | copy-done | bytes 4718616
  46.8 0.0 copy-start.7
  46.8 2.3 %copy-done.7 = f32[4608,256]{1,0:T(8,128)S(1)} copy-done((f32[4608,256]{1,0:T(8,128)S(1)}, f32[4608,256]{1,0:T(8,128)}, u32[]{:S(2)}) %copy-start.7) | copy-done | bytes 4718616
  49.2 0.0 copy-start.9
  49.2 11.3 %physics.1 = f32[256,144]{1,0:T(8,128)S(1)} custom-call(f32[256,288]{1,0:T(8,128)S(1)} %reshape.31.arrived_ref, f32[4608,256]{1,0:T(8,128)S(1)} %copy-done.1, f32[4608,256]{1,0:T(8,128)S(1)} %copy-done.3, f32[4608,256]{1,0:T(8,128)S(1)} %copy-done.5, f32[4608,256]{1,0:T(8,128)S(1)} %copy-done.7), custom_call_target="tpu_custom_call" | custom-call | tf_op jit(solution)/shard_map/physics/pallas_call | solution.py:204
  60.4 0.3 all_to_all.17
  60.8 14.0 %all_to_all.20 = f32[32,1,1152]{2,1,0:T(1,128)S(1)} all-to-all(f32[32,1,1152]{2,1,0:T(1,128)S(1)} %all_to_all.17), channel_id=1, replica_groups=mesh['sec'=4,'blk'=8] {'sec','blk'}, dimensions={0} | all-to-all | bytes 294912 | tf_op jit(solution)/shard_map/all_to_all | solution.py:216
  74.8 0.4 reduce.1
  75.1 0.2 reshape.32.back_ref
  75.3 0.0 copy-done.9
  75.3 0.9 %finish.1 = f32[144,128]{1,0:T(8,128)} custom-call(f32[144,128]{1,0:T(8,128)S(1)} %bitcast.6, f32[144,128]{1,0:T(8,128)S(1)} %get-tuple-element.12.dyn_ref, bf16[256,128]{1,0:T(8,128)(2,1)S(1)} %get-tuple-element.13.hot_ref, f32[256,144]{1,0:T(8,128)S(1)} %reshape.32.back_ref), custom_call_target="tpu_custom_call" | custom-call | tf_op jit(solution)/shard_map/finish/pallas_call | solution.py:218
Async XLA Ops:
  1.0 8.4 %collective-permute-start.1 = (f32[144,8]{1,0:T(8,128)S(1)}, f32[144,8]{1,0:T(8,128)S(1)}, u32[]{:S(2)}, u32[]{:S(2)}) collective-permute-start(f32[144,8]{1,0:T(8,128)S(1)} %get-tuple-element.19), channel_id=1, source_target_pairs={{1,0},{2,1},{3,2},{4,3},{5,4},{6,5},{7,6},{8,7},{9,8},{10,9},{11,1... | collective-permute-start | bytes 13832 | tf_op jit(solution)/shard_map/ppermute | solution.py:175
  7.5 7.4 %collective-permute-start = (f32[144,8]{1,0:T(8,128)S(1)}, f32[144,8]{1,0:T(8,128)S(1)}, u32[]{:S(2)}, u32[]{:S(2)}) collective-permute-start(f32[144,8]{1,0:T(8,128)S(1)} %get-tuple-element.20), channel_id=1, source_target_pairs={{0,1},{1,2},{2,3},{3,4},{4,5},{5,6},{6,7},{7,8},{8,9},{9,10},{10,1... | collective-permute-start | bytes 13832 | tf_op jit(solution)/shard_map/ppermute | solution.py:174
  14.9 0.9 %copy-start.8 = (f32[2,72,128]{2,1,0:T(8,128)S(1)}, f32[2,72,128]{2,1,0:T(8,128)}, u32[]{:S(2)}) copy-start(f32[2,72,128]{2,1,0:T(8,128)} %param.5) | copy-start | bytes 221188
  15.8 0.7 copy-start.10
  16.4 0.7 copy-start.11
  19.2 19.6 %all-to-all-start = ((f32[32,1,2304]{2,1,0:T(1,128)}), f32[32,1,2304]{2,1,0:T(1,128)S(1)}, u32[]{:S(2)}, u32[]{:S(2)}) async-start(f32[32,1,2304]{2,1,0:T(1,128)} %all_to_all.16), calls=%async_computation | async-start | bytes 589824 | tf_op jit(solution)/shard_map/all_to_all | solution.py:186
  30.2 2.1 %copy-start = (f32[4608,256]{1,0:T(8,128)}, f32[4608,256]{1,0:T(8,128)S(1)}, u32[]{:S(2)}) copy-start(f32[4608,256]{1,0:T(8,128)S(1)} %get-tuple-element.15.yt_ref) | copy-start | bytes 14155780
  32.3 2.2 %copy-start.2 = (f32[4608,256]{1,0:T(8,128)}, f32[4608,256]{1,0:T(8,128)S(1)}, u32[]{:S(2)}) copy-start(f32[4608,256]{1,0:T(8,128)S(1)} %get-tuple-element.16.ym_ref) | copy-start | bytes 14155780
  34.5 2.2 %copy-start.4 = (f32[4608,256]{1,0:T(8,128)}, f32[4608,256]{1,0:T(8,128)S(1)}, u32[]{:S(2)}) copy-start(f32[4608,256]{1,0:T(8,128)S(1)} %get-tuple-element.17.rate_ref) | copy-start | bytes 14155780
  36.7 2.1 %copy-start.6 = (f32[4608,256]{1,0:T(8,128)}, f32[4608,256]{1,0:T(8,128)S(1)}, u32[]{:S(2)}) copy-start(f32[4608,256]{1,0:T(8,128)S(1)} %get-tuple-element.18.both_ref) | copy-start | bytes 14155780
  39.8 2.3 %copy-start.1 = (f32[4608,256]{1,0:T(8,128)S(1)}, f32[4608,256]{1,0:T(8,128)}, u32[]{:S(2)}) copy-start(f32[4608,256]{1,0:T(8,128)} %copy-done) | copy-start | bytes 14155780
  42.2 2.3 %copy-start.3 = (f32[4608,256]{1,0:T(8,128)S(1)}, f32[4608,256]{1,0:T(8,128)}, u32[]{:S(2)}) copy-start(f32[4608,256]{1,0:T(8,128)} %copy-done.2) | copy-start | bytes 14155780
  44.5 2.3 %copy-start.5 = (f32[4608,256]{1,0:T(8,128)S(1)}, f32[4608,256]{1,0:T(8,128)}, u32[]{:S(2)}) copy-start(f32[4608,256]{1,0:T(8,128)} %copy-done.4) | copy-start | bytes 14155780
  46.8 2.3 %copy-start.7 = (f32[4608,256]{1,0:T(8,128)S(1)}, f32[4608,256]{1,0:T(8,128)}, u32[]{:S(2)}) copy-start(f32[4608,256]{1,0:T(8,128)} %copy-done.6) | copy-start | bytes 14155780
  49.2 26.1 %copy-start.9 = (f32[2,72,128]{2,1,0:T(8,128)S(1)}, f32[2,72,128]{2,1,0:T(8,128)}, u32[]{:S(2)}) copy-start(f32[2,72,128]{2,1,0:T(8,128)} %param.5) | copy-start | bytes 221188

commit v2 on v1

v2 whole, which is shorter than its diff:
```python
import functools
import math

import jax
import jax.numpy as jnp
from jax import lax
from jax.experimental import pallas as pl
from jax.experimental.pallas import tpu as pltpu
from jax.sharding import PartitionSpec as P

SUB = 4
REACH = 8
GROUP = 4
AXES = ("sec", "blk")
F32 = jnp.float32
BF16 = jnp.bfloat16
NT = (((1,), (1,)), ((), ()))
NN = (((1,), (0,)), ((), ()))
TN = (((0,), (0,)), ((), ()))
VMEM = pl.BlockSpec(memory_space=pltpu.VMEM)
FULL = 60 * 1024 * 1024
SMEM = pl.BlockSpec(memory_space=pltpu.SMEM)


def parts_of(x):
    high = x.astype(BF16)
    rest = x - high.astype(F32)
    middle = rest.astype(BF16)
    low = (rest - middle.astype(F32)).astype(BF16)
    return high, middle, low


def select_dot(x, onehot, dims, flip=False):
    total = None
    for part in parts_of(x):
        pair = (onehot, part) if flip else (part, onehot)
        term = lax.dot_general(*pair, dims, preferred_element_type=F32)
        total = term if total is None else total + term
    return total


def index_kernel(plan, first_ref, state_ref, near_ref, owner_ref, same_ref, part_ref, edge_ref, hot_ref, place_ref):
    cap, slots, total, dense = plan
    cdev = state_ref.shape[1]
    index = near_ref[...] - (first_ref[0] - REACH)
    index = jnp.where(index < 0, index + total, index)
    index = jnp.where(index >= total, index - total, index)
    own = lax.broadcasted_iota(jnp.int32, (cdev, cdev), 0) + REACH
    edge = lax.broadcasted_iota(jnp.int32, (2 * REACH, cdev), 0)
    edge = jnp.where(edge < REACH, edge, edge + cdev)
    inner, outer = jnp.zeros((cdev, cdev), F32), jnp.zeros((2 * REACH, cdev), F32)
    for k in range(near_ref.shape[0]):
        row = index[k:k + 1, :]
        inner = inner + jnp.where(own == row, 1.0, 0.0)
        outer = outer + jnp.where(edge == row, 1.0, 0.0)
    edge_ref[...] = outer.astype(BF16)
    same_ref[...] = state_ref[...]
    part_ref[...] = select_dot(state_ref[...], inner.astype(BF16), NN)
    mine = jnp.broadcast_to(owner_ref[...], (cdev, cdev)).astype(F32)
    lower = lax.broadcasted_iota(jnp.int32, (cdev, cdev), 0) < lax.broadcasted_iota(jnp.int32, (cdev, cdev), 1)
    rank = jnp.sum(jnp.where((mine == mine.T) & lower, 1.0, 0.0), axis=0, keepdims=True).astype(jnp.int32)
    to = owner_ref[...]
    if dense is None:
        target = to * cap + rank
        place_ref[0:1, :] = target
        wanted = [target]
    else:
        tiles, back = dense
        rest = (rank * 32) // 128
        wanted = [to * (tiles * cap + 2) + t * cap + rank for t in range(tiles)]
        wanted += [jnp.where(rank % 4 == q, to * (tiles * cap + 2) + tiles * cap + rest, -1) for q in range(4)]
        for t in range(back):
            place_ref[t:t + 1, :] = to * (back * cap + 1) + t * cap + rank
        place_ref[back:back + 1, :] = to * (back * cap + 1) + back * cap
        place_ref[back + 1:back + 2, :] = rank
    rows = lax.broadcasted_iota(jnp.int32, (hot_ref.shape[0], cdev), 0)
    for i, row in enumerate(wanted):
        hot_ref[:, i * cdev:(i + 1) * cdev] = jnp.where(rows == row, 1.0, 0.0).astype(BF16)


def pack_kernel(dense, odd_ref, state_ref, part_ref, edge_ref, far_ref, mate_ref, hot_ref, out_ref, dyn_ref):
    rows = state_ref.shape[0]
    state = state_ref[...]
    odd = jnp.broadcast_to(odd_ref[0], far_ref.shape) == 1
    before = jnp.where(odd, mate_ref[...], far_ref[...])
    after = jnp.where(odd, far_ref[...], mate_ref[...])
    halo = select_dot(before, edge_ref[0:REACH], NN) + select_dot(after, edge_ref[REACH:2 * REACH], NN)
    dyn = 0.15 * ((part_ref[...] + halo) - 4.0 * state)
    dyn_ref[...] = dyn
    if dense is None:
        out_ref[:, 0:rows] = select_dot(state, hot_ref[...], NT, True)
        out_ref[:, rows:2 * rows] = select_dot(dyn, hot_ref[...], NT, True)
        return
    load = jnp.concatenate([state, dyn], axis=0)
    tail = load[dense[0] * 128:]
    blocks = [load[t * 128:(t + 1) * 128] for t in range(dense[0])]
    for q in range(4):
        blocks.append(jnp.concatenate([tail if i == q else jnp.zeros_like(tail) for i in range(4)], axis=0))
    out_ref[...] = select_dot(jnp.concatenate(blocks, axis=1), hot_ref[...], NT, True)


def prepare_kernel(crmx, ct_ref, cm_ref, mask_ref, yt_ref, ym_ref, rate_ref, both_ref):
    width = ct_ref.shape[1]
    per = GROUP * crmx
    row = lax.broadcasted_iota(jnp.int32, (per, per), 0)
    col = lax.broadcasted_iota(jnp.int32, (per, per), 1)
    place = row % crmx
    apart = (((place % 8) * (crmx // 8) + place // 8) - col) & (crmx - 1)
    same = (row // crmx) == (col // crmx)
    move = jnp.where(same & (apart == 0), 1.0, 0.0)
    spread = jnp.where(same & ((apart == 1) | (apart == crmx - 1)), 1.0, 3.0 * move)
    move, spread = move.astype(BF16), spread.astype(BF16)
    for q in range(width // per):
        part = slice(q * per, (q + 1) * per)
        yt_ref[part, :] = lax.dot_general(spread, ct_ref[:, part], NT, preferred_element_type=F32)
        ym_ref[part, :] = lax.dot_general(spread, cm_ref[:, part], NT, preferred_element_type=F32)
        ice = lax.dot_general(move, mask_ref[:, part].astype(F32).astype(BF16), NT, preferred_element_type=F32)
        rate_ref[part, :] = 0.7 - 0.4 * ice
        both_ref[part, :] = 0.7 - 0.31 * ice


def arrivals(dense, arrived_ref, slots, wide):
    columns = []
    if dense is None:
        for start in range(0, wide, 128):
            size = min(128, wide - start)
            block = arrived_ref[:, start:start + size]
            if size < 128:
                block = jnp.concatenate([block, jnp.zeros((slots, 128 - size), F32)], axis=1)
            columns.append(block.T[:size])
        return jnp.concatenate(columns, axis=0)
    tiles, cap = dense[0], 8
    each = tiles * cap + 2
    for t in range(tiles):
        block = [arrived_ref[s * each + t * cap:s * each + (t + 1) * cap, :] for s in range(slots // cap)]
        columns.append(jnp.concatenate(block, axis=0).T)
    low = lax.broadcasted_iota(jnp.int32, (cap, 128), 0) < 4
    block = []
    for s in range(slots // cap):
        pair = [arrived_ref[s * each + tiles * cap + i:s * each + tiles * cap + i + 1, :] for i in range(2)]
        block.append(jnp.where(low, *[jnp.broadcast_to(p, (cap, 128)) for p in pair]))
    tail = jnp.concatenate(block, axis=0).T
    which = lax.broadcasted_iota(jnp.int32, (32, slots), 1) % 4
    columns.append(sum(jnp.where(which == q, tail[q * 32:(q + 1) * 32], 0.0) for q in range(4)))
    return jnp.concatenate(columns, axis=0)


def physics_kernel(levels, crmx, dense, arrived_ref, yt_ref, ym_ref, rate_ref, both_ref, out_ref, rows_ref, sums_ref):
    slots = yt_ref.shape[1]
    steps = crmx // 8
    scale = 0.3 * math.log2(math.e)
    shift = [math.log(0.8 * 5.0 ** j) / 0.3 for j in range(SUB + 1)]
    step = pl.program_id(0)
    per = yt_ref.shape[0] // crmx

    @pl.when(step == 0)
    def _():
        arrived = arrivals(dense, arrived_ref, slots, 4 * levels)
        temp, moist, push, wet = [arrived[i * levels:(i + 1) * levels] for i in range(4)]
        push, wet = push * (1.0 / SUB), wet * (1.0 / SUB)
        tables = [5.0 * (temp + push + shift[1]), 5.0 * (moist + wet)]
        for j in range(2, SUB + 1):
            tables += [5.0 ** j * (push + (shift[j] - shift[j - 1])), 5.0 ** j * wet]
        for i, table in enumerate(tables):
            for half in range(slots // 128):
                rows_ref[half, i * levels:(i + 1) * levels] = table[:, half * 128:(half + 1) * 128]

    def unit(inner, half):
        lanes = pl.ds(half * 128, 128)
        base = inner * crmx
        level = step * per + inner
        get = lambda ref, k: ref[pl.ds(base + 8 * k, 8), lanes]
        const = lambda i: rows_ref[half, pl.ds(level + i * levels, 8, stride=0), :]
        add_t, add_m = const(0), const(1)
        temp = [get(yt_ref, k) + add_t for k in range(steps)]
        moist = [get(ym_ref, k) + add_m for k in range(steps)]
        for j in range(1, SUB + 1):
            if j > 1:
                spread = []
                for field, add in ((temp, const(2 * j - 2)), (moist, const(2 * j - 1))):
                    after = pltpu.roll(field[0], 7, 0)
                    before = pltpu.roll(field[steps - 1], 1, 0)
                    ring = [before] + field + [after]
                    spread.append([((ring[k] + ring[k + 2]) + 3.0 * field[k]) + add for k in range(steps)])
                temp, moist = spread
            temp, moist = list(temp), list(moist)
            for k in range(steps):
                over = jnp.maximum(moist[k] - jnp.exp2((scale / 5.0 ** j) * temp[k]), 0.0)
                moist[k] = moist[k] - get(rate_ref, k) * over
                temp[k] = temp[k] + get(both_ref, k) * over
        for i, field in enumerate((temp, moist)):
            while len(field) > 1:
                field = [a + b for a, b in zip(field[0::2], field[1::2])]
            sums_ref[half, pl.ds(pl.multiple_of((i * levels + level) * 8, 8), 8), :] = field[0]

    for inner in range(per):
        for half in range(slots // 128):
            unit(inner, half)

    @pl.when(step == pl.num_programs(0) - 1)
    def _():
        factor = 1.0 / (crmx * 5.0 ** SUB)
        total = 2 * levels
        for half in range(slots // 128):
            summed = sums_ref[half, pl.ds(0, total, stride=8), :]
            for s in range(1, 8):
                summed = summed + sums_ref[half, pl.ds(s, total, stride=8), :]
            mean = summed * factor
            mean = jnp.concatenate([mean[:levels] - shift[SUB], mean[levels:]], axis=0)
            if dense is None:
                mean = jnp.concatenate([mean, jnp.zeros((256 - total, 128), F32)], axis=0)
                out_ref[pl.ds(half * 128, 128), :] = mean.T[:, :total]
                continue
            back, cap = dense[1], 8
            each = back * cap + 1
            for t in range(back):
                block = mean[t * 128:(t + 1) * 128].T
                for s in range(128 // cap):
                    to = (half * (128 // cap) + s) * each + t * cap
                    out_ref[to:to + cap, :] = block[s * cap:(s + 1) * cap]
            tail = jnp.concatenate([mean[back * 128:]] * cap, axis=0).T
            group = lax.broadcasted_iota(jnp.int32, (128, 128), 1) // (128 // cap)
            tail = jnp.where(group == lax.broadcasted_iota(jnp.int32, (128, 128), 0) % cap, tail, 0.0)
            for s in range(128 // cap):
                to = (half * (128 // cap) + s) * each + back * cap
                out_ref[to:to + 1, :] = jnp.sum(tail[s * cap:(s + 1) * cap], axis=0, keepdims=True)


def finish_kernel(dense, dyn_ref, place_ref, back_ref, out_ref):
    cdev = dyn_ref.shape[1]
    rows = lax.broadcasted_iota(jnp.int32, (back_ref.shape[0], cdev), 0)
    count = 1 if dense is None else dense[1] + 1
    hot = [jnp.where(rows == place_ref[i:i + 1, :], 1.0, 0.0).astype(BF16) for i in range(count)]
    means = select_dot(back_ref[...], jnp.concatenate(hot, axis=1), TN)
    if dense is None:
        out_ref[...] = dyn_ref[...] + means
        return
    back = dense[1]
    for t in range(back):
        out_ref[t * 128:(t + 1) * 128] = dyn_ref[t * 128:(t + 1) * 128] + means[:, t * cdev:(t + 1) * cdev]
    tail = means[:, back * cdev:]
    size = dyn_ref.shape[0] - back * 128
    rank = place_ref[back + 1:back + 2, :]
    mine = sum(jnp.where(rank == q, tail[q * size:(q + 1) * size], 0.0) for q in range(128 // size))
    out_ref[back * 128:] = dyn_ref[back * 128:] + mine


def local(state, neighbors, owner, crm_state, phase_mask):
    ndev = lax.axis_size(AXES)
    me = lax.axis_index(AXES)
    fields, levels, cdev = state.shape
    rows = fields * levels
    slots, wide = crm_state.shape
    crmx = wide // rows
    cap = slots // ndev
    flat = state.reshape(rows, cdev)
    sds = jax.ShapeDtypeStruct
    dense = (2 * rows // 128, rows // 128) if cap == 8 and rows % 128 == 16 else None
    out_each, back_each = 2 * rows * cap // 128, rows * cap // 128
    far = [(i, (i + 1) % ndev if i % 2 else (i - 1) % ndev) for i in range(ndev)]
    mate = [(i, i ^ 1) for i in range(ndev)]
    odd = me % 2
    first, last = flat[:, :REACH], flat[:, cdev - REACH:]
    from_far = lax.ppermute(jnp.where(odd == 1, last, first), AXES, far)
    from_mate = lax.ppermute(jnp.where(odd == 1, first, last), AXES, mate)

    def whole(*shape):
        return pl.BlockSpec(shape, lambda i: (0,) * len(shape))

    if dense is None:
        hot_shape, places = (slots, cdev), 1
    else:
        hot_shape, places = (ndev * out_each, cdev * (dense[0] + 4)), dense[1] + 2
    same, part, edge, hot, place = pl.pallas_call(
        functools.partial(index_kernel, (cap, slots, cdev * ndev, dense)),
        grid=(1,),
        in_specs=[SMEM, whole(rows, cdev), whole(*neighbors.shape), whole(1, cdev)],
        out_specs=[VMEM] * 5,
        out_shape=[sds((rows, cdev), F32)] * 2 + [sds((2 * REACH, cdev), BF16), sds(hot_shape, BF16), sds((places, cdev), jnp.int32)],
        compiler_params=pltpu.CompilerParams(vmem_limit_bytes=12 << 20),
        name="index",
    )((me * cdev).reshape(1), flat, neighbors, owner.reshape(1, cdev))
    outgoing, dyn = pl.pallas_call(
        functools.partial(pack_kernel, dense),
        in_specs=[SMEM] + [VMEM] * 6,
        out_specs=[VMEM] * 2,
        out_shape=[sds((slots, 2 * rows) if dense is None else (ndev * out_each, 128), F32), sds((rows, cdev), F32)],
        compiler_params=pltpu.CompilerParams(vmem_limit_bytes=12 << 20),
        name="pack",
    )(odd.reshape(1), same, part, edge, from_far, from_mate, hot)
    arrived = lax.all_to_all(outgoing.reshape(ndev, cap * 2 * rows), AXES, split_axis=0, concat_axis=0, tiled=True)
    arrived = arrived.reshape(outgoing.shape)

    block = 2 * GROUP * crmx
    count = levels * crmx // block
    take = lambda offset: pl.BlockSpec((slots, block), lambda g: (0, g + offset))
    big = sds((levels * crmx, slots), F32)
    prepared = pl.pallas_call(
        functools.partial(prepare_kernel, crmx),
        grid=(count,),
        in_specs=[take(0), take(count), take(0)],
        out_specs=[pl.BlockSpec((block, slots), lambda g: (g, 0))] * 4,
        out_shape=[big] * 4,
        compiler_params=pltpu.CompilerParams(vmem_limit_bytes=FULL),
        cost_estimate=pl.CostEstimate(flops=6 * slots * levels * crmx * GROUP * crmx, transcendentals=0, bytes_accessed=4 * slots * wide),
        name="prepare",
    )(crm_state, crm_state, phase_mask)

    back = pl.pallas_call(
        functools.partial(physics_kernel, levels, crmx, dense),
        grid=(count,),
        in_specs=[VMEM] + [pl.BlockSpec((block, slots), lambda g: (g, 0))] * 4,
        out_specs=VMEM,
        out_shape=sds((slots, rows) if dense is None else (ndev * back_each, 128), F32),
        scratch_shapes=[
            pltpu.VMEM((slots // 128, 2 * SUB * levels + 8, 128), F32),
            pltpu.VMEM((slots // 128, 8 * rows, 128), F32),
        ],
        compiler_params=pltpu.CompilerParams(vmem_limit_bytes=53000 << 10),
        name="physics",
    )(arrived, *prepared)
    returned = lax.all_to_all(back.reshape(ndev, cap * rows), AXES, split_axis=0, concat_axis=0, tiled=True)
    out = pl.pallas_call(
        functools.partial(finish_kernel, dense),
        in_specs=[VMEM] * 3,
        out_specs=VMEM,
        out_shape=sds((rows, cdev), F32),
        compiler_params=pltpu.CompilerParams(vmem_limit_bytes=12 << 20),
        name="finish",
    )(dyn, place, returned.reshape(back.shape))
    return out.reshape(state.shape)


def solution(mesh):
    return jax.shard_map(
        local,
        mesh=mesh,
        in_specs=(
            P(None, None, AXES),
            P(None, AXES),
            P(AXES, None),
            P(AXES, None),
            P(AXES, None),
        ),
        out_specs=P(None, None, AXES),
        check_vma=False,
    )
```

time: 76.8 us -> 59.9 us (0.78)
  local copies, waits for them, and re-layouts: 23.2 us -> 2.22 us
  Pallas kernels: 21.4 us -> 29.7 us
  waiting for transfers between devices: 7.37 us -> 0.01 us
  starting transfers between devices: 9.04 us -> 12.1 us
    unnamed x24 -> x6, local copies, waits for them, and re-layouts: 20.2 us -> 2.22 us
    ppermute x2, waiting for transfers between devices: 7.37 us -> 0.01 us  [the longest x1 0.01 us: local(): from_mate = lax.ppermute(jnp.where(odd == 1, first, last), AXES, mate)]
    pallas_call x1, Pallas kernels: 8.38 us -> 13 us  [local(): pl.pallas_call(functools.partial(prepare_kernel, crmx), grid=(count,), in...]
    pallas_call x3 -> x4, Pallas kernels: 13 us -> 16.7 us  [the longest x1 13.5 us: local(): pl.pallas_call(functools.partial(physics_kernel, levels, crmx, dense), gr...]
    all_to_all x1, starting transfers between devices: 2.59 us -> 4.94 us  [local(): lax.all_to_all(outgoing.reshape(ndev, cap * 2 * rows), AXES, split_axis=0...]
    all_to_all x2 -> x0, local copies, waits for them, and re-layouts: 1.55 us -> none  [the longest x1 1.24 us: local(): lax.all_to_all(outgoing.reshape(ndev, cap * 2 * rows), AXES, split_axis=0...]
    all_to_all x2 -> x0, other arithmetic: 1.05 us -> none  [the longest x1 0.69 us: local(): lax.all_to_all(outgoing.reshape(ndev, cap * 2 * rows), AXES, split_axis=0...]
    select_n x0 -> x1, other arithmetic: none -> 1.04 us  [local(): from_mate = lax.ppermute(jnp.where(odd == 1, first, last), AXES, mate)]
  transfers between devices with their start and end apart: 3 -> 3, of which waited for: 2 -> 0; matrix products, arithmetic and copies ran while one was open for 0% -> 0% of each run, Pallas kernels for 11% -> 23%
where the time goes in v2:
time: 59.9 us; the launch traced here: 59.1 us
  Pallas kernels  29.7 us (50%)
  blocking collectives  14 us (23%)
  starting transfers between devices  12.1 us (20%)
  local copies, waits for them, and re-layouts  2.22 us (4%)
  other arithmetic  1.04 us (2%)
    all_to_all x1, blocking collectives, local(): lax.all_to_all(back.reshape(ndev, cap * rows), AXES, split_axis=0, concat...  14 us
    pallas_call x1, Pallas kernels, local(): pl.pallas_call(functools.partial(physics_kernel, levels, crmx, dense), gr...  13.5 us
    pallas_call x1, Pallas kernels, local(): pl.pallas_call(functools.partial(prepare_kernel, crmx), grid=(count,), in...  13 us
    ppermute x1, starting transfers between devices, local(): from_far = lax.ppermute(jnp.where(odd == 1, last, first), AXES, far)  6.58 us
    all_to_all x1, starting transfers between devices, local(): lax.all_to_all(outgoing.reshape(ndev, cap * 2 * rows), AXES, split_axis=0...  4.94 us
    unnamed x6, local copies, waits for them, and re-layouts  2.22 us
    pallas_call x1, Pallas kernels, local(): pl.pallas_call(functools.partial(pack_kernel, dense), in_specs=[SMEM] + [...  1.79 us
  transfers between devices with their start and end apart: 3, of which 0 were waited for; matrix products, arithmetic and copies ran while one was open for 0% of the time, Pallas kernels for 23%

profile of v2, /device:TPU:0, one launch (start us, length us, event | category | flops | bytes accessed | tf_op | source)
XLA Modules:
  0.0 59.1 jit_solution(10513659361771150109)
XLA Ops:
  0.0 1.0 %slice_select_fusion = (f32[144,8]{1,0:T(8,128)S(1)}, f32[144,8]{1,0:T(8,128)S(1)}) fusion(f32[144,128]{1,0:T(8,128)} %bitcast.10, pred[]{:T(512)S(6)} %eq.6), kind=kLoop, calls=%fused_computation | loop fusion | flops 2304 | bytes 18433 | tf_op jit(solution)/shard_map/jit(_where)/select_n | solution.py:265
  1.1 0.6 collective-permute-start.1
  1.6 6.6 %collective-permute-start = (f32[144,8]{1,0:T(8,128)S(1)}, f32[144,8]{1,0:T(8,128)S(1)}, u32[]{:S(2)}, u32[]{:S(2)}) collective-permute-start(f32[144,8]{1,0:T(8,128)S(1)} %get-tuple-element.28), channel_id=1, source_target_pairs={{0,31},{1,2},{2,1},{3,4},{4,3},{5,6},{6,5},{7,8},{8,7},{9,10},{10,... | collective-permute-start | bytes 13832 | tf_op jit(solution)/shard_map/ppermute | solution.py:264
  8.2 0.0 copy-start
  8.2 0.9 %copy-done = f32[2,72,128]{2,1,0:T(8,128)S(1)} copy-done((f32[2,72,128]{2,1,0:T(8,128)S(1)}, f32[2,72,128]{2,1,0:T(8,128)}, u32[]{:S(2)}) %copy-start) | copy-done | bytes 73752
  9.1 0.0 copy-start.1
  9.1 0.7 %copy-done.1 = s32[4,128]{1,0:T(4,128)S(1)} copy-done((s32[4,128]{1,0:T(4,128)S(1)}, s32[4,128]{1,0:T(4,128)}, u32[]{:S(2)}) %copy-start.1) | copy-done | bytes 2072
  9.8 0.0 copy-start.2
  9.8 0.7 %copy-done.2 = s32[128,1]{0,1:T(1,128)S(1)} copy-done((s32[128,1]{0,1:T(1,128)S(1)}, s32[128,1]{0,1:T(1,128)}, u32[]{:S(2)}) %copy-start.2) | copy-done | bytes 536
  10.4 0.5 index.1
  11.0 0.0 collective-permute-done.1.mate_ref
  11.0 0.0 collective-permute-done.far_ref
  11.0 1.8 %pack.1 = (f32[576,128]{1,0:T(8,128)}, f32[144,128]{1,0:T(8,128)S(1)}) custom-call(s32[1]{0:T(128)} %bitcast.odd_ref, f32[144,128]{1,0:T(8,128)S(1)} %get-tuple-element.16.state_ref, f32[144,128]{1,0:T(8,128)S(1)} %get-tuple-element.17.part_ref, bf16[16,128]{1,0:T(8,128)(2,1)S(1)} %get-tuple-element.18.edge_ref, f32[144,8]{1,0:T(8,128)S(1)} %collective-permute-done.far_ref, ...), custom_call_target="tpu_custom_call" | custom-call | tf_op jit(solution)/shard_map/pack/pallas_call | solution.py:283
  12.8 4.9 %all-to-all-start = ((f32[32,1,2304]{2,1,0:T(1,128)}), f32[32,1,2304]{2,1,0:T(1,128)S(1)}, u32[]{:S(2)}, u32[]{:S(2)}) async-start(f32[32,1,2304]{2,1,0:T(1,128)} %bitcast.4), calls=%async_computation | async-start | bytes 589824 | tf_op jit(solution)/shard_map/all_to_all | solution.py:291
  17.7 13.0 %prepare.1 = (f32[4608,256]{1,0:T(8,128)}, f32[4608,256]{1,0:T(8,128)}, f32[4608,256]{1,0:T(8,128)}, f32[4608,256]{1,0:T(8,128)}) custom-call(bf16[256,9216]{1,0:T(8,128)(2,1)} %cm_ref.1, bf16[256,9216]{1,0:T(8,128)(2,1)} %cm_ref.1, s32[256,4608]{1,0:T(8,128)} %mask_ref.1), custom_call_target="tpu_custom_call" | custom-call | flops 1811939328 | bytes 9437184 | tf_op jit(solution)/shard_map/prepare/pallas_call | solution.py:298
  30.7 0.0 all-to-all-done
  30.7 13.5 %physics.1 = f32[288,128]{1,0:T(8,128)S(1)} custom-call(f32[576,128]{1,0:T(8,128)S(1)} %bitcast.9, f32[4608,256]{1,0:T(8,128)} %get-tuple-element.23.yt_ref, f32[4608,256]{1,0:T(8,128)} %get-tuple-element.24.ym_ref, f32[4608,256]{1,0:T(8,128)} %get-tuple-element.25.rate_ref, f32[4608,256]{1,0:T(8,128)} %get-tuple-element.26.both_ref), custom_call_target="tpu_custom_call" | custom-call | tf_op jit(solution)/shard_map/physics/pallas_call | solution.py:309
  44.2 14.0 %all_to_all.18 = f32[32,1,1152]{2,1,0:T(1,128)S(1)} all-to-all(f32[32,1,1152]{2,1,0:T(1,128)S(1)} %bitcast.13), channel_id=1, replica_groups=mesh['sec'=4,'blk'=8] {'sec','blk'}, dimensions={0} | all-to-all | bytes 294912 | tf_op jit(solution)/shard_map/all_to_all | solution.py:322
  58.2 0.9 %finish.1 = f32[144,128]{1,0:T(8,128)} custom-call(f32[144,128]{1,0:T(8,128)S(1)} %get-tuple-element.20.dyn_ref, s32[3,128]{1,0:T(4,128)S(1)} %get-tuple-element.21.place_ref, f32[288,128]{1,0:T(8,128)S(1)} %bitcast.12), custom_call_target="tpu_custom_call" | custom-call | tf_op jit(solution)/shard_map/finish/pallas_call | solution.py:323
Async XLA Ops:
  1.1 9.9 %collective-permute-start.1 = (f32[144,8]{1,0:T(8,128)S(1)}, f32[144,8]{1,0:T(8,128)S(1)}, u32[]{:S(2)}, u32[]{:S(2)}) collective-permute-start(f32[144,8]{1,0:T(8,128)S(1)} %get-tuple-element.27), channel_id=1, source_target_pairs={{0,1},{1,0},{2,3},{3,2},{4,5},{5,4},{6,7},{7,6},{8,9},{9,8},{10,11... | collective-permute-start | bytes 13832 | tf_op jit(solution)/shard_map/ppermute | solution.py:265
  1.6 9.4 %collective-permute-start = (f32[144,8]{1,0:T(8,128)S(1)}, f32[144,8]{1,0:T(8,128)S(1)}, u32[]{:S(2)}, u32[]{:S(2)}) collective-permute-start(f32[144,8]{1,0:T(8,128)S(1)} %get-tuple-element.28), channel_id=1, source_target_pairs={{0,31},{1,2},{2,1},{3,4},{4,3},{5,6},{6,5},{7,8},{8,7},{9,10},{10,... | collective-permute-start | bytes 13832 | tf_op jit(solution)/shard_map/ppermute | solution.py:264
  8.2 0.9 %copy-start = (f32[2,72,128]{2,1,0:T(8,128)S(1)}, f32[2,72,128]{2,1,0:T(8,128)}, u32[]{:S(2)}) copy-start(f32[2,72,128]{2,1,0:T(8,128)} %param.5) | copy-start | bytes 221188
  9.1 0.7 %copy-start.1 = (s32[4,128]{1,0:T(4,128)S(1)}, s32[4,128]{1,0:T(4,128)}, u32[]{:S(2)}) copy-start(s32[4,128]{1,0:T(4,128)} %near_ref.1) | copy-start | bytes 6148
  9.8 0.7 %copy-start.2 = (s32[128,1]{0,1:T(1,128)S(1)}, s32[128,1]{0,1:T(1,128)}, u32[]{:S(2)}) copy-start(s32[128,1]{0,1:T(1,128)} %param.7) | copy-start | bytes 1540
  12.8 17.9 %all-to-all-start = ((f32[32,1,2304]{2,1,0:T(1,128)}), f32[32,1,2304]{2,1,0:T(1,128)S(1)}, u32[]{:S(2)}, u32[]{:S(2)}) async-start(f32[32,1,2304]{2,1,0:T(1,128)} %bitcast.4), calls=%async_computation | async-start | bytes 589824 | tf_op jit(solution)/shard_map/all_to_all | solution.py:291

commit v3 on v2

--- a/solution.py
+++ b/solution.py
@@ -19,7 +19,6 @@
 TN = (((0,), (0,)), ((), ()))
 VMEM = pl.BlockSpec(memory_space=pltpu.VMEM)
 FULL = 60 * 1024 * 1024
-SMEM = pl.BlockSpec(memory_space=pltpu.SMEM)
 
 
 def parts_of(x):
@@ -31,18 +30,19 @@
 
 
 def select_dot(x, onehot, dims, flip=False):
-    total = None
-    for part in parts_of(x):
-        pair = (onehot, part) if flip else (part, onehot)
-        term = lax.dot_general(*pair, dims, preferred_element_type=F32)
-        total = term if total is None else total + term
-    return total
-
-
-def index_kernel(plan, first_ref, state_ref, near_ref, owner_ref, same_ref, part_ref, edge_ref, hot_ref, place_ref):
+    axis = 1 - dims[0][1 if flip else 0][0]
+    size = x.shape[axis]
+    wide = jnp.concatenate(parts_of(x), axis=axis)
+    pair = (onehot, wide) if flip else (wide, onehot)
+    out = lax.dot_general(*pair, dims, preferred_element_type=F32)
+    cut = (lambda i: out[:, i * size:(i + 1) * size]) if flip else (lambda i: out[i * size:(i + 1) * size])
+    return (cut(0) + cut(1)) + cut(2)
+
+
+def index_kernel(plan, state_ref, near_ref, owner_ref, same_ref, part_ref, edge_ref, hot_ref, place_ref, *tail_ref):
     cap, slots, total, dense = plan
     cdev = state_ref.shape[1]
-    index = near_ref[...] - (first_ref[0] - REACH)
+    index = near_ref[...] - (lax.axis_index(AXES) * cdev - REACH)
     index = jnp.where(index < 0, index + total, index)
     index = jnp.where(index >= total, index - total, index)
     own = lax.broadcasted_iota(jnp.int32, (cdev, cdev), 0) + REACH
@@ -60,28 +60,27 @@
     lower = lax.broadcasted_iota(jnp.int32, (cdev, cdev), 0) < lax.broadcasted_iota(jnp.int32, (cdev, cdev), 1)
     rank = jnp.sum(jnp.where((mine == mine.T) & lower, 1.0, 0.0), axis=0, keepdims=True).astype(jnp.int32)
     to = owner_ref[...]
+    target = to * cap + rank
+    rows = lax.broadcasted_iota(jnp.int32, (slots, cdev), 0)
+    hot_ref[...] = jnp.where(rows == target, 1.0, 0.0).astype(BF16)
     if dense is None:
-        target = to * cap + rank
         place_ref[0:1, :] = target
-        wanted = [target]
-    else:
-        tiles, back = dense
-        rest = (rank * 32) // 128
-        wanted = [to * (tiles * cap + 2) + t * cap + rank for t in range(tiles)]
-        wanted += [jnp.where(rank % 4 == q, to * (tiles * cap + 2) + tiles * cap + rest, -1) for q in range(4)]
-        for t in range(back):
-            place_ref[t:t + 1, :] = to * (back * cap + 1) + t * cap + rank
-        place_ref[back:back + 1, :] = to * (back * cap + 1) + back * cap
-        place_ref[back + 1:back + 2, :] = rank
-    rows = lax.broadcasted_iota(jnp.int32, (hot_ref.shape[0], cdev), 0)
-    for i, row in enumerate(wanted):
-        hot_ref[:, i * cdev:(i + 1) * cdev] = jnp.where(rows == row, 1.0, 0.0).astype(BF16)
-
-
-def pack_kernel(dense, odd_ref, state_ref, part_ref, edge_ref, far_ref, mate_ref, hot_ref, out_ref, dyn_ref):
+        return
+    back = dense[1]
+    for t in range(back):
+        place_ref[t:t + 1, :] = to * (back * cap + 1) + t * cap + rank
+    place_ref[back:back + 1, :] = to * (back * cap + 1) + back * cap
+    place_ref[back + 1:back + 2, :] = rank
+    rows = lax.broadcasted_iota(jnp.int32, (slots // 4, cdev), 0) * 4
+    for q in range(4):
+        tail_ref[0][:, q * cdev:(q + 1) * cdev] = jnp.where(rows + q == target, 1.0, 0.0).astype(BF16)
+
+
+def pack_kernel(dense, state_ref, part_ref, edge_ref, hot_ref, far_ref, mate_ref, *refs):
+    out_ref, dyn_ref = refs[-2:]
     rows = state_ref.shape[0]
     state = state_ref[...]
-    odd = jnp.broadcast_to(odd_ref[0], far_ref.shape) == 1
+    odd = jnp.broadcast_to(lax.axis_index(AXES) % 2, far_ref.shape) == 1
     before = jnp.where(odd, mate_ref[...], far_ref[...])
     after = jnp.where(odd, far_ref[...], mate_ref[...])
     halo = select_dot(before, edge_ref[0:REACH], NN) + select_dot(after, edge_ref[REACH:2 * REACH], NN)
@@ -92,11 +91,17 @@
         out_ref[:, rows:2 * rows] = select_dot(dyn, hot_ref[...], NT, True)
         return
     load = jnp.concatenate([state, dyn], axis=0)
-    tail = load[dense[0] * 128:]
-    blocks = [load[t * 128:(t + 1) * 128] for t in range(dense[0])]
-    for q in range(4):
-        blocks.append(jnp.concatenate([tail if i == q else jnp.zeros_like(tail) for i in range(4)], axis=0))
-    out_ref[...] = select_dot(jnp.concatenate(blocks, axis=1), hot_ref[...], NT, True)
+    tiles, cap = dense[0], 8
+    each = tiles * cap + 2
+    main = select_dot(load[:tiles * 128], hot_ref[...], NT, True)
+    tail = load[tiles * 128:]
+    blank = jnp.zeros_like(tail)
+    tail = [jnp.concatenate([tail if i == q else blank for i in range(4)], axis=0) for q in range(4)]
+    tail = select_dot(jnp.concatenate(tail, axis=1), refs[0][...], NT, True)
+    for s in range(hot_ref.shape[0] // cap):
+        for t in range(tiles):
+            out_ref[s * each + t * cap:s * each + (t + 1) * cap, :] = main[s * cap:(s + 1) * cap, t * 128:(t + 1) * 128]
+        out_ref[s * each + tiles * cap:(s + 1) * each, :] = tail[2 * s:2 * s + 2]
 
 
 def prepare_kernel(crmx, ct_ref, cm_ref, mask_ref, yt_ref, ym_ref, rate_ref, both_ref):
@@ -267,31 +272,31 @@
     def whole(*shape):
         return pl.BlockSpec(shape, lambda i: (0,) * len(shape))
 
-    if dense is None:
-        hot_shape, places = (slots, cdev), 1
-    else:
-        hot_shape, places = (ndev * out_each, cdev * (dense[0] + 4)), dense[1] + 2
-    same, part, edge, hot, place = pl.pallas_call(
+    index_out = [sds((rows, cdev), F32)] * 2 + [sds((2 * REACH, cdev), BF16), sds((slots, cdev), BF16)]
+    index_out.append(sds((1 if dense is None else dense[1] + 2, cdev), jnp.int32))
+    if dense is not None:
+        index_out.append(sds((slots // 4, 4 * cdev), BF16))
+    same, part, edge, hot, place, *tail = pl.pallas_call(
         functools.partial(index_kernel, (cap, slots, cdev * ndev, dense)),
         grid=(1,),
-        in_specs=[SMEM, whole(rows, cdev), whole(*neighbors.shape), whole(1, cdev)],
-        out_specs=[VMEM] * 5,
-        out_shape=[sds((rows, cdev), F32)] * 2 + [sds((2 * REACH, cdev), BF16), sds(hot_shape, BF16), sds((places, cdev), jnp.int32)],
+        in_specs=[whole(rows, cdev), whole(*neighbors.shape), whole(1, cdev)],
+        out_specs=[VMEM] * len(index_out),
+        out_shape=index_out,
         compiler_params=pltpu.CompilerParams(vmem_limit_bytes=12 << 20),
         name="index",
-    )((me * cdev).reshape(1), flat, neighbors, owner.reshape(1, cdev))
+    )(flat, neighbors, owner.reshape(1, cdev))
     outgoing, dyn = pl.pallas_call(
         functools.partial(pack_kernel, dense),
-        in_specs=[SMEM] + [VMEM] * 6,
+        in_specs=[VMEM] * (6 + len(tail)),
         out_specs=[VMEM] * 2,
         out_shape=[sds((slots, 2 * rows) if dense is None else (ndev * out_each, 128), F32), sds((rows, cdev), F32)],
         compiler_params=pltpu.CompilerParams(vmem_limit_bytes=12 << 20),
         name="pack",
-    )(odd.reshape(1), same, part, edge, from_far, from_mate, hot)
+    )(same, part, edge, hot, from_far, from_mate, *tail)
     arrived = lax.all_to_all(outgoing.reshape(ndev, cap * 2 * rows), AXES, split_axis=0, concat_axis=0, tiled=True)
     arrived = arrived.reshape(outgoing.shape)
 
-    block = 2 * GROUP * crmx
+    block = 3 * GROUP * crmx
     count = levels * crmx // block
     take = lambda offset: pl.BlockSpec((slots, block), lambda g: (0, g + offset))
     big = sds((levels * crmx, slots), F32)

time: 59.9 us -> 56.6 us (0.945)
  Pallas kernels: 29.7 us -> 26.4 us
    pallas_call x1, Pallas kernels: 13 us -> 11.4 us  [local(): pl.pallas_call(functools.partial(prepare_kernel, crmx), grid=(count,), in...]
    pallas_call x1, Pallas kernels: 13.5 us -> 12.4 us  [local(): pl.pallas_call(functools.partial(physics_kernel, levels, crmx, dense), gr...]
  transfers between devices with their start and end apart: 3 -> 3, of which waited for: 0 -> 0; matrix products, arithmetic and copies ran while one was open for 0% -> 0% of each run, Pallas kernels for 23% -> 21%
where the time goes in v3:
time: 56.6 us; the launch traced here: 56.1 us
  Pallas kernels  26.4 us (47%)
  blocking collectives  14 us (25%)
  starting transfers between devices  12.4 us (22%)
  local copies, waits for them, and re-layouts  2.22 us (4%)
  other arithmetic  1.04 us (2%)
    all_to_all x1, blocking collectives, local(): lax.all_to_all(back.reshape(ndev, cap * rows), AXES, split_axis=0, concat...  14 us
    pallas_call x1, Pallas kernels, local(): pl.pallas_call(functools.partial(physics_kernel, levels, crmx, dense), gr...  12.4 us
    pallas_call x1, Pallas kernels, local(): pl.pallas_call(functools.partial(prepare_kernel, crmx), grid=(count,), in...  11.4 us
    ppermute x1, starting transfers between devices, local(): from_far = lax.ppermute(jnp.where(odd == 1, last, first), AXES, far)  6.58 us
    all_to_all x1, starting transfers between devices, local(): lax.all_to_all(outgoing.reshape(ndev, cap * 2 * rows), AXES, split_axis=0...  5.25 us
    unnamed x6, local copies, waits for them, and re-layouts  2.22 us
    pallas_call x1, Pallas kernels, local(): pl.pallas_call(functools.partial(pack_kernel, dense), in_specs=[VMEM] * (...  1.35 us
  transfers between devices with their start and end apart: 3, of which 0 were waited for; matrix products, arithmetic and copies ran while one was open for 0% of the time, Pallas kernels for 21%

profile of v3, /device:TPU:0, one launch (start us, length us, event | category | flops | bytes accessed | tf_op | source)
XLA Modules:
  0.0 56.1 jit_solution(18312908502322468497)
XLA Ops:
  0.0 1.0 %slice_select_fusion = (f32[144,8]{1,0:T(8,128)S(1)}, f32[144,8]{1,0:T(8,128)S(1)}) fusion(f32[144,128]{1,0:T(8,128)} %bitcast.8, pred[]{:T(512)S(6)} %eq.6), kind=kLoop, calls=%fused_computation | loop fusion | flops 2304 | bytes 18433 | tf_op jit(solution)/shard_map/jit(_where)/select_n | solution.py:270
  1.1 0.6 collective-permute-start.1
  1.6 6.6 %collective-permute-start = (f32[144,8]{1,0:T(8,128)S(1)}, f32[144,8]{1,0:T(8,128)S(1)}, u32[]{:S(2)}, u32[]{:S(2)}) collective-permute-start(f32[144,8]{1,0:T(8,128)S(1)} %get-tuple-element.30), channel_id=1, source_target_pairs={{0,31},{1,2},{2,1},{3,4},{4,3},{5,6},{6,5},{7,8},{8,7},{9,10},{10,... | collective-permute-start | bytes 13832 | tf_op jit(solution)/shard_map/ppermute | solution.py:269
  8.2 0.0 copy-start
  8.2 0.9 %copy-done = f32[2,72,128]{2,1,0:T(8,128)S(1)} copy-done((f32[2,72,128]{2,1,0:T(8,128)S(1)}, f32[2,72,128]{2,1,0:T(8,128)}, u32[]{:S(2)}) %copy-start) | copy-done | bytes 73752
  9.1 0.0 copy-start.1
  9.1 0.7 %copy-done.1 = s32[4,128]{1,0:T(4,128)S(1)} copy-done((s32[4,128]{1,0:T(4,128)S(1)}, s32[4,128]{1,0:T(4,128)}, u32[]{:S(2)}) %copy-start.1) | copy-done | bytes 2072
  9.8 0.0 copy-start.2
  9.8 0.7 %copy-done.2 = s32[128,1]{0,1:T(1,128)S(1)} copy-done((s32[128,1]{0,1:T(1,128)S(1)}, s32[128,1]{0,1:T(1,128)}, u32[]{:S(2)}) %copy-start.2) | copy-done | bytes 536
  10.4 0.2 index.1
  10.7 0.0 collective-permute-done.1.mate_ref
  10.7 0.0 collective-permute-done.far_ref
  10.7 1.3 %pack.1 = (f32[576,128]{1,0:T(8,128)}, f32[144,128]{1,0:T(8,128)S(1)}) custom-call(f32[144,128]{1,0:T(8,128)S(1)} %get-tuple-element.17.state_ref, f32[144,128]{1,0:T(8,128)S(1)} %get-tuple-element.18.part_ref, bf16[16,128]{1,0:T(8,128)(2,1)S(1)} %get-tuple-element.19.edge_ref, bf16[256,128]{1,0:T(8,128)(2,1)S(1)} %get-tuple-element.20.hot_ref, ...), custom_call_target="tpu_custom_call" | custom-call | tf_op jit(solution)/shard_map/pack/pallas_call | solution.py:288
  12.0 5.2 %all-to-all-start = ((f32[32,1,2304]{2,1,0:T(1,128)}), f32[32,1,2304]{2,1,0:T(1,128)S(1)}, u32[]{:S(2)}, u32[]{:S(2)}) async-start(f32[32,1,2304]{2,1,0:T(1,128)} %bitcast.2), calls=%async_computation | async-start | bytes 589824 | tf_op jit(solution)/shard_map/all_to_all | solution.py:296
  17.3 11.4 %prepare.1 = (f32[4608,256]{1,0:T(8,128)}, f32[4608,256]{1,0:T(8,128)}, f32[4608,256]{1,0:T(8,128)}, f32[4608,256]{1,0:T(8,128)}) custom-call(bf16[256,9216]{1,0:T(8,128)(2,1)} %cm_ref.1, bf16[256,9216]{1,0:T(8,128)(2,1)} %cm_ref.1, s32[256,4608]{1,0:T(8,128)} %mask_ref.1), custom_call_target="tpu_custom_call" | custom-call | flops 1811939328 | bytes 9437184 | tf_op jit(solution)/shard_map/prepare/pallas_call | solution.py:303
  28.7 0.0 all-to-all-done
  28.7 12.4 %physics.1 = f32[288,128]{1,0:T(8,128)S(1)} custom-call(f32[576,128]{1,0:T(8,128)S(1)} %bitcast.7, f32[4608,256]{1,0:T(8,128)} %get-tuple-element.25.yt_ref, f32[4608,256]{1,0:T(8,128)} %get-tuple-element.26.ym_ref, f32[4608,256]{1,0:T(8,128)} %get-tuple-element.27.rate_ref, f32[4608,256]{1,0:T(8,128)} %get-tuple-element.28.both_ref), custom_call_target="tpu_custom_call" | custom-call | tf_op jit(solution)/shard_map/physics/pallas_call | solution.py:314
  41.2 14.0 %all_to_all.18 = f32[32,1,1152]{2,1,0:T(1,128)S(1)} all-to-all(f32[32,1,1152]{2,1,0:T(1,128)S(1)} %bitcast.11), channel_id=1, replica_groups=mesh['sec'=4,'blk'=8] {'sec','blk'}, dimensions={0} | all-to-all | bytes 294912 | tf_op jit(solution)/shard_map/all_to_all | solution.py:327
  55.2 0.9 %finish.1 = f32[144,128]{1,0:T(8,128)} custom-call(f32[144,128]{1,0:T(8,128)S(1)} %get-tuple-element.22.dyn_ref, s32[3,128]{1,0:T(4,128)S(1)} %get-tuple-element.23.place_ref, f32[288,128]{1,0:T(8,128)S(1)} %bitcast.10), custom_call_target="tpu_custom_call" | custom-call | tf_op jit(solution)/shard_map/finish/pallas_call | solution.py:328
Async XLA Ops:
  1.1 9.6 %collective-permute-start.1 = (f32[144,8]{1,0:T(8,128)S(1)}, f32[144,8]{1,0:T(8,128)S(1)}, u32[]{:S(2)}, u32[]{:S(2)}) collective-permute-start(f32[144,8]{1,0:T(8,128)S(1)} %get-tuple-element.29), channel_id=1, source_target_pairs={{0,1},{1,0},{2,3},{3,2},{4,5},{5,4},{6,7},{7,6},{8,9},{9,8},{10,11... | collective-permute-start | bytes 13832 | tf_op jit(solution)/shard_map/ppermute | solution.py:270
  1.6 9.1 %collective-permute-start = (f32[144,8]{1,0:T(8,128)S(1)}, f32[144,8]{1,0:T(8,128)S(1)}, u32[]{:S(2)}, u32[]{:S(2)}) collective-permute-start(f32[144,8]{1,0:T(8,128)S(1)} %get-tuple-element.30), channel_id=1, source_target_pairs={{0,31},{1,2},{2,1},{3,4},{4,3},{5,6},{6,5},{7,8},{8,7},{9,10},{10,... | collective-permute-start | bytes 13832 | tf_op jit(solution)/shard_map/ppermute | solution.py:269
  8.2 0.9 %copy-start = (f32[2,72,128]{2,1,0:T(8,128)S(1)}, f32[2,72,128]{2,1,0:T(8,128)}, u32[]{:S(2)}) copy-start(f32[2,72,128]{2,1,0:T(8,128)} %param.5) | copy-start | bytes 221188
  9.1 0.7 %copy-start.1 = (s32[4,128]{1,0:T(4,128)S(1)}, s32[4,128]{1,0:T(4,128)}, u32[]{:S(2)}) copy-start(s32[4,128]{1,0:T(4,128)} %near_ref.1) | copy-start | bytes 6148
  9.8 0.7 %copy-start.2 = (s32[128,1]{0,1:T(1,128)S(1)}, s32[128,1]{0,1:T(1,128)}, u32[]{:S(2)}) copy-start(s32[128,1]{0,1:T(1,128)} %param.7) | copy-start | bytes 1540
  12.0 16.7 %all-to-all-start = ((f32[32,1,2304]{2,1,0:T(1,128)}), f32[32,1,2304]{2,1,0:T(1,128)S(1)}, u32[]{:S(2)}, u32[]{:S(2)}) async-start(f32[32,1,2304]{2,1,0:T(1,128)} %bitcast.2), calls=%async_computation | async-start | bytes 589824 | tf_op jit(solution)/shard_map/all_to_all | solution.py:296

commit v4 on v3

--- a/solution.py
+++ b/solution.py
@@ -19,6 +19,8 @@
 TN = (((0,), (0,)), ((), ()))
 VMEM = pl.BlockSpec(memory_space=pltpu.VMEM)
 FULL = 60 * 1024 * 1024
+LOG = 0.3 * math.log2(math.e)
+TRIO = 3
 
 
 def parts_of(x):
@@ -104,24 +106,23 @@
         out_ref[s * each + tiles * cap:(s + 1) * each, :] = tail[2 * s:2 * s + 2]
 
 
-def prepare_kernel(crmx, ct_ref, cm_ref, mask_ref, yt_ref, ym_ref, rate_ref, both_ref):
-    width = ct_ref.shape[1]
+def near_matrix(rows, columns, crmx, centre, side):
+    row = lax.broadcasted_iota(jnp.int32, (rows, columns), 0)
+    col = lax.broadcasted_iota(jnp.int32, (rows, columns), 1)
+    apart = (row - col) & (crmx - 1)
+    same = (row // crmx) == (col // crmx)
+    off = jnp.where((apart == 1) | (apart == crmx - 1), side, 0.0)
+    return jnp.where(same, jnp.where(apart == 0, centre, off), 0.0)
+
+
+def prepare_kernel(crmx, mask_ref, rate_ref, both_ref):
     per = GROUP * crmx
-    row = lax.broadcasted_iota(jnp.int32, (per, per), 0)
-    col = lax.broadcasted_iota(jnp.int32, (per, per), 1)
-    place = row % crmx
-    apart = (((place % 8) * (crmx // 8) + place // 8) - col) & (crmx - 1)
-    same = (row // crmx) == (col // crmx)
-    move = jnp.where(same & (apart == 0), 1.0, 0.0)
-    spread = jnp.where(same & ((apart == 1) | (apart == crmx - 1)), 1.0, 3.0 * move)
-    move, spread = move.astype(BF16), spread.astype(BF16)
-    for q in range(width // per):
+    move = near_matrix(per, per, crmx, 1.0, 0.0).astype(BF16)
+    for q in range(mask_ref.shape[1] // per):
         part = slice(q * per, (q + 1) * per)
-        yt_ref[part, :] = lax.dot_general(spread, ct_ref[:, part], NT, preferred_element_type=F32)
-        ym_ref[part, :] = lax.dot_general(spread, cm_ref[:, part], NT, preferred_element_type=F32)
         ice = lax.dot_general(move, mask_ref[:, part].astype(F32).astype(BF16), NT, preferred_element_type=F32)
         rate_ref[part, :] = 0.7 - 0.4 * ice
-        both_ref[part, :] = 0.7 - 0.31 * ice
+        both_ref[part, :] = 0.7 * LOG - (0.31 * LOG) * ice
 
 
 def arrivals(dense, arrived_ref, slots, wide):
@@ -150,68 +151,108 @@
     return jnp.concatenate(columns, axis=0)
 
 
-def physics_kernel(levels, crmx, dense, arrived_ref, yt_ref, ym_ref, rate_ref, both_ref, out_ref, rows_ref, sums_ref):
-    slots = yt_ref.shape[1]
-    steps = crmx // 8
-    scale = 0.3 * math.log2(math.e)
-    shift = [math.log(0.8 * 5.0 ** j) / 0.3 for j in range(SUB + 1)]
+def physics_kernel(levels, crmx, dense, arrived_ref, ct_ref, cm_ref, rate_ref, both_ref, out_ref, *scratch):
+    rows_ref, sums_ref, t_ref, m_ref, bt_ref, bm_ref, ft_ref, fm_ref, w_ref = scratch
+    slots = ct_ref.shape[0]
+    halves = slots // 128
     step = pl.program_id(0)
-    per = yt_ref.shape[0] // crmx
+    here = rate_ref.shape[0] // crmx
+    deep = TRIO * crmx
+    shift = math.log2(0.8)
 
     @pl.when(step == 0)
     def _():
         arrived = arrivals(dense, arrived_ref, slots, 4 * levels)
         temp, moist, push, wet = [arrived[i * levels:(i + 1) * levels] for i in range(4)]
         push, wet = push * (1.0 / SUB), wet * (1.0 / SUB)
-        tables = [5.0 * (temp + push + shift[1]), 5.0 * (moist + wet)]
-        for j in range(2, SUB + 1):
-            tables += [5.0 ** j * (push + (shift[j] - shift[j - 1])), 5.0 ** j * wet]
-        for i, table in enumerate(tables):
-            for half in range(slots // 128):
+        for i, table in enumerate((LOG * (temp + push) + shift, moist + wet)):
+            for half in range(halves):
                 rows_ref[half, i * levels:(i + 1) * levels] = table[:, half * 128:(half + 1) * 128]
-
-    def unit(inner, half):
-        lanes = pl.ds(half * 128, 128)
-        base = inner * crmx
-        level = step * per + inner
-        get = lambda ref, k: ref[pl.ds(base + 8 * k, 8), lanes]
-        const = lambda i: rows_ref[half, pl.ds(level + i * levels, 8, stride=0), :]
-        add_t, add_m = const(0), const(1)
-        temp = [get(yt_ref, k) + add_t for k in range(steps)]
-        moist = [get(ym_ref, k) + add_m for k in range(steps)]
-        for j in range(1, SUB + 1):
-            if j > 1:
-                spread = []
-                for field, add in ((temp, const(2 * j - 2)), (moist, const(2 * j - 1))):
-                    after = pltpu.roll(field[0], 7, 0)
-                    before = pltpu.roll(field[steps - 1], 1, 0)
-                    ring = [before] + field + [after]
-                    spread.append([((ring[k] + ring[k + 2]) + 3.0 * field[k]) + add for k in range(steps)])
-                temp, moist = spread
-            temp, moist = list(temp), list(moist)
-            for k in range(steps):
-                over = jnp.maximum(moist[k] - jnp.exp2((scale / 5.0 ** j) * temp[k]), 0.0)
-                moist[k] = moist[k] - get(rate_ref, k) * over
-                temp[k] = temp[k] + get(both_ref, k) * over
-        for i, field in enumerate((temp, moist)):
-            while len(field) > 1:
-                field = [a + b for a, b in zip(field[0::2], field[1::2])]
-            sums_ref[half, pl.ds(pl.multiple_of((i * levels + level) * 8, 8), 8), :] = field[0]
-
-    for inner in range(per):
-        for half in range(slots // 128):
-            unit(inner, half)
+        for ref, force in ((ft_ref, LOG * push), (fm_ref, wet)):
+            high = force.astype(BF16).astype(F32)
+            low = force - high
+            blank = jnp.zeros((16 - 2 * TRIO, slots), F32)
+            for g in range(levels // TRIO):
+                cut = slice(g * TRIO, (g + 1) * TRIO)
+                ref[g * 16:(g + 1) * 16, :] = jnp.concatenate([high[cut], low[cut], blank], axis=0).astype(BF16)
+        w_ref[:, :deep] = near_matrix(deep, deep, crmx, -0.4, 0.2).astype(BF16)
+        row = lax.broadcasted_iota(jnp.int32, (deep, 16), 0) // crmx
+        col = lax.broadcasted_iota(jnp.int32, (deep, 16), 1)
+        w_ref[:, deep:] = jnp.where((col < 2 * TRIO) & (row == col % TRIO), 1.0, 0.0).astype(BF16)
+
+    first = near_matrix(GROUP * crmx, GROUP * crmx, crmx, 3.0, 1.0).astype(BF16)
+    for q in range(here // GROUP):
+        part = slice(q * GROUP * crmx, (q + 1) * GROUP * crmx)
+        t_ref[part, :] = lax.dot_general(first, ct_ref[:, part], NT, preferred_element_type=F32)
+        m_ref[part, :] = lax.dot_general(first, cm_ref[:, part], NT, preferred_element_type=F32)
+
+    def spread(group):
+        rows = slice(group * deep, (group + 1) * deep)
+        at = pl.ds(pl.multiple_of((step * (here // TRIO) + group) * 16, 16), 16)
+        weights = w_ref[...]
+        return [
+            lax.dot_general(weights, jnp.concatenate([b_ref[rows, :], f_ref[at, :]], axis=0), NN, preferred_element_type=F32)
+            for b_ref, f_ref in ((bt_ref, ft_ref), (bm_ref, fm_ref))
+        ]
+
+    def advance(group, sub, moved):
+        for level in range(TRIO):
+            inner = group * TRIO + level
+            for half in range(halves):
+                lanes = slice(half * 128, (half + 1) * 128)
+                if sub == 1:
+                    add_t, add_m = [
+                        rows_ref[half, pl.ds(step * here + inner + i * levels, 8, stride=0), :] for i in range(2)
+                    ]
+                ends = [[], []]
+                for k in range(0, crmx, 16):
+                    pair = [[], []]
+                    for i in (k, k + 8):
+                        at = slice(inner * crmx + i, inner * crmx + i + 8)
+                        temp, moist = t_ref[at, lanes], m_ref[at, lanes]
+                        if sub == 1:
+                            temp, moist = temp * (LOG * 0.2) + add_t, moist * 0.2 + add_m
+                        else:
+                            local_at = slice(level * crmx + i, level * crmx + i + 8)
+                            temp, moist = temp + moved[0][local_at, lanes], moist + moved[1][local_at, lanes]
+                        over = jnp.maximum(moist - jnp.exp2(temp), 0.0)
+                        moist = moist - rate_ref[at, lanes] * over
+                        temp = temp + both_ref[at, lanes] * over
+                        if sub < SUB:
+                            t_ref[at, lanes], m_ref[at, lanes] = temp, moist
+                        pair[0].append(temp)
+                        pair[1].append(moist)
+                    if sub < SUB:
+                        wide = slice(inner * crmx + k, inner * crmx + k + 16)
+                        bt_ref[wide, lanes] = jnp.concatenate(pair[0], axis=0).astype(BF16)
+                        bm_ref[wide, lanes] = jnp.concatenate(pair[1], axis=0).astype(BF16)
+                    else:
+                        for i in range(2):
+                            ends[i].append(pair[i][0] + pair[i][1])
+                if sub == SUB:
+                    for i, field in enumerate(ends):
+                        while len(field) > 1:
+                            field = [a + b for a, b in zip(field[0::2], field[1::2])]
+                        at = pl.ds(pl.multiple_of((i * levels + step * here + inner) * 8, 8), 8)
+                        sums_ref[half, at, :] = field[0]
+
+    for pair in range(0, here // TRIO, 2):
+        moved = [None, None]
+        for sub in range(1, SUB + 1):
+            for i in range(2):
+                advance(pair + i, sub, moved[i])
+                if sub < SUB:
+                    moved[i] = spread(pair + i)
 
     @pl.when(step == pl.num_programs(0) - 1)
     def _():
-        factor = 1.0 / (crmx * 5.0 ** SUB)
         total = 2 * levels
-        for half in range(slots // 128):
+        for half in range(halves):
             summed = sums_ref[half, pl.ds(0, total, stride=8), :]
             for s in range(1, 8):
                 summed = summed + sums_ref[half, pl.ds(s, total, stride=8), :]
-            mean = summed * factor
-            mean = jnp.concatenate([mean[:levels] - shift[SUB], mean[levels:]], axis=0)
+            mean = summed * (1.0 / crmx)
+            mean = jnp.concatenate([(mean[:levels] - shift) * (1.0 / LOG), mean[levels:]], axis=0)
             if dense is None:
                 mean = jnp.concatenate([mean, jnp.zeros((256 - total, 128), F32)], axis=0)
                 out_ref[pl.ds(half * 128, 128), :] = mean.T[:, :total]
@@ -296,34 +337,41 @@
     arrived = lax.all_to_all(outgoing.reshape(ndev, cap * 2 * rows), AXES, split_axis=0, concat_axis=0, tiled=True)
     arrived = arrived.reshape(outgoing.shape)
 
-    block = 3 * GROUP * crmx
+    block = TRIO * GROUP * crmx
     count = levels * crmx // block
     take = lambda offset: pl.BlockSpec((slots, block), lambda g: (0, g + offset))
-    big = sds((levels * crmx, slots), F32)
-    prepared = pl.pallas_call(
+    rates_spec = [pl.BlockSpec((block, slots), lambda g: (g, 0))] * 2
+    rates = pl.pallas_call(
         functools.partial(prepare_kernel, crmx),
         grid=(count,),
-        in_specs=[take(0), take(count), take(0)],
-        out_specs=[pl.BlockSpec((block, slots), lambda g: (g, 0))] * 4,
-        out_shape=[big] * 4,
+        in_specs=[take(0)],
+        out_specs=rates_spec,
+        out_shape=[sds((levels * crmx, slots), F32)] * 2,
         compiler_params=pltpu.CompilerParams(vmem_limit_bytes=FULL),
-        cost_estimate=pl.CostEstimate(flops=6 * slots * levels * crmx * GROUP * crmx, transcendentals=0, bytes_accessed=4 * slots * wide),
+        cost_estimate=pl.CostEstimate(flops=2 * slots * levels * crmx * GROUP * crmx, transcendentals=0, bytes_accessed=6 * slots * wide),
         name="prepare",
-    )(crm_state, crm_state, phase_mask)
+    )(phase_mask)
 
     back = pl.pallas_call(
         functools.partial(physics_kernel, levels, crmx, dense),
         grid=(count,),
-        in_specs=[VMEM] + [pl.BlockSpec((block, slots), lambda g: (g, 0))] * 4,
+        in_specs=[VMEM, take(0), take(count)] + rates_spec,
         out_specs=VMEM,
         out_shape=sds((slots, rows) if dense is None else (ndev * back_each, 128), F32),
         scratch_shapes=[
-            pltpu.VMEM((slots // 128, 2 * SUB * levels + 8, 128), F32),
+            pltpu.VMEM((slots // 128, 2 * levels + 8, 128), F32),
             pltpu.VMEM((slots // 128, 8 * rows, 128), F32),
+            pltpu.VMEM((block, slots), F32),
+            pltpu.VMEM((block, slots), F32),
+            pltpu.VMEM((block, slots), BF16),
+            pltpu.VMEM((block, slots), BF16),
+            pltpu.VMEM((levels // TRIO * 16, slots), BF16),
+            pltpu.VMEM((levels // TRIO * 16, slots), BF16),
+            pltpu.VMEM((TRIO * crmx, TRIO * crmx + 16), BF16),
         ],
         compiler_params=pltpu.CompilerParams(vmem_limit_bytes=53000 << 10),
         name="physics",
-    )(arrived, *prepared)
+    )(arrived, crm_state, crm_state, *rates)
     returned = lax.all_to_all(back.reshape(ndev, cap * rows), AXES, split_axis=0, concat_axis=0, tiled=True)
     out = pl.pallas_call(
         functools.partial(finish_kernel, dense),

time: 56.6 us -> 55.5 us (0.981)
  blocking collectives: 14 us -> 10.5 us
  waiting for transfers between devices: 0.01 us -> 3.5 us
  Pallas kernels: 26.4 us -> 25.3 us
    pallas_call x1, Pallas kernels: 11.4 us -> 7.82 us  [local(): pl.pallas_call(functools.partial(prepare_kernel, crmx), grid=(count,), in...]
    all_to_all x1, waiting for transfers between devices: 0.01 us -> 3.49 us  [local(): lax.all_to_all(outgoing.reshape(ndev, cap * 2 * rows), AXES, split_axis=0...]
    all_to_all x1, blocking collectives: 14 us -> 10.5 us  [local(): lax.all_to_all(back.reshape(ndev, cap * rows), AXES, split_axis=0, concat...]
    pallas_call x1, Pallas kernels: 12.4 us -> 14.9 us  [local(): pl.pallas_call(functools.partial(physics_kernel, levels, crmx, dense), gr...]
  transfers between devices with their start and end apart: 3 -> 3, of which waited for: 0 -> 1; matrix products, arithmetic and copies ran while one was open for 0% -> 0% of each run, Pallas kernels for 21% -> 15%
where the time goes in v4:
time: 55.5 us; the launch traced here: 55 us
  Pallas kernels  25.3 us (46%)
  starting transfers between devices  12.4 us (22%)
  blocking collectives  10.5 us (19%)
  waiting for transfers between devices  3.5 us (6%)
  local copies, waits for them, and re-layouts  2.22 us (4%)
  other arithmetic  1.04 us (2%)
    pallas_call x1, Pallas kernels, local(): pl.pallas_call(functools.partial(physics_kernel, levels, crmx, dense), gr...  14.9 us
    all_to_all x1, blocking collectives, local(): lax.all_to_all(back.reshape(ndev, cap * rows), AXES, split_axis=0, concat...  10.5 us
    pallas_call x1, Pallas kernels, local(): pl.pallas_call(functools.partial(prepare_kernel, crmx), grid=(count,), in...  7.82 us
    ppermute x1, starting transfers between devices, local(): from_far = lax.ppermute(jnp.where(odd == 1, last, first), AXES, far)  6.58 us
    all_to_all x1, starting transfers between devices, local(): lax.all_to_all(outgoing.reshape(ndev, cap * 2 * rows), AXES, split_axis=0...  5.25 us
    all_to_all x1, waiting for transfers between devices, local(): lax.all_to_all(outgoing.reshape(ndev, cap * 2 * rows), AXES, split_axis=0...  3.49 us
    unnamed x6, local copies, waits for them, and re-layouts  2.22 us
    pallas_call x1, Pallas kernels, local(): pl.pallas_call(functools.partial(pack_kernel, dense), in_specs=[VMEM] * (...  1.36 us
  transfers between devices with their start and end apart: 3, of which 1 were waited for; matrix products, arithmetic and copies ran while one was open for 0% of the time, Pallas kernels for 15%

profile of v4, /device:TPU:0, one launch (start us, length us, event | category | flops | bytes accessed | tf_op | source)
XLA Modules:
  0.0 55.0 jit_solution(8002436976905727982)
XLA Ops:
  0.0 1.0 %slice_select_fusion = (f32[144,8]{1,0:T(8,128)S(1)}, f32[144,8]{1,0:T(8,128)S(1)}) fusion(f32[144,128]{1,0:T(8,128)} %bitcast.8, pred[]{:T(512)S(6)} %eq.6), kind=kLoop, calls=%fused_computation | loop fusion | flops 2304 | bytes 18433 | tf_op jit(solution)/shard_map/jit(_where)/select_n | solution.py:311
  1.1 0.6 %collective-permute-start.1 = (f32[144,8]{1,0:T(8,128)S(1)}, f32[144,8]{1,0:T(8,128)S(1)}, u32[]{:S(2)}, u32[]{:S(2)}) collective-permute-start(f32[144,8]{1,0:T(8,128)S(1)} %get-tuple-element.25), channel_id=1, source_target_pairs={{0,1},{1,0},{2,3},{3,2},{4,5},{5,4},{6,7},{7,6},{8,9},{9,8},{10,11... | collective-permute-start | bytes 13832 | tf_op jit(solution)/shard_map/ppermute | solution.py:311
  1.6 6.6 %collective-permute-start = (f32[144,8]{1,0:T(8,128)S(1)}, f32[144,8]{1,0:T(8,128)S(1)}, u32[]{:S(2)}, u32[]{:S(2)}) collective-permute-start(f32[144,8]{1,0:T(8,128)S(1)} %get-tuple-element.26), channel_id=1, source_target_pairs={{0,31},{1,2},{2,1},{3,4},{4,3},{5,6},{6,5},{7,8},{8,7},{9,10},{10,... | collective-permute-start | bytes 13832 | tf_op jit(solution)/shard_map/ppermute | solution.py:310
  8.2 0.0 copy-start
  8.2 0.9 %copy-done = f32[2,72,128]{2,1,0:T(8,128)S(1)} copy-done((f32[2,72,128]{2,1,0:T(8,128)S(1)}, f32[2,72,128]{2,1,0:T(8,128)}, u32[]{:S(2)}) %copy-start) | copy-done | bytes 73752
  9.1 0.0 copy-start.1
  9.1 0.7 %copy-done.1 = s32[4,128]{1,0:T(4,128)S(1)} copy-done((s32[4,128]{1,0:T(4,128)S(1)}, s32[4,128]{1,0:T(4,128)}, u32[]{:S(2)}) %copy-start.1) | copy-done | bytes 2072
  9.8 0.0 copy-start.2
  9.8 0.7 %copy-done.2 = s32[128,1]{0,1:T(1,128)S(1)} copy-done((s32[128,1]{0,1:T(1,128)S(1)}, s32[128,1]{0,1:T(1,128)}, u32[]{:S(2)}) %copy-start.2) | copy-done | bytes 536
  10.4 0.2 index.1
  10.7 0.0 collective-permute-done.1.mate_ref
  10.7 0.0 collective-permute-done.far_ref
  10.7 1.4 %pack.1 = (f32[576,128]{1,0:T(8,128)}, f32[144,128]{1,0:T(8,128)S(1)}) custom-call(f32[144,128]{1,0:T(8,128)S(1)} %get-tuple-element.15.state_ref, f32[144,128]{1,0:T(8,128)S(1)} %get-tuple-element.16.part_ref, bf16[16,128]{1,0:T(8,128)(2,1)S(1)} %get-tuple-element.17.edge_ref, bf16[256,128]{1,0:T(8,128)(2,1)S(1)} %get-tuple-element.18.hot_ref, ...), custom_call_target="tpu_custom_call" | custom-call | tf_op jit(solution)/shard_map/pack/pallas_call | solution.py:329
  12.0 5.2 %all-to-all-start = ((f32[32,1,2304]{2,1,0:T(1,128)}), f32[32,1,2304]{2,1,0:T(1,128)S(1)}, u32[]{:S(2)}, u32[]{:S(2)}) async-start(f32[32,1,2304]{2,1,0:T(1,128)} %bitcast.2), calls=%async_computation | async-start | bytes 589824 | tf_op jit(solution)/shard_map/all_to_all | solution.py:337
  17.3 7.8 %prepare.1 = (f32[4608,256]{1,0:T(8,128)}, f32[4608,256]{1,0:T(8,128)}) custom-call(s32[256,4608]{1,0:T(8,128)} %mask_ref.1), custom_call_target="tpu_custom_call" | custom-call | flops 603979776 | bytes 14155776 | tf_op jit(solution)/shard_map/prepare/pallas_call | solution.py:344
  25.1 3.5 %all-to-all-done = f32[32,1,2304]{2,1,0:T(1,128)S(1)} async-done(((f32[32,1,2304]{2,1,0:T(1,128)}), f32[32,1,2304]{2,1,0:T(1,128)S(1)}, u32[]{:S(2)}, u32[]{:S(2)}) %all-to-all-start) | async-done | bytes 294944 | tf_op jit(solution)/shard_map/all_to_all | solution.py:337
  28.6 14.9 %physics.1 = f32[288,128]{1,0:T(8,128)S(1)} custom-call(f32[576,128]{1,0:T(8,128)S(1)} %bitcast.7, bf16[256,9216]{1,0:T(8,128)(2,1)} %cm_ref.1, bf16[256,9216]{1,0:T(8,128)(2,1)} %cm_ref.1, f32[4608,256]{1,0:T(8,128)} %get-tuple-element.23.rate_ref, f32[4608,256]{1,0:T(8,128)} %get-tuple-element.24.both_ref), custom_call_target="tpu_custom_call" | custom-call | tf_op jit(solution)/shard_map/physics/pallas_call | solution.py:355
  43.5 10.5 %all_to_all.18 = f32[32,1,1152]{2,1,0:T(1,128)S(1)} all-to-all(f32[32,1,1152]{2,1,0:T(1,128)S(1)} %bitcast.11), channel_id=1, replica_groups=mesh['sec'=4,'blk'=8] {'sec','blk'}, dimensions={0} | all-to-all | bytes 294912 | tf_op jit(solution)/shard_map/all_to_all | solution.py:375
  54.1 0.9 %finish.1 = f32[144,128]{1,0:T(8,128)} custom-call(f32[144,128]{1,0:T(8,128)S(1)} %get-tuple-element.20.dyn_ref, s32[3,128]{1,0:T(4,128)S(1)} %get-tuple-element.21.place_ref, f32[288,128]{1,0:T(8,128)S(1)} %bitcast.10), custom_call_target="tpu_custom_call" | custom-call | tf_op jit(solution)/shard_map/finish/pallas_call | solution.py:376
Async XLA Ops:
  1.1 9.6 %collective-permute-start.1 = (f32[144,8]{1,0:T(8,128)S(1)}, f32[144,8]{1,0:T(8,128)S(1)}, u32[]{:S(2)}, u32[]{:S(2)}) collective-permute-start(f32[144,8]{1,0:T(8,128)S(1)} %get-tuple-element.25), channel_id=1, source_target_pairs={{0,1},{1,0},{2,3},{3,2},{4,5},{5,4},{6,7},{7,6},{8,9},{9,8},{10,11... | collective-permute-start | bytes 13832 | tf_op jit(solution)/shard_map/ppermute | solution.py:311
  1.6 9.1 %collective-permute-start = (f32[144,8]{1,0:T(8,128)S(1)}, f32[144,8]{1,0:T(8,128)S(1)}, u32[]{:S(2)}, u32[]{:S(2)}) collective-permute-start(f32[144,8]{1,0:T(8,128)S(1)} %get-tuple-element.26), channel_id=1, source_target_pairs={{0,31},{1,2},{2,1},{3,4},{4,3},{5,6},{6,5},{7,8},{8,7},{9,10},{10,... | collective-permute-start | bytes 13832 | tf_op jit(solution)/shard_map/ppermute | solution.py:310
  8.2 0.9 %copy-start = (f32[2,72,128]{2,1,0:T(8,128)S(1)}, f32[2,72,128]{2,1,0:T(8,128)}, u32[]{:S(2)}) copy-start(f32[2,72,128]{2,1,0:T(8,128)} %param.5) | copy-start | bytes 221188
  9.1 0.7 %copy-start.1 = (s32[4,128]{1,0:T(4,128)S(1)}, s32[4,128]{1,0:T(4,128)}, u32[]{:S(2)}) copy-start(s32[4,128]{1,0:T(4,128)} %near_ref.1) | copy-start | bytes 6148
  9.8 0.7 %copy-start.2 = (s32[128,1]{0,1:T(1,128)S(1)}, s32[128,1]{0,1:T(1,128)}, u32[]{:S(2)}) copy-start(s32[128,1]{0,1:T(1,128)} %param.7) | copy-start | bytes 1540
  12.0 16.6 %all-to-all-start = ((f32[32,1,2304]{2,1,0:T(1,128)}), f32[32,1,2304]{2,1,0:T(1,128)S(1)}, u32[]{:S(2)}, u32[]{:S(2)}) async-start(f32[32,1,2304]{2,1,0:T(1,128)} %bitcast.2), calls=%async_computation | async-start | bytes 589824 | tf_op jit(solution)/shard_map/all_to_all | solution.py:337

commit v5 on v3

--- a/solution.py
+++ b/solution.py
@@ -7,6 +7,7 @@
 from jax.experimental import pallas as pl
 from jax.experimental.pallas import tpu as pltpu
 from jax.sharding import PartitionSpec as P
+
 
 SUB = 4
 REACH = 8
@@ -19,6 +20,8 @@
 TN = (((0,), (0,)), ((), ()))
 VMEM = pl.BlockSpec(memory_space=pltpu.VMEM)
 FULL = 60 * 1024 * 1024
+LOG = 0.3 * math.log2(math.e)
+TRIO = 3
 
 
 def parts_of(x):
@@ -104,21 +107,21 @@
         out_ref[s * each + tiles * cap:(s + 1) * each, :] = tail[2 * s:2 * s + 2]
 
 
-def prepare_kernel(crmx, ct_ref, cm_ref, mask_ref, yt_ref, ym_ref, rate_ref, both_ref):
-    width = ct_ref.shape[1]
+def near_matrix(rows, columns, crmx, centre, side):
+    row = lax.broadcasted_iota(jnp.int32, (rows, columns), 0)
+    col = lax.broadcasted_iota(jnp.int32, (rows, columns), 1)
+    place = row & (crmx - 1)
+    apart = (((place & 7) * (crmx // 8) + (place >> 3)) - col) & (crmx - 1)
+    same = (row // crmx) == (col // crmx)
+    off = jnp.where((apart == 1) | (apart == crmx - 1), side, 0.0)
+    return jnp.where(same, jnp.where(apart == 0, centre, off), 0.0)
+
+
+def prepare_kernel(crmx, mask_ref, rate_ref, both_ref):
     per = GROUP * crmx
-    row = lax.broadcasted_iota(jnp.int32, (per, per), 0)
-    col = lax.broadcasted_iota(jnp.int32, (per, per), 1)
-    place = row % crmx
-    apart = (((place % 8) * (crmx // 8) + place // 8) - col) & (crmx - 1)
-    same = (row // crmx) == (col // crmx)
-    move = jnp.where(same & (apart == 0), 1.0, 0.0)
-    spread = jnp.where(same & ((apart == 1) | (apart == crmx - 1)), 1.0, 3.0 * move)
-    move, spread = move.astype(BF16), spread.astype(BF16)
-    for q in range(width // per):
+    move = near_matrix(per, per, crmx, 1.0, 0.0).astype(BF16)
+    for q in range(mask_ref.shape[1] // per):
         part = slice(q * per, (q + 1) * per)
-        yt_ref[part, :] = lax.dot_general(spread, ct_ref[:, part], NT, preferred_element_type=F32)
-        ym_ref[part, :] = lax.dot_general(spread, cm_ref[:, part], NT, preferred_element_type=F32)
         ice = lax.dot_general(move, mask_ref[:, part].astype(F32).astype(BF16), NT, preferred_element_type=F32)
         rate_ref[part, :] = 0.7 - 0.4 * ice
         both_ref[part, :] = 0.7 - 0.31 * ice
@@ -150,16 +153,25 @@
     return jnp.concatenate(columns, axis=0)
 
 
-def physics_kernel(levels, crmx, dense, arrived_ref, yt_ref, ym_ref, rate_ref, both_ref, out_ref, rows_ref, sums_ref):
-    slots = yt_ref.shape[1]
+def physics_kernel(levels, crmx, dense, arrived_ref, ct_ref, cm_ref, nt_ref, nm_ref, rate_ref, both_ref, out_ref, *scratch):
+    rows_ref, sums_ref, first_ref = scratch[:3]
+    ahead = scratch[3:]
+    slots = ct_ref.shape[0]
+    halves = slots // 128
     steps = crmx // 8
-    scale = 0.3 * math.log2(math.e)
+    step = pl.program_id(0)
+    here = rate_ref.shape[0] // crmx
+    part = GROUP * crmx
     shift = [math.log(0.8 * 5.0 ** j) / 0.3 for j in range(SUB + 1)]
-    step = pl.program_id(0)
-    per = yt_ref.shape[0] // crmx
+
+    def diffuse(q, temp, moist):
+        for ref, source in zip(ahead[2 * q:2 * q + 2], (temp, moist)):
+            ref[...] = lax.dot_general(first_ref[...], source, NT, preferred_element_type=F32)
 
     @pl.when(step == 0)
     def _():
+        first_ref[...] = near_matrix(part, part, crmx, 3.0, 1.0).astype(BF16)
+        diffuse(0, ct_ref[:, :part], cm_ref[:, :part])
         arrived = arrivals(dense, arrived_ref, slots, 4 * levels)
         temp, moist, push, wet = [arrived[i * levels:(i + 1) * levels] for i in range(4)]
         push, wet = push * (1.0 / SUB), wet * (1.0 / SUB)
@@ -167,18 +179,20 @@
         for j in range(2, SUB + 1):
             tables += [5.0 ** j * (push + (shift[j] - shift[j - 1])), 5.0 ** j * wet]
         for i, table in enumerate(tables):
-            for half in range(slots // 128):
+            for half in range(halves):
                 rows_ref[half, i * levels:(i + 1) * levels] = table[:, half * 128:(half + 1) * 128]
 
     def unit(inner, half):
         lanes = pl.ds(half * 128, 128)
         base = inner * crmx
-        level = step * per + inner
+        level = step * here + inner
         get = lambda ref, k: ref[pl.ds(base + 8 * k, 8), lanes]
         const = lambda i: rows_ref[half, pl.ds(level + i * levels, 8, stride=0), :]
-        add_t, add_m = const(0), const(1)
-        temp = [get(yt_ref, k) + add_t for k in range(steps)]
-        moist = [get(ym_ref, k) + add_m for k in range(steps)]
+        q, within = inner // GROUP, inner % GROUP * crmx
+        temp, moist = [
+            [ahead[2 * q + i][pl.ds(within + 8 * k, 8), lanes] + add for k in range(steps)]
+            for i, add in enumerate((const(0), const(1)))
+        ]
         for j in range(1, SUB + 1):
             if j > 1:
                 spread = []
@@ -188,9 +202,8 @@
                     ring = [before] + field + [after]
                     spread.append([((ring[k] + ring[k + 2]) + 3.0 * field[k]) + add for k in range(steps)])
                 temp, moist = spread
-            temp, moist = list(temp), list(moist)
             for k in range(steps):
-                over = jnp.maximum(moist[k] - jnp.exp2((scale / 5.0 ** j) * temp[k]), 0.0)
+                over = jnp.maximum(moist[k] - jnp.exp2((LOG / 5.0 ** j) * temp[k]), 0.0)
                 moist[k] = moist[k] - get(rate_ref, k) * over
                 temp[k] = temp[k] + get(both_ref, k) * over
         for i, field in enumerate((temp, moist)):
@@ -198,19 +211,22 @@
                 field = [a + b for a, b in zip(field[0::2], field[1::2])]
             sums_ref[half, pl.ds(pl.multiple_of((i * levels + level) * 8, 8), 8), :] = field[0]
 
-    for inner in range(per):
-        for half in range(slots // 128):
+    for q in range(1, here // GROUP):
+        diffuse(q, ct_ref[:, q * part:(q + 1) * part], cm_ref[:, q * part:(q + 1) * part])
+    for inner in range(here):
+        if inner == GROUP:
+            diffuse(0, nt_ref[...], nm_ref[...])
+        for half in range(halves):
             unit(inner, half)
 
     @pl.when(step == pl.num_programs(0) - 1)
     def _():
-        factor = 1.0 / (crmx * 5.0 ** SUB)
         total = 2 * levels
-        for half in range(slots // 128):
+        for half in range(halves):
             summed = sums_ref[half, pl.ds(0, total, stride=8), :]
             for s in range(1, 8):
                 summed = summed + sums_ref[half, pl.ds(s, total, stride=8), :]
-            mean = summed * factor
+            mean = summed * (1.0 / (crmx * 5.0 ** SUB))
             mean = jnp.concatenate([mean[:levels] - shift[SUB], mean[levels:]], axis=0)
             if dense is None:
                 mean = jnp.concatenate([mean, jnp.zeros((256 - total, 128), F32)], axis=0)
@@ -266,11 +282,9 @@
     mate = [(i, i ^ 1) for i in range(ndev)]
     odd = me % 2
     first, last = flat[:, :REACH], flat[:, cdev - REACH:]
-    from_far = lax.ppermute(jnp.where(odd == 1, last, first), AXES, far)
-    from_mate = lax.ppermute(jnp.where(odd == 1, first, last), AXES, mate)
-
-    def whole(*shape):
-        return pl.BlockSpec(shape, lambda i: (0,) * len(shape))
+    to_far, to_mate = jnp.where(odd == 1, last, first), jnp.where(odd == 1, first, last)
+    from_far = lax.ppermute(to_far, AXES, far)
+    from_mate = lax.ppermute(to_mate, AXES, mate)
 
     index_out = [sds((rows, cdev), F32)] * 2 + [sds((2 * REACH, cdev), BF16), sds((slots, cdev), BF16)]
     index_out.append(sds((1 if dense is None else dense[1] + 2, cdev), jnp.int32))
@@ -278,8 +292,7 @@
         index_out.append(sds((slots // 4, 4 * cdev), BF16))
     same, part, edge, hot, place, *tail = pl.pallas_call(
         functools.partial(index_kernel, (cap, slots, cdev * ndev, dense)),
-        grid=(1,),
-        in_specs=[whole(rows, cdev), whole(*neighbors.shape), whole(1, cdev)],
+        in_specs=[VMEM] * 3,
         out_specs=[VMEM] * len(index_out),
         out_shape=index_out,
         compiler_params=pltpu.CompilerParams(vmem_limit_bytes=12 << 20),
@@ -296,34 +309,37 @@
     arrived = lax.all_to_all(outgoing.reshape(ndev, cap * 2 * rows), AXES, split_axis=0, concat_axis=0, tiled=True)
     arrived = arrived.reshape(outgoing.shape)
 
-    block = 3 * GROUP * crmx
+    block = TRIO * GROUP * crmx
     count = levels * crmx // block
     take = lambda offset: pl.BlockSpec((slots, block), lambda g: (0, g + offset))
-    big = sds((levels * crmx, slots), F32)
-    prepared = pl.pallas_call(
+    last = TRIO * (count - 1)
+    soon = lambda offset: pl.BlockSpec((slots, GROUP * crmx), lambda g: (0, TRIO * offset + jnp.minimum(TRIO * (g + 1), last)))
+    rates_spec = [pl.BlockSpec((block, slots), lambda g: (g, 0))] * 2
+    rates = pl.pallas_call(
         functools.partial(prepare_kernel, crmx),
         grid=(count,),
-        in_specs=[take(0), take(count), take(0)],
-        out_specs=[pl.BlockSpec((block, slots), lambda g: (g, 0))] * 4,
-        out_shape=[big] * 4,
+        in_specs=[take(0)],
+        out_specs=rates_spec,
+        out_shape=[sds((levels * crmx, slots), F32)] * 2,
         compiler_params=pltpu.CompilerParams(vmem_limit_bytes=FULL),
-        cost_estimate=pl.CostEstimate(flops=6 * slots * levels * crmx * GROUP * crmx, transcendentals=0, bytes_accessed=4 * slots * wide),
+        cost_estimate=pl.CostEstimate(flops=2 * slots * levels * crmx * GROUP * crmx, transcendentals=0, bytes_accessed=6 * slots * wide),
         name="prepare",
-    )(crm_state, crm_state, phase_mask)
+    )(phase_mask)
 
     back = pl.pallas_call(
         functools.partial(physics_kernel, levels, crmx, dense),
         grid=(count,),
-        in_specs=[VMEM] + [pl.BlockSpec((block, slots), lambda g: (g, 0))] * 4,
+        in_specs=[VMEM, take(0), take(count), soon(0), soon(count)] + rates_spec,
         out_specs=VMEM,
         out_shape=sds((slots, rows) if dense is None else (ndev * back_each, 128), F32),
         scratch_shapes=[
             pltpu.VMEM((slots // 128, 2 * SUB * levels + 8, 128), F32),
             pltpu.VMEM((slots // 128, 8 * rows, 128), F32),
-        ],
+            pltpu.VMEM((GROUP * crmx, GROUP * crmx), BF16),
+        ] + [pltpu.VMEM((GROUP * crmx, slots), F32)] * (2 * TRIO),
         compiler_params=pltpu.CompilerParams(vmem_limit_bytes=53000 << 10),
         name="physics",
-    )(arrived, *prepared)
+    )(arrived, crm_state, crm_state, crm_state, crm_state, *rates)
     returned = lax.all_to_all(back.reshape(ndev, cap * rows), AXES, split_axis=0, concat_axis=0, tiled=True)
     out = pl.pallas_call(
         functools.partial(finish_kernel, dense),

time: 56.6 us -> 54.2 us (0.958)
  blocking collectives: 14 us -> 10.5 us
  waiting for transfers between devices: 0.01 us -> 3.49 us
  Pallas kernels: 26.4 us -> 24 us
    pallas_call x1, Pallas kernels: 11.4 us -> 7.83 us  [local(): pl.pallas_call(functools.partial(prepare_kernel, crmx), grid=(count,), in...]
    all_to_all x1, waiting for transfers between devices: 0.01 us -> 3.49 us  [local(): lax.all_to_all(outgoing.reshape(ndev, cap * 2 * rows), AXES, split_axis=0...]
    all_to_all x1, blocking collectives: 14 us -> 10.5 us  [local(): lax.all_to_all(back.reshape(ndev, cap * rows), AXES, split_axis=0, concat...]
    pallas_call x1, Pallas kernels: 12.4 us -> 13.6 us  [local(): pl.pallas_call(functools.partial(physics_kernel, levels, crmx, dense), gr...]
  transfers between devices with their start and end apart: 3 -> 3, of which waited for: 0 -> 1; matrix products, arithmetic and copies ran while one was open for 0% -> 0% of each run, Pallas kernels for 21% -> 15%
where the time goes in v5:
time: 54.2 us; the launch traced here: 53.7 us
  Pallas kernels  24 us (44%)
  starting transfers between devices  12.4 us (23%)
  blocking collectives  10.5 us (19%)
  waiting for transfers between devices  3.49 us (6%)
  local copies, waits for them, and re-layouts  2.22 us (4%)
  other arithmetic  1.04 us (2%)
    pallas_call x1, Pallas kernels, local(): pl.pallas_call(functools.partial(physics_kernel, levels, crmx, dense), gr...  13.6 us
    all_to_all x1, blocking collectives, local(): lax.all_to_all(back.reshape(ndev, cap * rows), AXES, split_axis=0, concat...  10.5 us
    pallas_call x1, Pallas kernels, local(): pl.pallas_call(functools.partial(prepare_kernel, crmx), grid=(count,), in...  7.83 us
    ppermute x1, starting transfers between devices, local(): from_far = lax.ppermute(to_far, AXES, far)  6.58 us
    all_to_all x1, starting transfers between devices, local(): lax.all_to_all(outgoing.reshape(ndev, cap * 2 * rows), AXES, split_axis=0...  5.25 us
    all_to_all x1, waiting for transfers between devices, local(): lax.all_to_all(outgoing.reshape(ndev, cap * 2 * rows), AXES, split_axis=0...  3.49 us
    unnamed x6, local copies, waits for them, and re-layouts  2.22 us
    pallas_call x1, Pallas kernels, local(): pl.pallas_call(functools.partial(pack_kernel, dense), in_specs=[VMEM] * (...  1.36 us
  transfers between devices with their start and end apart: 3, of which 1 were waited for; matrix products, arithmetic and copies ran while one was open for 0% of the time, Pallas kernels for 15%

profile of v5, /device:TPU:0, one launch (start us, length us, event | category | flops | bytes accessed | tf_op | source)
XLA Modules:
  0.0 53.7 jit_solution(280523332316541730)
XLA Ops:
  0.0 1.0 %slice_select_fusion = (f32[144,8]{1,0:T(8,128)S(1)}, f32[144,8]{1,0:T(8,128)S(1)}) fusion(f32[144,128]{1,0:T(8,128)} %bitcast.8, pred[]{:T(512)S(6)} %eq.6), kind=kLoop, calls=%fused_computation | loop fusion | flops 2304 | bytes 18433 | tf_op jit(solution)/shard_map/jit(_where)/select_n | solution.py:285
  1.1 0.6 %collective-permute-start.1 = (f32[144,8]{1,0:T(8,128)S(1)}, f32[144,8]{1,0:T(8,128)S(1)}, u32[]{:S(2)}, u32[]{:S(2)}) collective-permute-start(f32[144,8]{1,0:T(8,128)S(1)} %get-tuple-element.25), channel_id=1, source_target_pairs={{0,1},{1,0},{2,3},{3,2},{4,5},{5,4},{6,7},{7,6},{8,9},{9,8},{10,11... | collective-permute-start | bytes 13832 | tf_op jit(solution)/shard_map/ppermute | solution.py:287
  1.6 6.6 %collective-permute-start = (f32[144,8]{1,0:T(8,128)S(1)}, f32[144,8]{1,0:T(8,128)S(1)}, u32[]{:S(2)}, u32[]{:S(2)}) collective-permute-start(f32[144,8]{1,0:T(8,128)S(1)} %get-tuple-element.26), channel_id=1, source_target_pairs={{0,31},{1,2},{2,1},{3,4},{4,3},{5,6},{6,5},{7,8},{8,7},{9,10},{10,... | collective-permute-start | bytes 13832 | tf_op jit(solution)/shard_map/ppermute | solution.py:286
  8.2 0.0 copy-start
  8.2 0.9 %copy-done = f32[2,72,128]{2,1,0:T(8,128)S(1)} copy-done((f32[2,72,128]{2,1,0:T(8,128)S(1)}, f32[2,72,128]{2,1,0:T(8,128)}, u32[]{:S(2)}) %copy-start) | copy-done | bytes 73752
  9.1 0.0 copy-start.1
  9.1 0.7 %copy-done.1 = s32[4,128]{1,0:T(4,128)S(1)} copy-done((s32[4,128]{1,0:T(4,128)S(1)}, s32[4,128]{1,0:T(4,128)}, u32[]{:S(2)}) %copy-start.1) | copy-done | bytes 2072
  9.8 0.0 copy-start.2
  9.8 0.7 %copy-done.2 = s32[128,1]{0,1:T(1,128)S(1)} copy-done((s32[128,1]{0,1:T(1,128)S(1)}, s32[128,1]{0,1:T(1,128)}, u32[]{:S(2)}) %copy-start.2) | copy-done | bytes 536
  10.4 0.2 index.1
  10.7 0.0 collective-permute-done.1.mate_ref
  10.7 0.0 collective-permute-done.far_ref
  10.7 1.4 %pack.1 = (f32[576,128]{1,0:T(8,128)}, f32[144,128]{1,0:T(8,128)S(1)}) custom-call(f32[144,128]{1,0:T(8,128)S(1)} %get-tuple-element.15.state_ref, f32[144,128]{1,0:T(8,128)S(1)} %get-tuple-element.16.part_ref, bf16[16,128]{1,0:T(8,128)(2,1)S(1)} %get-tuple-element.17.edge_ref, bf16[256,128]{1,0:T(8,128)(2,1)S(1)} %get-tuple-element.18.hot_ref, ...), custom_call_target="tpu_custom_call" | custom-call | tf_op jit(solution)/shard_map/pack/pallas_call | solution.py:301
  12.0 5.2 %all-to-all-start = ((f32[32,1,2304]{2,1,0:T(1,128)}), f32[32,1,2304]{2,1,0:T(1,128)S(1)}, u32[]{:S(2)}, u32[]{:S(2)}) async-start(f32[32,1,2304]{2,1,0:T(1,128)} %bitcast.2), calls=%async_computation | async-start | bytes 589824 | tf_op jit(solution)/shard_map/all_to_all | solution.py:309
  17.3 7.8 %prepare.1 = (f32[4608,256]{1,0:T(8,128)}, f32[4608,256]{1,0:T(8,128)}) custom-call(s32[256,4608]{1,0:T(8,128)} %mask_ref.1), custom_call_target="tpu_custom_call" | custom-call | flops 603979776 | bytes 14155776 | tf_op jit(solution)/shard_map/prepare/pallas_call | solution.py:318
  25.1 3.5 %all-to-all-done = f32[32,1,2304]{2,1,0:T(1,128)S(1)} async-done(((f32[32,1,2304]{2,1,0:T(1,128)}), f32[32,1,2304]{2,1,0:T(1,128)S(1)}, u32[]{:S(2)}, u32[]{:S(2)}) %all-to-all-start) | async-done | bytes 294944 | tf_op jit(solution)/shard_map/all_to_all | solution.py:309
  28.6 13.6 %physics.1 = f32[288,128]{1,0:T(8,128)S(1)} custom-call(f32[576,128]{1,0:T(8,128)S(1)} %bitcast.7, bf16[256,9216]{1,0:T(8,128)(2,1)} %nm_ref.1, bf16[256,9216]{1,0:T(8,128)(2,1)} %nm_ref.1, bf16[256,9216]{1,0:T(8,128)(2,1)} %nm_ref.1, bf16[256,9216]{1,0:T(8,128)(2,1)} %nm_ref.1, f32[4608,256]{1,0:T(8,128)} %get-tuple-element.23.rate_ref, ...), custom_call_target="tpu_custom_call" | custom-call | tf_op jit(solution)/shard_map/physics/pallas_call | solution.py:329
  42.2 10.5 %all_to_all.18 = f32[32,1,1152]{2,1,0:T(1,128)S(1)} all-to-all(f32[32,1,1152]{2,1,0:T(1,128)S(1)} %bitcast.10), channel_id=1, replica_groups=mesh['sec'=4,'blk'=8] {'sec','blk'}, dimensions={0} | all-to-all | bytes 294912 | tf_op jit(solution)/shard_map/all_to_all | solution.py:343
  52.8 0.9 %finish.1 = f32[144,128]{1,0:T(8,128)} custom-call(f32[144,128]{1,0:T(8,128)S(1)} %get-tuple-element.20.dyn_ref, s32[3,128]{1,0:T(4,128)S(1)} %get-tuple-element.21.place_ref, f32[288,128]{1,0:T(8,128)S(1)} %bitcast.11), custom_call_target="tpu_custom_call" | custom-call | tf_op jit(solution)/shard_map/finish/pallas_call | solution.py:344
Async XLA Ops:
  1.1 9.6 %collective-permute-start.1 = (f32[144,8]{1,0:T(8,128)S(1)}, f32[144,8]{1,0:T(8,128)S(1)}, u32[]{:S(2)}, u32[]{:S(2)}) collective-permute-start(f32[144,8]{1,0:T(8,128)S(1)} %get-tuple-element.25), channel_id=1, source_target_pairs={{0,1},{1,0},{2,3},{3,2},{4,5},{5,4},{6,7},{7,6},{8,9},{9,8},{10,11... | collective-permute-start | bytes 13832 | tf_op jit(solution)/shard_map/ppermute | solution.py:287
  1.6 9.1 %collective-permute-start = (f32[144,8]{1,0:T(8,128)S(1)}, f32[144,8]{1,0:T(8,128)S(1)}, u32[]{:S(2)}, u32[]{:S(2)}) collective-permute-start(f32[144,8]{1,0:T(8,128)S(1)} %get-tuple-element.26), channel_id=1, source_target_pairs={{0,31},{1,2},{2,1},{3,4},{4,3},{5,6},{6,5},{7,8},{8,7},{9,10},{10,... | collective-permute-start | bytes 13832 | tf_op jit(solution)/shard_map/ppermute | solution.py:286
  8.2 0.9 %copy-start = (f32[2,72,128]{2,1,0:T(8,128)S(1)}, f32[2,72,128]{2,1,0:T(8,128)}, u32[]{:S(2)}) copy-start(f32[2,72,128]{2,1,0:T(8,128)} %param.5) | copy-start | bytes 221188
  9.1 0.7 %copy-start.1 = (s32[4,128]{1,0:T(4,128)S(1)}, s32[4,128]{1,0:T(4,128)}, u32[]{:S(2)}) copy-start(s32[4,128]{1,0:T(4,128)} %near_ref.1) | copy-start | bytes 6148
  9.8 0.7 %copy-start.2 = (s32[128,1]{0,1:T(1,128)S(1)}, s32[128,1]{0,1:T(1,128)}, u32[]{:S(2)}) copy-start(s32[128,1]{0,1:T(1,128)} %param.7) | copy-start | bytes 1540
  12.0 16.6 %all-to-all-start = ((f32[32,1,2304]{2,1,0:T(1,128)}), f32[32,1,2304]{2,1,0:T(1,128)S(1)}, u32[]{:S(2)}, u32[]{:S(2)}) async-start(f32[32,1,2304]{2,1,0:T(1,128)} %bitcast.2), calls=%async_computation | async-start | bytes 589824 | tf_op jit(solution)/shard_map/all_to_all | solution.py:309

commit v6 on v5

--- a/solution.py
+++ b/solution.py
@@ -19,9 +19,9 @@
 NN = (((1,), (0,)), ((), ()))
 TN = (((0,), (0,)), ((), ()))
 VMEM = pl.BlockSpec(memory_space=pltpu.VMEM)
-FULL = 60 * 1024 * 1024
 LOG = 0.3 * math.log2(math.e)
 TRIO = 3
+HEAD = 8
 
 
 def parts_of(x):
@@ -117,7 +117,11 @@
     return jnp.where(same, jnp.where(apart == 0, centre, off), 0.0)
 
 
-def prepare_kernel(crmx, mask_ref, rate_ref, both_ref):
+def diffusion(first, source):
+    return lax.dot_general(first, source, NT, preferred_element_type=F32)
+
+
+def prepare_kernel(crmx, mask_ref, ct_ref, cm_ref, rate_ref, both_ref, *head_refs):
     per = GROUP * crmx
     move = near_matrix(per, per, crmx, 1.0, 0.0).astype(BF16)
     for q in range(mask_ref.shape[1] // per):
@@ -125,6 +129,17 @@
         ice = lax.dot_general(move, mask_ref[:, part].astype(F32).astype(BF16), NT, preferred_element_type=F32)
         rate_ref[part, :] = 0.7 - 0.4 * ice
         both_ref[part, :] = 0.7 - 0.31 * ice
+
+    @pl.when(pl.program_id(0) == 0)
+    def _():
+        yt_ref, ym_ref, head_rate_ref = head_refs
+        size = yt_ref.shape[0]
+        first = near_matrix(per, per, crmx, 3.0, 1.0).astype(BF16)
+        for q in range(size // per):
+            part = slice(q * per, (q + 1) * per)
+            yt_ref[part, :] = diffusion(first, ct_ref[:, part])
+            ym_ref[part, :] = diffusion(first, cm_ref[:, part])
+        head_rate_ref[...] = rate_ref[:size]
 
 
 def arrivals(dense, arrived_ref, slots, wide):
@@ -153,46 +168,67 @@
     return jnp.concatenate(columns, axis=0)
 
 
-def physics_kernel(levels, crmx, dense, arrived_ref, ct_ref, cm_ref, nt_ref, nm_ref, rate_ref, both_ref, out_ref, *scratch):
-    rows_ref, sums_ref, first_ref = scratch[:3]
-    ahead = scratch[3:]
-    slots = ct_ref.shape[0]
+def physics_kernel(levels, crmx, dense, arrived_ref, *refs):
+    head, (crm_hbm, rate_hbm, both_hbm, out_ref), refs = refs[:3], refs[3:7], refs[7:]
+    rows_ref, sums_ref, first_ref, crm_sems, rate_sems = refs[:5]
+    head = (*head, refs[17])
+    fields, coefs, crm_bufs = (refs[5:7], refs[7:9]), (refs[9:11], refs[11:13]), (refs[13:15], refs[15:17])
+    slots = crm_hbm.shape[0]
     halves = slots // 128
     steps = crmx // 8
-    step = pl.program_id(0)
-    here = rate_ref.shape[0] // crmx
     part = GROUP * crmx
+    size = head[0].shape[0]
+    here = size // crmx
+    count = levels // here
     shift = [math.log(0.8 * 5.0 ** j) / 0.3 for j in range(SUB + 1)]
 
-    def diffuse(q, temp, moist):
-        for ref, source in zip(ahead[2 * q:2 * q + 2], (temp, moist)):
-            ref[...] = lax.dot_general(first_ref[...], source, NT, preferred_element_type=F32)
-
-    @pl.when(step == 0)
-    def _():
-        first_ref[...] = near_matrix(part, part, crmx, 3.0, 1.0).astype(BF16)
-        diffuse(0, ct_ref[:, :part], cm_ref[:, :part])
-        arrived = arrivals(dense, arrived_ref, slots, 4 * levels)
-        temp, moist, push, wet = [arrived[i * levels:(i + 1) * levels] for i in range(4)]
-        push, wet = push * (1.0 / SUB), wet * (1.0 / SUB)
-        tables = [5.0 * (temp + push + shift[1]), 5.0 * (moist + wet)]
-        for j in range(2, SUB + 1):
-            tables += [5.0 ** j * (push + (shift[j] - shift[j - 1])), 5.0 ** j * wet]
-        for i, table in enumerate(tables):
-            for half in range(halves):
-                rows_ref[half, i * levels:(i + 1) * levels] = table[:, half * 128:(half + 1) * 128]
-
-    def unit(inner, half):
+    def crm_copies(group, k):
+        width = levels * crmx
+        at = [pl.ds(pl.multiple_of(i * width + group * size, 128), size) for i in range(2)]
+        return [pltpu.make_async_copy(crm_hbm.at[:, at[i]], crm_bufs[k][i], crm_sems.at[k, i]) for i in range(2)]
+
+    def rate_copies(group, k):
+        at = pl.ds(pl.multiple_of(group * size, 8), size)
+        return [
+            pltpu.make_async_copy(ref.at[at, :], coefs[k][i], rate_sems.at[k, i])
+            for i, ref in enumerate((rate_hbm, both_hbm))
+        ]
+
+    def start(copies):
+        for copy in copies:
+            copy.start()
+
+    def wait(copies):
+        for copy in copies:
+            copy.wait()
+
+    def diffuse(k):
+        for ref, source in zip(fields[k], crm_bufs[k]):
+            for q in range(size // part):
+                cut = slice(q * part, (q + 1) * part)
+                ref[cut, :] = diffusion(first_ref[...], source[:, cut])
+
+    for group in (1, 2):
+        start(crm_copies(group, (group - 1) % 2))
+        start(rate_copies(group, (group - 1) % 2))
+    first_ref[...] = near_matrix(part, part, crmx, 3.0, 1.0).astype(BF16)
+    arrived = arrivals(dense, arrived_ref, slots, 4 * levels)
+    temp, moist, push, wet = [arrived[i * levels:(i + 1) * levels] for i in range(4)]
+    push, wet = push * (1.0 / SUB), wet * (1.0 / SUB)
+    tables = [5.0 * (temp + push + shift[1]), 5.0 * (moist + wet)]
+    for j in range(2, SUB + 1):
+        tables += [5.0 ** j * (push + (shift[j] - shift[j - 1])), 5.0 ** j * wet]
+    for i, table in enumerate(tables):
+        for half in range(halves):
+            rows_ref[half, i * levels:(i + 1) * levels] = table[:, half * 128:(half + 1) * 128]
+
+    def unit(group, inner, half, sources):
         lanes = pl.ds(half * 128, 128)
         base = inner * crmx
-        level = step * here + inner
+        level = group * here + inner
         get = lambda ref, k: ref[pl.ds(base + 8 * k, 8), lanes]
         const = lambda i: rows_ref[half, pl.ds(level + i * levels, 8, stride=0), :]
-        q, within = inner // GROUP, inner % GROUP * crmx
-        temp, moist = [
-            [ahead[2 * q + i][pl.ds(within + 8 * k, 8), lanes] + add for k in range(steps)]
-            for i, add in enumerate((const(0), const(1)))
-        ]
+        temp, moist = [[get(sources[i], k) + add for k in range(steps)] for i, add in enumerate((const(0), const(1)))]
         for j in range(1, SUB + 1):
             if j > 1:
                 spread = []
@@ -204,47 +240,69 @@
                 temp, moist = spread
             for k in range(steps):
                 over = jnp.maximum(moist[k] - jnp.exp2((LOG / 5.0 ** j) * temp[k]), 0.0)
-                moist[k] = moist[k] - get(rate_ref, k) * over
-                temp[k] = temp[k] + get(both_ref, k) * over
+                moist[k] = moist[k] - get(sources[2], k) * over
+                temp[k] = temp[k] + get(sources[3], k) * over
         for i, field in enumerate((temp, moist)):
             while len(field) > 1:
                 field = [a + b for a, b in zip(field[0::2], field[1::2])]
             sums_ref[half, pl.ds(pl.multiple_of((i * levels + level) * 8, 8), 8), :] = field[0]
 
-    for q in range(1, here // GROUP):
-        diffuse(q, ct_ref[:, q * part:(q + 1) * part], cm_ref[:, q * part:(q + 1) * part])
-    for inner in range(here):
-        if inner == GROUP:
-            diffuse(0, nt_ref[...], nm_ref[...])
-        for half in range(halves):
-            unit(inner, half)
-
-    @pl.when(step == pl.num_programs(0) - 1)
-    def _():
-        total = 2 * levels
-        for half in range(halves):
-            summed = sums_ref[half, pl.ds(0, total, stride=8), :]
-            for s in range(1, 8):
-                summed = summed + sums_ref[half, pl.ds(s, total, stride=8), :]
-            mean = summed * (1.0 / (crmx * 5.0 ** SUB))
-            mean = jnp.concatenate([mean[:levels] - shift[SUB], mean[levels:]], axis=0)
-            if dense is None:
-                mean = jnp.concatenate([mean, jnp.zeros((256 - total, 128), F32)], axis=0)
-                out_ref[pl.ds(half * 128, 128), :] = mean.T[:, :total]
-                continue
-            back, cap = dense[1], 8
-            each = back * cap + 1
-            for t in range(back):
-                block = mean[t * 128:(t + 1) * 128].T
-                for s in range(128 // cap):
-                    to = (half * (128 // cap) + s) * each + t * cap
-                    out_ref[to:to + cap, :] = block[s * cap:(s + 1) * cap]
-            tail = jnp.concatenate([mean[back * 128:]] * cap, axis=0).T
-            group = lax.broadcasted_iota(jnp.int32, (128, 128), 1) // (128 // cap)
-            tail = jnp.where(group == lax.broadcasted_iota(jnp.int32, (128, 128), 0) % cap, tail, 0.0)
+    def run(group, sources):
+        for inner in range(here):
+            for half in range(halves):
+                unit(group, inner, half, sources)
+
+    head[3][...] = 0.7 - 0.775 * (0.7 - head[2][...])
+    wait(crm_copies(1, 0))
+    diffuse(0)
+    run(0, head)
+
+    @pl.loop(0, (count - 1) // 2)
+    def _(trip):
+        for k in range(2):
+            group = 1 + 2 * trip + k
+
+            @pl.when(group + 2 < count)
+            def _():
+                start(crm_copies(group + 2, k))
+
+            wait(rate_copies(group, k))
+
+            @pl.when(group + 1 < count)
+            def _():
+                wait(crm_copies(group + 1, 1 - k))
+
+            diffuse(1 - k)
+            run(group, fields[k] + coefs[k])
+
+            @pl.when(group + 2 < count)
+            def _():
+                start(rate_copies(group + 2, k))
+
+    total = 2 * levels
+    for half in range(halves):
+        summed = sums_ref[half, pl.ds(0, total, stride=8), :]
+        for s in range(1, 8):
+            summed = summed + sums_ref[half, pl.ds(s, total, stride=8), :]
+        mean = summed * (1.0 / (crmx * 5.0 ** SUB))
+        mean = jnp.concatenate([mean[:levels] - shift[SUB], mean[levels:]], axis=0)
+        if dense is None:
+            mean = jnp.concatenate([mean, jnp.zeros((256 - total, 128), F32)], axis=0)
+            out_ref[pl.ds(half * 128, 128), :] = mean.T[:, :total]
+            continue
+        back, cap = dense[1], 8
+        each = back * cap + 1
+        for t in range(back):
+            block = mean[t * 128:(t + 1) * 128].T
             for s in range(128 // cap):
-                to = (half * (128 // cap) + s) * each + back * cap
-                out_ref[to:to + 1, :] = jnp.sum(tail[s * cap:(s + 1) * cap], axis=0, keepdims=True)
+                to = (half * (128 // cap) + s) * each + t * cap
+                out_ref[to:to + cap, :] = block[s * cap:(s + 1) * cap]
+        tail = jnp.concatenate([mean[back * 128:]] * cap, axis=0).T
+        group = lax.broadcasted_iota(jnp.int32, (128, 128), 1) // (128 // cap)
+        tail = jnp.where(group == lax.broadcasted_iota(jnp.int32, (128, 128), 0) % cap, tail, 0.0)
+        for s in range(128 // cap):
+            to = (half * (128 // cap) + s) * each + back * cap
+            out_ref[to:to + 1, :] = jnp.sum(tail[s * cap:(s + 1) * cap], axis=0, keepdims=True)
 
 
 def finish_kernel(dense, dyn_ref, place_ref, back_ref, out_ref):
@@ -312,34 +370,39 @@
     block = TRIO * GROUP * crmx
     count = levels * crmx // block
     take = lambda offset: pl.BlockSpec((slots, block), lambda g: (0, g + offset))
-    last = TRIO * (count - 1)
-    soon = lambda offset: pl.BlockSpec((slots, GROUP * crmx), lambda g: (0, TRIO * offset + jnp.minimum(TRIO * (g + 1), last)))
     rates_spec = [pl.BlockSpec((block, slots), lambda g: (g, 0))] * 2
-    rates = pl.pallas_call(
+    size = HEAD * crmx
+    field, coef = sds((levels * crmx, slots), F32), sds((size, slots), F32)
+    offset = levels // HEAD
+    *rates, yt, ym, head_rate = pl.pallas_call(
         functools.partial(prepare_kernel, crmx),
         grid=(count,),
-        in_specs=[take(0)],
-        out_specs=rates_spec,
-        out_shape=[sds((levels * crmx, slots), F32)] * 2,
-        compiler_params=pltpu.CompilerParams(vmem_limit_bytes=FULL),
+        in_specs=[take(0)] + [pl.BlockSpec((slots, size), lambda g, i=i: (0, i * offset)) for i in range(2)],
+        out_specs=rates_spec + [VMEM] * 3,
+        out_shape=[field] * 2 + [coef] * 3,
+        compiler_params=pltpu.CompilerParams(vmem_limit_bytes=53000 << 10),
         cost_estimate=pl.CostEstimate(flops=2 * slots * levels * crmx * GROUP * crmx, transcendentals=0, bytes_accessed=6 * slots * wide),
         name="prepare",
-    )(phase_mask)
+    )(phase_mask, crm_state, crm_state)
 
     back = pl.pallas_call(
         functools.partial(physics_kernel, levels, crmx, dense),
-        grid=(count,),
-        in_specs=[VMEM, take(0), take(count), soon(0), soon(count)] + rates_spec,
+        in_specs=[VMEM] * 4 + [pl.BlockSpec(memory_space=pl.ANY)] * 3,
         out_specs=VMEM,
         out_shape=sds((slots, rows) if dense is None else (ndev * back_each, 128), F32),
         scratch_shapes=[
             pltpu.VMEM((slots // 128, 2 * SUB * levels + 8, 128), F32),
             pltpu.VMEM((slots // 128, 8 * rows, 128), F32),
             pltpu.VMEM((GROUP * crmx, GROUP * crmx), BF16),
-        ] + [pltpu.VMEM((GROUP * crmx, slots), F32)] * (2 * TRIO),
+            pltpu.SemaphoreType.DMA((2, 2)),
+            pltpu.SemaphoreType.DMA((2, 2)),
+        ]
+        + [pltpu.VMEM((size, slots), F32)] * 8
+        + [pltpu.VMEM((slots, size), BF16)] * 4
+        + [pltpu.VMEM((size, slots), F32)],
         compiler_params=pltpu.CompilerParams(vmem_limit_bytes=53000 << 10),
         name="physics",
-    )(arrived, crm_state, crm_state, crm_state, crm_state, *rates)
+    )(arrived, yt, ym, head_rate, crm_state, *rates)
     returned = lax.all_to_all(back.reshape(ndev, cap * rows), AXES, split_axis=0, concat_axis=0, tiled=True)
     out = pl.pallas_call(
         functools.partial(finish_kernel, dense),

time: 54.2 us -> 54.2 us (level)
  transfers between devices with their start and end apart: 3 -> 3, of which waited for: 1 -> 1; matrix products, arithmetic and copies ran while one was open for 0% -> 0% of each run, Pallas kernels for 15% -> 16%
where the time goes in v6:
time: 54.2 us; the launch traced here: 53.7 us
  Pallas kernels  24 us (44%)
  starting transfers between devices  12.4 us (23%)
  blocking collectives  11 us (20%)
  waiting for transfers between devices  3.02 us (6%)
  local copies, waits for them, and re-layouts  2.22 us (4%)
  other arithmetic  1.04 us (2%)
    pallas_call x1, Pallas kernels, local(): pl.pallas_call(functools.partial(physics_kernel, levels, crmx, dense), in...  13.1 us
    all_to_all x1, blocking collectives, local(): lax.all_to_all(back.reshape(ndev, cap * rows), AXES, split_axis=0, concat...  11 us
    pallas_call x1, Pallas kernels, local(): pl.pallas_call(functools.partial(prepare_kernel, crmx), grid=(count,), in...  8.3 us
    ppermute x1, starting transfers between devices, local(): from_far = lax.ppermute(to_far, AXES, far)  6.58 us
    all_to_all x1, starting transfers between devices, local(): lax.all_to_all(outgoing.reshape(ndev, cap * 2 * rows), AXES, split_axis=0...  5.25 us
    all_to_all x1, waiting for transfers between devices, local(): lax.all_to_all(outgoing.reshape(ndev, cap * 2 * rows), AXES, split_axis=0...  3.02 us
    unnamed x6, local copies, waits for them, and re-layouts  2.22 us
    pallas_call x1, Pallas kernels, local(): pl.pallas_call(functools.partial(pack_kernel, dense), in_specs=[VMEM] * (...  1.36 us
  transfers between devices with their start and end apart: 3, of which 1 were waited for; matrix products, arithmetic and copies ran while one was open for 0% of the time, Pallas kernels for 16%

profile of v6, /device:TPU:0, one launch (start us, length us, event | category | flops | bytes accessed | tf_op | source)
XLA Modules:
  0.0 53.7 jit_solution(8018278396456396047)
XLA Ops:
  0.0 1.0 %slice_select_fusion = (f32[144,8]{1,0:T(8,128)S(1)}, f32[144,8]{1,0:T(8,128)S(1)}) fusion(f32[144,128]{1,0:T(8,128)} %bitcast.8, pred[]{:T(512)S(6)} %eq.6), kind=kLoop, calls=%fused_computation | loop fusion | flops 2304 | bytes 18433 | tf_op jit(solution)/shard_map/jit(_where)/select_n | solution.py:343
  1.1 0.6 %collective-permute-start.1 = (f32[144,8]{1,0:T(8,128)S(1)}, f32[144,8]{1,0:T(8,128)S(1)}, u32[]{:S(2)}, u32[]{:S(2)}) collective-permute-start(f32[144,8]{1,0:T(8,128)S(1)} %get-tuple-element.31), channel_id=1, source_target_pairs={{0,1},{1,0},{2,3},{3,2},{4,5},{5,4},{6,7},{7,6},{8,9},{9,8},{10,11... | collective-permute-start | bytes 13832 | tf_op jit(solution)/shard_map/ppermute | solution.py:345
  1.6 6.6 %collective-permute-start = (f32[144,8]{1,0:T(8,128)S(1)}, f32[144,8]{1,0:T(8,128)S(1)}, u32[]{:S(2)}, u32[]{:S(2)}) collective-permute-start(f32[144,8]{1,0:T(8,128)S(1)} %get-tuple-element.32), channel_id=1, source_target_pairs={{0,31},{1,2},{2,1},{3,4},{4,3},{5,6},{6,5},{7,8},{8,7},{9,10},{10,... | collective-permute-start | bytes 13832 | tf_op jit(solution)/shard_map/ppermute | solution.py:344
  8.2 0.0 copy-start
  8.2 0.9 %copy-done = f32[2,72,128]{2,1,0:T(8,128)S(1)} copy-done((f32[2,72,128]{2,1,0:T(8,128)S(1)}, f32[2,72,128]{2,1,0:T(8,128)}, u32[]{:S(2)}) %copy-start) | copy-done | bytes 73752
  9.1 0.0 copy-start.1
  9.1 0.7 %copy-done.1 = s32[4,128]{1,0:T(4,128)S(1)} copy-done((s32[4,128]{1,0:T(4,128)S(1)}, s32[4,128]{1,0:T(4,128)}, u32[]{:S(2)}) %copy-start.1) | copy-done | bytes 2072
  9.8 0.0 copy-start.2
  9.8 0.7 %copy-done.2 = s32[128,1]{0,1:T(1,128)S(1)} copy-done((s32[128,1]{0,1:T(1,128)S(1)}, s32[128,1]{0,1:T(1,128)}, u32[]{:S(2)}) %copy-start.2) | copy-done | bytes 536
  10.4 0.2 index.1
  10.7 0.0 collective-permute-done.1.mate_ref
  10.7 0.0 collective-permute-done.far_ref
  10.7 1.4 %pack.1 = (f32[576,128]{1,0:T(8,128)}, f32[144,128]{1,0:T(8,128)S(1)}) custom-call(f32[144,128]{1,0:T(8,128)S(1)} %get-tuple-element.18.state_ref, f32[144,128]{1,0:T(8,128)S(1)} %get-tuple-element.19.part_ref, bf16[16,128]{1,0:T(8,128)(2,1)S(1)} %get-tuple-element.20.edge_ref, bf16[256,128]{1,0:T(8,128)(2,1)S(1)} %get-tuple-element.21.hot_ref, ...), custom_call_target="tpu_custom_call" | custom-call | tf_op jit(solution)/shard_map/pack/pallas_call | solution.py:359
  12.0 5.2 %all-to-all-start = ((f32[32,1,2304]{2,1,0:T(1,128)}), f32[32,1,2304]{2,1,0:T(1,128)S(1)}, u32[]{:S(2)}, u32[]{:S(2)}) async-start(f32[32,1,2304]{2,1,0:T(1,128)} %bitcast.2), calls=%async_computation | async-start | bytes 589824 | tf_op jit(solution)/shard_map/all_to_all | solution.py:367
  17.3 8.3 %prepare.1 = (f32[4608,256]{1,0:T(8,128)}, f32[4608,256]{1,0:T(8,128)}, f32[512,256]{1,0:T(8,128)S(1)}, f32[512,256]{1,0:T(8,128)S(1)}, f32[512,256]{1,0:T(8,128)S(1)}) custom-call(s32[256,4608]{1,0:T(8,128)} %mask_ref.1, bf16[256,9216]{1,0:T(8,128)(2,1)} %refs_3_.1, bf16[256,9216]{1,0:T(8,128)(2,1)} %refs_3_.1), custom_call_target="tpu_custom_call" | custom-call | flops 603979776 | bytes 14155776 | tf_op jit(solution)/shard_map/prepare/pallas_call | solution.py:377
  25.6 3.0 %all-to-all-done = f32[32,1,2304]{2,1,0:T(1,128)S(1)} async-done(((f32[32,1,2304]{2,1,0:T(1,128)}), f32[32,1,2304]{2,1,0:T(1,128)S(1)}, u32[]{:S(2)}, u32[]{:S(2)}) %all-to-all-start) | async-done | bytes 294944 | tf_op jit(solution)/shard_map/all_to_all | solution.py:367
  28.6 13.1 %physics.1 = f32[288,128]{1,0:T(8,128)S(1)} custom-call(f32[576,128]{1,0:T(8,128)S(1)} %bitcast.7, f32[512,256]{1,0:T(8,128)S(1)} %get-tuple-element.26.refs_0_, f32[512,256]{1,0:T(8,128)S(1)} %get-tuple-element.27.refs_1_, f32[512,256]{1,0:T(8,128)S(1)} %get-tuple-element.28.refs_2_, bf16[256,9216]{1,0:T(8,128)(2,1)} %refs_3_.1, ...), custom_call_target="tpu_custom_call" | custom-call | tf_op jit(solution)/shard_map/physics/pallas_call | solution.py:388
  41.8 11.0 %all_to_all.18 = f32[32,1,1152]{2,1,0:T(1,128)S(1)} all-to-all(f32[32,1,1152]{2,1,0:T(1,128)S(1)} %bitcast.10), channel_id=1, replica_groups=mesh['sec'=4,'blk'=8] {'sec','blk'}, dimensions={0} | all-to-all | bytes 294912 | tf_op jit(solution)/shard_map/all_to_all | solution.py:406
  52.7 0.9 %finish.1 = f32[144,128]{1,0:T(8,128)} custom-call(f32[144,128]{1,0:T(8,128)S(1)} %get-tuple-element.23.dyn_ref, s32[3,128]{1,0:T(4,128)S(1)} %get-tuple-element.24.place_ref, f32[288,128]{1,0:T(8,128)S(1)} %bitcast.11), custom_call_target="tpu_custom_call" | custom-call | tf_op jit(solution)/shard_map/finish/pallas_call | solution.py:407
Async XLA Ops:
  1.1 9.6 %collective-permute-start.1 = (f32[144,8]{1,0:T(8,128)S(1)}, f32[144,8]{1,0:T(8,128)S(1)}, u32[]{:S(2)}, u32[]{:S(2)}) collective-permute-start(f32[144,8]{1,0:T(8,128)S(1)} %get-tuple-element.31), channel_id=1, source_target_pairs={{0,1},{1,0},{2,3},{3,2},{4,5},{5,4},{6,7},{7,6},{8,9},{9,8},{10,11... | collective-permute-start | bytes 13832 | tf_op jit(solution)/shard_map/ppermute | solution.py:345
  1.6 9.1 %collective-permute-start = (f32[144,8]{1,0:T(8,128)S(1)}, f32[144,8]{1,0:T(8,128)S(1)}, u32[]{:S(2)}, u32[]{:S(2)}) collective-permute-start(f32[144,8]{1,0:T(8,128)S(1)} %get-tuple-element.32), channel_id=1, source_target_pairs={{0,31},{1,2},{2,1},{3,4},{4,3},{5,6},{6,5},{7,8},{8,7},{9,10},{10,... | collective-permute-start | bytes 13832 | tf_op jit(solution)/shard_map/ppermute | solution.py:344
  8.2 0.9 %copy-start = (f32[2,72,128]{2,1,0:T(8,128)S(1)}, f32[2,72,128]{2,1,0:T(8,128)}, u32[]{:S(2)}) copy-start(f32[2,72,128]{2,1,0:T(8,128)} %param.5) | copy-start | bytes 221188
  9.1 0.7 %copy-start.1 = (s32[4,128]{1,0:T(4,128)S(1)}, s32[4,128]{1,0:T(4,128)}, u32[]{:S(2)}) copy-start(s32[4,128]{1,0:T(4,128)} %near_ref.1) | copy-start | bytes 6148
  9.8 0.7 %copy-start.2 = (s32[128,1]{0,1:T(1,128)S(1)}, s32[128,1]{0,1:T(1,128)}, u32[]{:S(2)}) copy-start(s32[128,1]{0,1:T(1,128)} %param.7) | copy-start | bytes 1540
  12.0 16.6 %all-to-all-start = ((f32[32,1,2304]{2,1,0:T(1,128)}), f32[32,1,2304]{2,1,0:T(1,128)S(1)}, u32[]{:S(2)}, u32[]{:S(2)}) async-start(f32[32,1,2304]{2,1,0:T(1,128)} %bitcast.2), calls=%async_computation | async-start | bytes 589824 | tf_op jit(solution)/shard_map/all_to_all | solution.py:367

commit v7 on v6

--- a/solution.py
+++ b/solution.py
@@ -42,9 +42,10 @@
     return (cut(0) + cut(1)) + cut(2)
 
 
-def index_kernel(plan, state_ref, near_ref, owner_ref, same_ref, part_ref, edge_ref, hot_ref, place_ref, *tail_ref):
+def index_kernel(plan, state_ref, near_ref, owner_ref, base_ref, part_ref, edge_ref, share_ref, place_ref):
     cap, slots, total, dense = plan
-    cdev = state_ref.shape[1]
+    _, cdev = state_ref.shape
+    state = state_ref[...]
     index = near_ref[...] - (lax.axis_index(AXES) * cdev - REACH)
     index = jnp.where(index < 0, index + total, index)
     index = jnp.where(index >= total, index - total, index)
@@ -56,55 +57,65 @@
         row = index[k:k + 1, :]
         inner = inner + jnp.where(own == row, 1.0, 0.0)
         outer = outer + jnp.where(edge == row, 1.0, 0.0)
-    edge_ref[...] = outer.astype(BF16)
-    same_ref[...] = state_ref[...]
-    part_ref[...] = select_dot(state_ref[...], inner.astype(BF16), NN)
+    outer = outer.astype(BF16)
+    edge_ref[...] = outer
+    part = 0.15 * (select_dot(state, inner.astype(BF16), NN) - 4.0 * state)
+    part_ref[...] = part
     mine = jnp.broadcast_to(owner_ref[...], (cdev, cdev)).astype(F32)
     lower = lax.broadcasted_iota(jnp.int32, (cdev, cdev), 0) < lax.broadcasted_iota(jnp.int32, (cdev, cdev), 1)
     rank = jnp.sum(jnp.where((mine == mine.T) & lower, 1.0, 0.0), axis=0, keepdims=True).astype(jnp.int32)
     to = owner_ref[...]
     target = to * cap + rank
-    rows = lax.broadcasted_iota(jnp.int32, (slots, cdev), 0)
-    hot_ref[...] = jnp.where(rows == target, 1.0, 0.0).astype(BF16)
+    load = jnp.concatenate([part, state], axis=0)
+
+    def hot(count, place):
+        return jnp.where(lax.broadcasted_iota(jnp.int32, (count, cdev), 0) == place, 1.0, 0.0).astype(BF16)
+
+    def share(chosen):
+        return lax.dot_general(chosen, outer, NT, preferred_element_type=F32).astype(BF16)
+
     if dense is None:
         place_ref[0:1, :] = target
+        chosen = hot(slots, target)
+        base_ref[...] = select_dot(load, chosen, NT, True)
+        share_ref[...] = share(chosen)
         return
-    back = dense[1]
+    tiles, back = dense
     for t in range(back):
         place_ref[t:t + 1, :] = to * (back * cap + 1) + t * cap + rank
     place_ref[back:back + 1, :] = to * (back * cap + 1) + back * cap
     place_ref[back + 1:back + 2, :] = rank
-    rows = lax.broadcasted_iota(jnp.int32, (slots // 4, cdev), 0) * 4
-    for q in range(4):
-        tail_ref[0][:, q * cdev:(q + 1) * cdev] = jnp.where(rows + q == target, 1.0, 0.0).astype(BF16)
-
-
-def pack_kernel(dense, state_ref, part_ref, edge_ref, hot_ref, far_ref, mate_ref, *refs):
-    out_ref, dyn_ref = refs[-2:]
-    rows = state_ref.shape[0]
-    state = state_ref[...]
-    odd = jnp.broadcast_to(lax.axis_index(AXES) % 2, far_ref.shape) == 1
-    before = jnp.where(odd, mate_ref[...], far_ref[...])
-    after = jnp.where(odd, far_ref[...], mate_ref[...])
-    halo = select_dot(before, edge_ref[0:REACH], NN) + select_dot(after, edge_ref[REACH:2 * REACH], NN)
-    dyn = 0.15 * ((part_ref[...] + halo) - 4.0 * state)
-    dyn_ref[...] = dyn
-    if dense is None:
-        out_ref[:, 0:rows] = select_dot(state, hot_ref[...], NT, True)
-        out_ref[:, rows:2 * rows] = select_dot(dyn, hot_ref[...], NT, True)
-        return
-    load = jnp.concatenate([state, dyn], axis=0)
-    tiles, cap = dense[0], 8
     each = tiles * cap + 2
-    main = select_dot(load[:tiles * 128], hot_ref[...], NT, True)
+    for t in range(2):
+        share_ref[:, 2 * REACH * t:2 * REACH * (t + 1)] = share(hot(share_ref.shape[0], to * each + t * cap + rank))
+    main = select_dot(load[:tiles * 128], hot(slots, target), NT, True)
     tail = load[tiles * 128:]
     blank = jnp.zeros_like(tail)
     tail = [jnp.concatenate([tail if i == q else blank for i in range(4)], axis=0) for q in range(4)]
-    tail = select_dot(jnp.concatenate(tail, axis=1), refs[0][...], NT, True)
-    for s in range(hot_ref.shape[0] // cap):
+    chosen = [hot(slots // 4, jnp.where(rank % 4 == q, target // 4, -1)) for q in range(4)]
+    tail = select_dot(jnp.concatenate(tail, axis=1), jnp.concatenate(chosen, axis=1), NT, True)
+    for s in range(slots // cap):
         for t in range(tiles):
-            out_ref[s * each + t * cap:s * each + (t + 1) * cap, :] = main[s * cap:(s + 1) * cap, t * 128:(t + 1) * 128]
-        out_ref[s * each + tiles * cap:(s + 1) * each, :] = tail[2 * s:2 * s + 2]
+            base_ref[s * each + t * cap:s * each + (t + 1) * cap, :] = main[s * cap:(s + 1) * cap, t * 128:(t + 1) * 128]
+        base_ref[s * each + tiles * cap:(s + 1) * each, :] = tail[2 * s:2 * s + 2]
+
+
+def pack_kernel(dense, base_ref, part_ref, edge_ref, share_ref, far_ref, mate_ref, out_ref, dyn_ref, halo_ref):
+    rows = part_ref.shape[0]
+    odd = jnp.broadcast_to(lax.axis_index(AXES) % 2, far_ref.shape) == 1
+    before = 0.15 * jnp.where(odd, mate_ref[...], far_ref[...])
+    after = 0.15 * jnp.where(odd, far_ref[...], mate_ref[...])
+    if dense is None:
+        halo_ref[:, :REACH], halo_ref[:, REACH:] = before, after
+        out_ref[:, :rows] = base_ref[:, :rows] + select_dot(halo_ref[...], share_ref[...], NT, True)
+        out_ref[:, rows:] = base_ref[:, rows:]
+    else:
+        halo_ref[:, 2 * REACH:] = jnp.zeros((128, 2 * REACH), F32)
+        for i, side in enumerate((before, after)):
+            halo_ref[:, i * REACH:(i + 1) * REACH] = side[:128]
+            halo_ref[0:rows - 128, (2 + i) * REACH:(3 + i) * REACH] = side[128:]
+        out_ref[...] = base_ref[...] + select_dot(halo_ref[...], share_ref[...], NT, True)
+    dyn_ref[...] = part_ref[...] + (select_dot(before, edge_ref[:REACH], NN) + select_dot(after, edge_ref[REACH:], NN))
 
 
 def near_matrix(rows, columns, crmx, centre, side):
@@ -132,9 +143,10 @@
 
     @pl.when(pl.program_id(0) == 0)
     def _():
-        yt_ref, ym_ref, head_rate_ref = head_refs
+        yt_ref, ym_ref, head_rate_ref, first_ref = head_refs
         size = yt_ref.shape[0]
         first = near_matrix(per, per, crmx, 3.0, 1.0).astype(BF16)
+        first_ref[...] = first
         for q in range(size // per):
             part = slice(q * per, (q + 1) * per)
             yt_ref[part, :] = diffusion(first, ct_ref[:, part])
@@ -169,10 +181,10 @@
 
 
 def physics_kernel(levels, crmx, dense, arrived_ref, *refs):
-    head, (crm_hbm, rate_hbm, both_hbm, out_ref), refs = refs[:3], refs[3:7], refs[7:]
-    rows_ref, sums_ref, first_ref, crm_sems, rate_sems = refs[:5]
-    head = (*head, refs[17])
-    fields, coefs, crm_bufs = (refs[5:7], refs[7:9]), (refs[9:11], refs[11:13]), (refs[13:15], refs[15:17])
+    head, (first_ref, crm_hbm, rate_hbm, both_hbm, out_ref), refs = refs[:3], refs[3:8], refs[8:]
+    rows_ref, sums_ref, crm_sems, rate_sems = refs[:4]
+    head = (*head, refs[4])
+    fields, coefs, crm_bufs = (refs[5:7], refs[7:9]), refs[9:11], refs[11:13]
     slots = crm_hbm.shape[0]
     halves = slots // 128
     steps = crmx // 8
@@ -182,15 +194,15 @@
     count = levels // here
     shift = [math.log(0.8 * 5.0 ** j) / 0.3 for j in range(SUB + 1)]
 
-    def crm_copies(group, k):
+    def crm_copies(group):
         width = levels * crmx
         at = [pl.ds(pl.multiple_of(i * width + group * size, 128), size) for i in range(2)]
-        return [pltpu.make_async_copy(crm_hbm.at[:, at[i]], crm_bufs[k][i], crm_sems.at[k, i]) for i in range(2)]
-
-    def rate_copies(group, k):
+        return [pltpu.make_async_copy(crm_hbm.at[:, at[i]], crm_bufs[i].at[group - 1], crm_sems.at[group - 1, i]) for i in range(2)]
+
+    def rate_copies(group):
         at = pl.ds(pl.multiple_of(group * size, 8), size)
         return [
-            pltpu.make_async_copy(ref.at[at, :], coefs[k][i], rate_sems.at[k, i])
+            pltpu.make_async_copy(ref.at[at, :], coefs[i].at[group - 1], rate_sems.at[group - 1, i])
             for i, ref in enumerate((rate_hbm, both_hbm))
         ]
 
@@ -202,18 +214,17 @@
         for copy in copies:
             copy.wait()
 
-    def diffuse(k):
-        for ref, source in zip(fields[k], crm_bufs[k]):
+    def diffuse(group, k):
+        for ref, source in zip(fields[k], crm_bufs):
             for q in range(size // part):
                 cut = slice(q * part, (q + 1) * part)
-                ref[cut, :] = diffusion(first_ref[...], source[:, cut])
-
-    for group in (1, 2):
-        start(crm_copies(group, (group - 1) % 2))
-        start(rate_copies(group, (group - 1) % 2))
-    first_ref[...] = near_matrix(part, part, crmx, 3.0, 1.0).astype(BF16)
+                ref[cut, :] = diffusion(first_ref[...], source[group - 1, :, cut])
+
+    for group in range(1, count):
+        start(crm_copies(group))
+        start(rate_copies(group))
     arrived = arrivals(dense, arrived_ref, slots, 4 * levels)
-    temp, moist, push, wet = [arrived[i * levels:(i + 1) * levels] for i in range(4)]
+    push, wet, temp, moist = [arrived[i * levels:(i + 1) * levels] for i in range(4)]
     push, wet = push * (1.0 / SUB), wet * (1.0 / SUB)
     tables = [5.0 * (temp + push + shift[1]), 5.0 * (moist + wet)]
     for j in range(2, SUB + 1):
@@ -253,31 +264,24 @@
                 unit(group, inner, half, sources)
 
     head[3][...] = 0.7 - 0.775 * (0.7 - head[2][...])
-    wait(crm_copies(1, 0))
-    diffuse(0)
+    wait(crm_copies(1))
+    diffuse(1, 0)
     run(0, head)
 
     @pl.loop(0, (count - 1) // 2)
     def _(trip):
         for k in range(2):
             group = 1 + 2 * trip + k
-
-            @pl.when(group + 2 < count)
-            def _():
-                start(crm_copies(group + 2, k))
-
-            wait(rate_copies(group, k))
-
-            @pl.when(group + 1 < count)
-            def _():
-                wait(crm_copies(group + 1, 1 - k))
-
-            diffuse(1 - k)
-            run(group, fields[k] + coefs[k])
-
-            @pl.when(group + 2 < count)
-            def _():
-                start(rate_copies(group + 2, k))
+            ahead = jnp.minimum(group + 1, count - 1)
+            wait(rate_copies(group))
+            if k == 0:
+                wait(crm_copies(ahead))
+            else:
+                @pl.when(group + 1 < count)
+                def _():
+                    wait(crm_copies(group + 1))
+            diffuse(ahead, 1 - k)
+            run(group, (*fields[k], coefs[0].at[group - 1], coefs[1].at[group - 1]))
 
     total = 2 * levels
     for half in range(halves):
@@ -344,26 +348,31 @@
     from_far = lax.ppermute(to_far, AXES, far)
     from_mate = lax.ppermute(to_mate, AXES, mate)
 
-    index_out = [sds((rows, cdev), F32)] * 2 + [sds((2 * REACH, cdev), BF16), sds((slots, cdev), BF16)]
-    index_out.append(sds((1 if dense is None else dense[1] + 2, cdev), jnp.int32))
-    if dense is not None:
-        index_out.append(sds((slots // 4, 4 * cdev), BF16))
-    same, part, edge, hot, place, *tail = pl.pallas_call(
+    base_shape = (slots, 2 * rows) if dense is None else (ndev * out_each, 128)
+    wide_halo = 1 if dense is None else 2
+    base, part, edge, share, place = pl.pallas_call(
         functools.partial(index_kernel, (cap, slots, cdev * ndev, dense)),
         in_specs=[VMEM] * 3,
-        out_specs=[VMEM] * len(index_out),
-        out_shape=index_out,
+        out_specs=[VMEM] * 5,
+        out_shape=[
+            sds(base_shape, F32),
+            sds((rows, cdev), F32),
+            sds((2 * REACH, cdev), BF16),
+            sds((base_shape[0], 2 * REACH * wide_halo), BF16),
+            sds((1 if dense is None else dense[1] + 2, cdev), jnp.int32),
+        ],
         compiler_params=pltpu.CompilerParams(vmem_limit_bytes=12 << 20),
         name="index",
     )(flat, neighbors, owner.reshape(1, cdev))
     outgoing, dyn = pl.pallas_call(
         functools.partial(pack_kernel, dense),
-        in_specs=[VMEM] * (6 + len(tail)),
+        in_specs=[VMEM] * 6,
         out_specs=[VMEM] * 2,
-        out_shape=[sds((slots, 2 * rows) if dense is None else (ndev * out_each, 128), F32), sds((rows, cdev), F32)],
+        out_shape=[sds(base_shape, F32), sds((rows, cdev), F32)],
+        scratch_shapes=[pltpu.VMEM((rows if dense is None else 128, 2 * REACH * wide_halo), F32)],
         compiler_params=pltpu.CompilerParams(vmem_limit_bytes=12 << 20),
         name="pack",
-    )(same, part, edge, hot, from_far, from_mate, *tail)
+    )(base, part, edge, share, from_far, from_mate)
     arrived = lax.all_to_all(outgoing.reshape(ndev, cap * 2 * rows), AXES, split_axis=0, concat_axis=0, tiled=True)
     arrived = arrived.reshape(outgoing.shape)
 
@@ -374,12 +383,12 @@
     size = HEAD * crmx
     field, coef = sds((levels * crmx, slots), F32), sds((size, slots), F32)
     offset = levels // HEAD
-    *rates, yt, ym, head_rate = pl.pallas_call(
+    *rates, yt, ym, head_rate, first_matrix = pl.pallas_call(
         functools.partial(prepare_kernel, crmx),
         grid=(count,),
         in_specs=[take(0)] + [pl.BlockSpec((slots, size), lambda g, i=i: (0, i * offset)) for i in range(2)],
-        out_specs=rates_spec + [VMEM] * 3,
-        out_shape=[field] * 2 + [coef] * 3,
+        out_specs=rates_spec + [VMEM] * 4,
+        out_shape=[field] * 2 + [coef] * 3 + [sds((GROUP * crmx, GROUP * crmx), BF16)],
         compiler_params=pltpu.CompilerParams(vmem_limit_bytes=53000 << 10),
         cost_estimate=pl.CostEstimate(flops=2 * slots * levels * crmx * GROUP * crmx, transcendentals=0, bytes_accessed=6 * slots * wide),
         name="prepare",
@@ -387,22 +396,21 @@
 
     back = pl.pallas_call(
         functools.partial(physics_kernel, levels, crmx, dense),
-        in_specs=[VMEM] * 4 + [pl.BlockSpec(memory_space=pl.ANY)] * 3,
+        in_specs=[VMEM] * 5 + [pl.BlockSpec(memory_space=pl.ANY)] * 3,
         out_specs=VMEM,
         out_shape=sds((slots, rows) if dense is None else (ndev * back_each, 128), F32),
         scratch_shapes=[
             pltpu.VMEM((slots // 128, 2 * SUB * levels + 8, 128), F32),
             pltpu.VMEM((slots // 128, 8 * rows, 128), F32),
-            pltpu.VMEM((GROUP * crmx, GROUP * crmx), BF16),
-            pltpu.SemaphoreType.DMA((2, 2)),
-            pltpu.SemaphoreType.DMA((2, 2)),
+            pltpu.SemaphoreType.DMA((offset - 1, 2)),
+            pltpu.SemaphoreType.DMA((offset - 1, 2)),
         ]
-        + [pltpu.VMEM((size, slots), F32)] * 8
-        + [pltpu.VMEM((slots, size), BF16)] * 4
-        + [pltpu.VMEM((size, slots), F32)],
+        + [pltpu.VMEM((size, slots), F32)] * 5
+        + [pltpu.VMEM((offset - 1, size, slots), F32)] * 2
+        + [pltpu.VMEM((offset - 1, slots, size), BF16)] * 2,
         compiler_params=pltpu.CompilerParams(vmem_limit_bytes=53000 << 10),
         name="physics",
-    )(arrived, yt, ym, head_rate, crm_state, *rates)
+    )(arrived, yt, ym, head_rate, first_matrix, crm_state, *rates)
     returned = lax.all_to_all(back.reshape(ndev, cap * rows), AXES, split_axis=0, concat_axis=0, tiled=True)
     out = pl.pallas_call(
         functools.partial(finish_kernel, dense),

time: 54.2 us -> 52.6 us (0.970)
  Pallas kernels: 24 us -> 22.8 us
    pallas_call x1, Pallas kernels: 13.1 us -> 11.9 us  [local(): pl.pallas_call(functools.partial(physics_kernel, levels, crmx, dense), in...]
  transfers between devices with their start and end apart: 3 -> 3, of which waited for: 1 -> 1; matrix products, arithmetic and copies ran while one was open for 0% -> 0% of each run, Pallas kernels for 16% -> 17%
where the time goes in v7:
time: 52.6 us; the launch traced here: 52.2 us
  Pallas kernels  22.8 us (43%)
  starting transfers between devices  12 us (23%)
  blocking collectives  11 us (21%)
  waiting for transfers between devices  3.01 us (6%)
  local copies, waits for them, and re-layouts  2.22 us (4%)
  other arithmetic  1.04 us (2%)
    pallas_call x1, Pallas kernels, local(): pl.pallas_call(functools.partial(physics_kernel, levels, crmx, dense), in...  11.9 us
    all_to_all x1, blocking collectives, local(): lax.all_to_all(back.reshape(ndev, cap * rows), AXES, split_axis=0, concat...  11 us
    pallas_call x1, Pallas kernels, local(): pl.pallas_call(functools.partial(prepare_kernel, crmx), grid=(count,), in...  8.31 us
    ppermute x1, starting transfers between devices, local(): from_far = lax.ppermute(to_far, AXES, far)  6.58 us
    all_to_all x1, starting transfers between devices, local(): lax.all_to_all(outgoing.reshape(ndev, cap * 2 * rows), AXES, split_axis=0...  4.86 us
    all_to_all x1, waiting for transfers between devices, local(): lax.all_to_all(outgoing.reshape(ndev, cap * 2 * rows), AXES, split_axis=0...  3.01 us
    unnamed x6, local copies, waits for them, and re-layouts  2.22 us
    pallas_call x1, Pallas kernels, local(): pl.pallas_call(functools.partial(pack_kernel, dense), in_specs=[VMEM] * 6...  1.11 us
  transfers between devices with their start and end apart: 3, of which 1 were waited for; matrix products, arithmetic and copies ran while one was open for 0% of the time, Pallas kernels for 17%

profile of v7, /device:TPU:0, one launch (start us, length us, event | category | flops | bytes accessed | tf_op | source)
XLA Modules:
  0.0 52.2 jit_solution(2451782918648086795)
XLA Ops:
  0.0 1.0 %slice_select_fusion = (f32[144,8]{1,0:T(8,128)S(1)}, f32[144,8]{1,0:T(8,128)S(1)}) fusion(f32[144,128]{1,0:T(8,128)} %bitcast.8, pred[]{:T(512)S(6)} %eq.6), kind=kLoop, calls=%fused_computation | loop fusion | flops 2304 | bytes 18433 | tf_op jit(solution)/shard_map/jit(_where)/select_n | solution.py:347
  1.1 0.6 %collective-permute-start.1 = (f32[144,8]{1,0:T(8,128)S(1)}, f32[144,8]{1,0:T(8,128)S(1)}, u32[]{:S(2)}, u32[]{:S(2)}) collective-permute-start(f32[144,8]{1,0:T(8,128)S(1)} %get-tuple-element.31), channel_id=1, source_target_pairs={{0,1},{1,0},{2,3},{3,2},{4,5},{5,4},{6,7},{7,6},{8,9},{9,8},{10,11... | collective-permute-start | bytes 13832 | tf_op jit(solution)/shard_map/ppermute | solution.py:349
  1.6 6.6 %collective-permute-start = (f32[144,8]{1,0:T(8,128)S(1)}, f32[144,8]{1,0:T(8,128)S(1)}, u32[]{:S(2)}, u32[]{:S(2)}) collective-permute-start(f32[144,8]{1,0:T(8,128)S(1)} %get-tuple-element.32), channel_id=1, source_target_pairs={{0,31},{1,2},{2,1},{3,4},{4,3},{5,6},{6,5},{7,8},{8,7},{9,10},{10,... | collective-permute-start | bytes 13832 | tf_op jit(solution)/shard_map/ppermute | solution.py:348
  8.2 0.0 copy-start
  8.2 0.9 %copy-done = f32[2,72,128]{2,1,0:T(8,128)S(1)} copy-done((f32[2,72,128]{2,1,0:T(8,128)S(1)}, f32[2,72,128]{2,1,0:T(8,128)}, u32[]{:S(2)}) %copy-start) | copy-done | bytes 73752
  9.1 0.0 copy-start.1
  9.1 0.7 %copy-done.1 = s32[4,128]{1,0:T(4,128)S(1)} copy-done((s32[4,128]{1,0:T(4,128)S(1)}, s32[4,128]{1,0:T(4,128)}, u32[]{:S(2)}) %copy-start.1) | copy-done | bytes 2072
  9.8 0.0 copy-start.2
  9.8 0.7 %copy-done.2 = s32[128,1]{0,1:T(1,128)S(1)} copy-done((s32[128,1]{0,1:T(1,128)S(1)}, s32[128,1]{0,1:T(1,128)}, u32[]{:S(2)}) %copy-start.2) | copy-done | bytes 536
  10.4 0.6 %index.1 = (f32[576,128]{1,0:T(8,128)S(1)}, f32[144,128]{1,0:T(8,128)S(1)}, bf16[16,128]{1,0:T(8,128)(2,1)S(1)}, bf16[576,32]{1,0:T(8,128)(2,1)S(1)}, s32[3,128]{1,0:T(4,128)S(1)}) custom-call(f32[144,128]{1,0:T(8,128)S(1)} %bitcast.9, s32[4,128]{1,0:T(4,128)S(1)} %copy-done.1, s32[1,128]{1,0:T(1,128)S(1)} %bitcast.12), custom_call_target="tpu_custom_call" | custom-call | tf_op jit(solution)/shard_map/index/pallas_call | solution.py:353
  11.0 0.0 collective-permute-done.1.mate_ref
  11.1 0.0 collective-permute-done.far_ref
  11.1 1.1 %pack.1 = (f32[576,128]{1,0:T(8,128)}, f32[144,128]{1,0:T(8,128)S(1)}) custom-call(f32[576,128]{1,0:T(8,128)S(1)} %get-tuple-element.18.base_ref, f32[144,128]{1,0:T(8,128)S(1)} %get-tuple-element.19.part_ref, bf16[16,128]{1,0:T(8,128)(2,1)S(1)} %get-tuple-element.20.edge_ref, bf16[576,32]{1,0:T(8,128)(2,1)S(1)} %get-tuple-element.21.share_ref, ...), custom_call_target="tpu_custom_call" | custom-call | tf_op jit(solution)/shard_map/pack/pallas_call | solution.py:367
  12.2 4.9 %all-to-all-start = ((f32[32,1,2304]{2,1,0:T(1,128)}), f32[32,1,2304]{2,1,0:T(1,128)S(1)}, u32[]{:S(2)}, u32[]{:S(2)}) async-start(f32[32,1,2304]{2,1,0:T(1,128)} %bitcast.2), calls=%async_computation | async-start | bytes 589824 | tf_op jit(solution)/shard_map/all_to_all | solution.py:376
  17.0 8.3 %prepare.1 = (f32[4608,256]{1,0:T(8,128)}, f32[4608,256]{1,0:T(8,128)}, f32[512,256]{1,0:T(8,128)S(1)}, f32[512,256]{1,0:T(8,128)S(1)}, f32[512,256]{1,0:T(8,128)S(1)}, /*index=5*/bf16[256,256]{1,0:T(8,128)(2,1)S(1)}) custom-call(s32[256,4608]{1,0:T(8,128)} %mask_ref.1, bf16[256,9216]{1,0:T(8,128)(2,1)} %refs_4_.1, bf16[256,9216]{1,0:T(8,128)(2,1)} %refs_4_.1), custom_call_target="tpu_custom_call" | custom-call | flops 603979776 | bytes 14155776 | tf_op jit(solution)/shard_map/prepare/pallas_call | solution.py:386
  25.3 3.0 %all-to-all-done = f32[32,1,2304]{2,1,0:T(1,128)S(1)} async-done(((f32[32,1,2304]{2,1,0:T(1,128)}), f32[32,1,2304]{2,1,0:T(1,128)S(1)}, u32[]{:S(2)}, u32[]{:S(2)}) %all-to-all-start) | async-done | bytes 294944 | tf_op jit(solution)/shard_map/all_to_all | solution.py:376
  28.4 11.9 %physics.1 = f32[288,128]{1,0:T(8,128)S(1)} custom-call(f32[576,128]{1,0:T(8,128)S(1)} %bitcast.7, f32[512,256]{1,0:T(8,128)S(1)} %get-tuple-element.25.refs_0_, f32[512,256]{1,0:T(8,128)S(1)} %get-tuple-element.26.refs_1_, f32[512,256]{1,0:T(8,128)S(1)} %get-tuple-element.27.refs_2_, bf16[256,256]{1,0:T(8,128)(2,1)S(1)} %get-tuple-element.28.refs_3_, ...), custom_call_target="tpu_custom_call" | custom-call | tf_op jit(solution)/shard_map/physics/pallas_call | solution.py:397
  40.2 11.0 %all_to_all.18 = f32[32,1,1152]{2,1,0:T(1,128)S(1)} all-to-all(f32[32,1,1152]{2,1,0:T(1,128)S(1)} %bitcast.10), channel_id=1, replica_groups=mesh['sec'=4,'blk'=8] {'sec','blk'}, dimensions={0} | all-to-all | bytes 294912 | tf_op jit(solution)/shard_map/all_to_all | solution.py:414
  51.2 0.9 %finish.1 = f32[144,128]{1,0:T(8,128)} custom-call(f32[144,128]{1,0:T(8,128)S(1)} %get-tuple-element.22.dyn_ref, s32[3,128]{1,0:T(4,128)S(1)} %get-tuple-element.23.place_ref, f32[288,128]{1,0:T(8,128)S(1)} %bitcast.11), custom_call_target="tpu_custom_call" | custom-call | tf_op jit(solution)/shard_map/finish/pallas_call | solution.py:415
Async XLA Ops:
  1.1 10.0 %collective-permute-start.1 = (f32[144,8]{1,0:T(8,128)S(1)}, f32[144,8]{1,0:T(8,128)S(1)}, u32[]{:S(2)}, u32[]{:S(2)}) collective-permute-start(f32[144,8]{1,0:T(8,128)S(1)} %get-tuple-element.31), channel_id=1, source_target_pairs={{0,1},{1,0},{2,3},{3,2},{4,5},{5,4},{6,7},{7,6},{8,9},{9,8},{10,11... | collective-permute-start | bytes 13832 | tf_op jit(solution)/shard_map/ppermute | solution.py:349
  1.6 9.4 %collective-permute-start = (f32[144,8]{1,0:T(8,128)S(1)}, f32[144,8]{1,0:T(8,128)S(1)}, u32[]{:S(2)}, u32[]{:S(2)}) collective-permute-start(f32[144,8]{1,0:T(8,128)S(1)} %get-tuple-element.32), channel_id=1, source_target_pairs={{0,31},{1,2},{2,1},{3,4},{4,3},{5,6},{6,5},{7,8},{8,7},{9,10},{10,... | collective-permute-start | bytes 13832 | tf_op jit(solution)/shard_map/ppermute | solution.py:348
  8.2 0.9 %copy-start = (f32[2,72,128]{2,1,0:T(8,128)S(1)}, f32[2,72,128]{2,1,0:T(8,128)}, u32[]{:S(2)}) copy-start(f32[2,72,128]{2,1,0:T(8,128)} %param.5) | copy-start | bytes 221188
  9.1 0.7 %copy-start.1 = (s32[4,128]{1,0:T(4,128)S(1)}, s32[4,128]{1,0:T(4,128)}, u32[]{:S(2)}) copy-start(s32[4,128]{1,0:T(4,128)} %near_ref.1) | copy-start | bytes 6148
  9.8 0.7 %copy-start.2 = (s32[128,1]{0,1:T(1,128)S(1)}, s32[128,1]{0,1:T(1,128)}, u32[]{:S(2)}) copy-start(s32[128,1]{0,1:T(1,128)} %param.7) | copy-start | bytes 1540
  12.2 16.2 %all-to-all-start = ((f32[32,1,2304]{2,1,0:T(1,128)}), f32[32,1,2304]{2,1,0:T(1,128)S(1)}, u32[]{:S(2)}, u32[]{:S(2)}) async-start(f32[32,1,2304]{2,1,0:T(1,128)} %bitcast.2), calls=%async_computation | async-start | bytes 589824 | tf_op jit(solution)/shard_map/all_to_all | solution.py:376

commit v8 on v7

--- a/solution.py
+++ b/solution.py
@@ -40,6 +40,17 @@
     out = lax.dot_general(*pair, dims, preferred_element_type=F32)
     cut = (lambda i: out[:, i * size:(i + 1) * size]) if flip else (lambda i: out[i * size:(i + 1) * size])
     return (cut(0) + cut(1)) + cut(2)
+
+
+def edges_kernel(state_ref, far_ref, mate_ref, same_ref):
+    rows, cdev = state_ref.shape
+    state = state_ref[...]
+    same_ref[...] = state
+    turned = jnp.concatenate([state, jnp.zeros((256 - rows, cdev), F32)], axis=0).T[:, :rows]
+    first, last = turned[:REACH], turned[cdev - REACH:]
+    odd = jnp.broadcast_to(lax.axis_index(AXES) % 2, first.shape) == 1
+    far_ref[...] = jnp.where(odd, last, first)
+    mate_ref[...] = jnp.where(odd, first, last)
 
 
 def index_kernel(plan, state_ref, near_ref, owner_ref, base_ref, part_ref, edge_ref, share_ref, place_ref):
@@ -105,17 +116,18 @@
     odd = jnp.broadcast_to(lax.axis_index(AXES) % 2, far_ref.shape) == 1
     before = 0.15 * jnp.where(odd, mate_ref[...], far_ref[...])
     after = 0.15 * jnp.where(odd, far_ref[...], mate_ref[...])
+    for i, side in enumerate((before, after)):
+        halo_ref[i * REACH:(i + 1) * REACH, :] = side if dense is None else side[:, :128]
+        if dense is not None:
+            pad = jnp.zeros((REACH, 256 - rows), F32)
+            halo_ref[(2 + i) * REACH:(3 + i) * REACH, :] = jnp.concatenate([side[:, 128:], pad], axis=1)
+    moved = select_dot(halo_ref[...], share_ref[...], NN, True)
     if dense is None:
-        halo_ref[:, :REACH], halo_ref[:, REACH:] = before, after
-        out_ref[:, :rows] = base_ref[:, :rows] + select_dot(halo_ref[...], share_ref[...], NT, True)
+        out_ref[:, :rows] = base_ref[:, :rows] + moved
         out_ref[:, rows:] = base_ref[:, rows:]
     else:
-        halo_ref[:, 2 * REACH:] = jnp.zeros((128, 2 * REACH), F32)
-        for i, side in enumerate((before, after)):
-            halo_ref[:, i * REACH:(i + 1) * REACH] = side[:128]
-            halo_ref[0:rows - 128, (2 + i) * REACH:(3 + i) * REACH] = side[128:]
-        out_ref[...] = base_ref[...] + select_dot(halo_ref[...], share_ref[...], NT, True)
-    dyn_ref[...] = part_ref[...] + (select_dot(before, edge_ref[:REACH], NN) + select_dot(after, edge_ref[REACH:], NN))
+        out_ref[...] = base_ref[...] + moved
+    dyn_ref[...] = part_ref[...] + (select_dot(before, edge_ref[:REACH], TN) + select_dot(after, edge_ref[REACH:], TN))
 
 
 def near_matrix(rows, columns, crmx, centre, side):
@@ -330,7 +342,6 @@
 
 def local(state, neighbors, owner, crm_state, phase_mask):
     ndev = lax.axis_size(AXES)
-    me = lax.axis_index(AXES)
     fields, levels, cdev = state.shape
     rows = fields * levels
     slots, wide = crm_state.shape
@@ -342,9 +353,14 @@
     out_each, back_each = 2 * rows * cap // 128, rows * cap // 128
     far = [(i, (i + 1) % ndev if i % 2 else (i - 1) % ndev) for i in range(ndev)]
     mate = [(i, i ^ 1) for i in range(ndev)]
-    odd = me % 2
-    first, last = flat[:, :REACH], flat[:, cdev - REACH:]
-    to_far, to_mate = jnp.where(odd == 1, last, first), jnp.where(odd == 1, first, last)
+    to_far, to_mate, same = pl.pallas_call(
+        edges_kernel,
+        in_specs=[VMEM],
+        out_specs=[VMEM] * 3,
+        out_shape=[sds((REACH, rows), F32)] * 2 + [sds((rows, cdev), F32)],
+        compiler_params=pltpu.CompilerParams(vmem_limit_bytes=8 << 20),
+        name="edges",
+    )(flat)
     from_far = lax.ppermute(to_far, AXES, far)
     from_mate = lax.ppermute(to_mate, AXES, mate)
 
@@ -363,13 +379,13 @@
         ],
         compiler_params=pltpu.CompilerParams(vmem_limit_bytes=12 << 20),
         name="index",
-    )(flat, neighbors, owner.reshape(1, cdev))
+    )(same, neighbors, owner.reshape(1, cdev))
     outgoing, dyn = pl.pallas_call(
         functools.partial(pack_kernel, dense),
         in_specs=[VMEM] * 6,
         out_specs=[VMEM] * 2,
         out_shape=[sds(base_shape, F32), sds((rows, cdev), F32)],
-        scratch_shapes=[pltpu.VMEM((rows if dense is None else 128, 2 * REACH * wide_halo), F32)],
+        scratch_shapes=[pltpu.VMEM((2 * REACH * wide_halo, rows if dense is None else 128), F32)],
         compiler_params=pltpu.CompilerParams(vmem_limit_bytes=12 << 20),
         name="pack",
     )(base, part, edge, share, from_far, from_mate)

time: 52.6 us -> 51 us (0.970)
  other arithmetic: 1.04 us -> 0 us
    select_n x1 -> x0, other arithmetic: 1.04 us -> none  [local(): jnp.where(odd == 1, first, last)]
    ppermute x1, starting transfers between devices: 0.56 us -> 0.01 us  [local(): from_mate = lax.ppermute(to_mate, AXES, mate)]
  transfers between devices with their start and end apart: 3 -> 3, of which waited for: 1 -> 1; matrix products, arithmetic and copies ran while one was open for 0% -> 0% of each run, Pallas kernels for 17% -> 18%
where the time goes in v8:
time: 51 us; the launch traced here: 50.6 us
  Pallas kernels  22.8 us (45%)
  starting transfers between devices  11.5 us (23%)
  blocking collectives  11 us (22%)
  waiting for transfers between devices  3.01 us (6%)
  local copies, waits for them, and re-layouts  2.22 us (4%)
    pallas_call x1, Pallas kernels, local(): pl.pallas_call(functools.partial(physics_kernel, levels, crmx, dense), in...  11.9 us
    all_to_all x1, blocking collectives, local(): lax.all_to_all(back.reshape(ndev, cap * rows), AXES, split_axis=0, concat...  11 us
    pallas_call x1, Pallas kernels, local(): pl.pallas_call(functools.partial(prepare_kernel, crmx), grid=(count,), in...  8.31 us
    ppermute x1, starting transfers between devices, local(): from_far = lax.ppermute(to_far, AXES, far)  6.47 us
    all_to_all x1, starting transfers between devices, local(): lax.all_to_all(outgoing.reshape(ndev, cap * 2 * rows), AXES, split_axis=0...  5.04 us
    all_to_all x1, waiting for transfers between devices, local(): lax.all_to_all(outgoing.reshape(ndev, cap * 2 * rows), AXES, split_axis=0...  3.01 us
    unnamed x6, local copies, waits for them, and re-layouts  2.22 us
  transfers between devices with their start and end apart: 3, of which 1 were waited for; matrix products, arithmetic and copies ran while one was open for 0% of the time, Pallas kernels for 18%

profile of v8, /device:TPU:0, one launch (start us, length us, event | category | flops | bytes accessed | tf_op | source)
XLA Modules:
  0.0 50.6 jit_solution(3912938551499357326)
XLA Ops:
  0.0 0.0 copy-start
  0.0 0.9 %copy-done = f32[2,72,128]{2,1,0:T(8,128)S(1)} copy-done((f32[2,72,128]{2,1,0:T(8,128)S(1)}, f32[2,72,128]{2,1,0:T(8,128)}, u32[]{:S(2)}) %copy-start) | copy-done | bytes 73752
  0.9 0.1 edges.1
  1.0 6.5 %collective-permute-start = (f32[8,144]{1,0:T(8,128)S(1)}, f32[8,144]{1,0:T(8,128)S(1)}, u32[]{:S(2)}, u32[]{:S(2)}) collective-permute-start(f32[8,144]{1,0:T(8,128)S(1)} %get-tuple-element.26), channel_id=1, source_target_pairs={{0,31},{1,2},{2,1},{3,4},{4,3},{5,6},{6,5},{7,8},{8,7},{9,10},{10,... | collective-permute-start | bytes 13832 | tf_op jit(solution)/shard_map/ppermute | solution.py:364
  7.4 0.0 collective-permute-start.1
  7.5 0.0 copy-start.1
  7.5 0.7 %copy-done.1 = s32[4,128]{1,0:T(4,128)S(1)} copy-done((s32[4,128]{1,0:T(4,128)S(1)}, s32[4,128]{1,0:T(4,128)}, u32[]{:S(2)}) %copy-start.1) | copy-done | bytes 2072
  8.1 0.0 copy-start.2
  8.1 0.7 %copy-done.2 = s32[128,1]{0,1:T(1,128)S(1)} copy-done((s32[128,1]{0,1:T(1,128)S(1)}, s32[128,1]{0,1:T(1,128)}, u32[]{:S(2)}) %copy-start.2) | copy-done | bytes 536
  8.8 0.6 %index.1 = (f32[576,128]{1,0:T(8,128)S(1)}, f32[144,128]{1,0:T(8,128)S(1)}, bf16[16,128]{1,0:T(8,128)(2,1)S(1)}, bf16[576,32]{1,0:T(8,128)(2,1)S(1)}, s32[3,128]{1,0:T(4,128)S(1)}) custom-call(f32[144,128]{1,0:T(8,128)S(1)} %get-tuple-element.21.state_ref, s32[4,128]{1,0:T(4,128)S(1)} %copy-done.1, s32[1,128]{1,0:T(1,128)S(1)} %bitcast.11), custom_call_target="tpu_custom_call" | custom-call | tf_op jit(solution)/shard_map/index/pallas_call | solution.py:369
  9.4 0.0 collective-permute-done.far_ref
  9.4 0.0 collective-permute-done.1.mate_ref
  9.4 1.0 %pack.1 = (f32[576,128]{1,0:T(8,128)}, f32[144,128]{1,0:T(8,128)S(1)}) custom-call(f32[576,128]{1,0:T(8,128)S(1)} %get-tuple-element.22.base_ref, f32[144,128]{1,0:T(8,128)S(1)} %get-tuple-element.23.part_ref, bf16[16,128]{1,0:T(8,128)(2,1)S(1)} %get-tuple-element.24.edge_ref, bf16[576,32]{1,0:T(8,128)(2,1)S(1)} %get-tuple-element.25.share_ref, ...), custom_call_target="tpu_custom_call" | custom-call | tf_op jit(solution)/shard_map/pack/pallas_call | solution.py:383
  10.4 5.0 %all-to-all-start = ((f32[32,1,2304]{2,1,0:T(1,128)}), f32[32,1,2304]{2,1,0:T(1,128)S(1)}, u32[]{:S(2)}, u32[]{:S(2)}) async-start(f32[32,1,2304]{2,1,0:T(1,128)} %bitcast.2), calls=%async_computation | async-start | bytes 589824 | tf_op jit(solution)/shard_map/all_to_all | solution.py:392
  15.5 8.3 %prepare.1 = (f32[4608,256]{1,0:T(8,128)}, f32[4608,256]{1,0:T(8,128)}, f32[512,256]{1,0:T(8,128)S(1)}, f32[512,256]{1,0:T(8,128)S(1)}, f32[512,256]{1,0:T(8,128)S(1)}, /*index=5*/bf16[256,256]{1,0:T(8,128)(2,1)S(1)}) custom-call(s32[256,4608]{1,0:T(8,128)} %mask_ref.1, bf16[256,9216]{1,0:T(8,128)(2,1)} %refs_4_.1, bf16[256,9216]{1,0:T(8,128)(2,1)} %refs_4_.1), custom_call_target="tpu_custom_call" | custom-call | flops 603979776 | bytes 14155776 | tf_op jit(solution)/shard_map/prepare/pallas_call | solution.py:402
  23.8 3.0 %all-to-all-done = f32[32,1,2304]{2,1,0:T(1,128)S(1)} async-done(((f32[32,1,2304]{2,1,0:T(1,128)}), f32[32,1,2304]{2,1,0:T(1,128)S(1)}, u32[]{:S(2)}, u32[]{:S(2)}) %all-to-all-start) | async-done | bytes 294944 | tf_op jit(solution)/shard_map/all_to_all | solution.py:392
  26.8 11.9 %physics.1 = f32[288,128]{1,0:T(8,128)S(1)} custom-call(f32[576,128]{1,0:T(8,128)S(1)} %bitcast.7, f32[512,256]{1,0:T(8,128)S(1)} %get-tuple-element.31.refs_0_, f32[512,256]{1,0:T(8,128)S(1)} %get-tuple-element.32.refs_1_, f32[512,256]{1,0:T(8,128)S(1)} %get-tuple-element.33.refs_2_, bf16[256,256]{1,0:T(8,128)(2,1)S(1)} %get-tuple-element.34.refs_3_, ...), custom_call_target="tpu_custom_call" | custom-call | tf_op jit(solution)/shard_map/physics/pallas_call | solution.py:413
  38.7 11.0 %all_to_all.18 = f32[32,1,1152]{2,1,0:T(1,128)S(1)} all-to-all(f32[32,1,1152]{2,1,0:T(1,128)S(1)} %bitcast.8), channel_id=1, replica_groups=mesh['sec'=4,'blk'=8] {'sec','blk'}, dimensions={0} | all-to-all | bytes 294912 | tf_op jit(solution)/shard_map/all_to_all | solution.py:430
  49.7 0.9 %finish.1 = f32[144,128]{1,0:T(8,128)} custom-call(f32[144,128]{1,0:T(8,128)S(1)} %get-tuple-element.28.dyn_ref, s32[3,128]{1,0:T(4,128)S(1)} %get-tuple-element.29.place_ref, f32[288,128]{1,0:T(8,128)S(1)} %bitcast.9), custom_call_target="tpu_custom_call" | custom-call | tf_op jit(solution)/shard_map/finish/pallas_call | solution.py:431
Async XLA Ops:
  0.0 0.9 %copy-start = (f32[2,72,128]{2,1,0:T(8,128)S(1)}, f32[2,72,128]{2,1,0:T(8,128)}, u32[]{:S(2)}) copy-start(f32[2,72,128]{2,1,0:T(8,128)} %param.5) | copy-start | bytes 221188
  1.0 8.4 %collective-permute-start = (f32[8,144]{1,0:T(8,128)S(1)}, f32[8,144]{1,0:T(8,128)S(1)}, u32[]{:S(2)}, u32[]{:S(2)}) collective-permute-start(f32[8,144]{1,0:T(8,128)S(1)} %get-tuple-element.26), channel_id=1, source_target_pairs={{0,31},{1,2},{2,1},{3,4},{4,3},{5,6},{6,5},{7,8},{8,7},{9,10},{10,... | collective-permute-start | bytes 13832 | tf_op jit(solution)/shard_map/ppermute | solution.py:364
  7.4 2.0 %collective-permute-start.1 = (f32[8,144]{1,0:T(8,128)S(1)}, f32[8,144]{1,0:T(8,128)S(1)}, u32[]{:S(2)}, u32[]{:S(2)}) collective-permute-start(f32[8,144]{1,0:T(8,128)S(1)} %get-tuple-element.27), channel_id=1, source_target_pairs={{0,1},{1,0},{2,3},{3,2},{4,5},{5,4},{6,7},{7,6},{8,9},{9,8},{10,11... | collective-permute-start | bytes 13832 | tf_op jit(solution)/shard_map/ppermute | solution.py:365
  7.5 0.7 %copy-start.1 = (s32[4,128]{1,0:T(4,128)S(1)}, s32[4,128]{1,0:T(4,128)}, u32[]{:S(2)}) copy-start(s32[4,128]{1,0:T(4,128)} %near_ref.1) | copy-start | bytes 6148
  8.1 0.7 %copy-start.2 = (s32[128,1]{0,1:T(1,128)S(1)}, s32[128,1]{0,1:T(1,128)}, u32[]{:S(2)}) copy-start(s32[128,1]{0,1:T(1,128)} %param.7) | copy-start | bytes 1540
  10.4 16.4 %all-to-all-start = ((f32[32,1,2304]{2,1,0:T(1,128)}), f32[32,1,2304]{2,1,0:T(1,128)S(1)}, u32[]{:S(2)}, u32[]{:S(2)}) async-start(f32[32,1,2304]{2,1,0:T(1,128)} %bitcast.2), calls=%async_computation | async-start | bytes 589824 | tf_op jit(solution)/shard_map/all_to_all | solution.py:392

commit v9 on v8

--- a/solution.py
+++ b/solution.py
@@ -20,7 +20,7 @@
 TN = (((0,), (0,)), ((), ()))
 VMEM = pl.BlockSpec(memory_space=pltpu.VMEM)
 LOG = 0.3 * math.log2(math.e)
-TRIO = 3
+PREP = 24
 HEAD = 8
 
 
@@ -144,25 +144,30 @@
     return lax.dot_general(first, source, NT, preferred_element_type=F32)
 
 
-def prepare_kernel(crmx, mask_ref, ct_ref, cm_ref, rate_ref, both_ref, *head_refs):
+def prepare_kernel(crmx, mask_ref, ct_ref, cm_ref, rate_ref, both_ref, *refs):
+    yt_ref, ym_ref, head_rate_ref, first_ref, move_ref = refs
     per = GROUP * crmx
-    move = near_matrix(per, per, crmx, 1.0, 0.0).astype(BF16)
-    for q in range(mask_ref.shape[1] // per):
-        part = slice(q * per, (q + 1) * per)
-        ice = lax.dot_general(move, mask_ref[:, part].astype(F32).astype(BF16), NT, preferred_element_type=F32)
-        rate_ref[part, :] = 0.7 - 0.4 * ice
-        both_ref[part, :] = 0.7 - 0.31 * ice
+    size = yt_ref.shape[0]
 
     @pl.when(pl.program_id(0) == 0)
     def _():
-        yt_ref, ym_ref, head_rate_ref, first_ref = head_refs
-        size = yt_ref.shape[0]
+        move_ref[...] = near_matrix(per, per, crmx, 1.0, 0.0).astype(BF16)
         first = near_matrix(per, per, crmx, 3.0, 1.0).astype(BF16)
         first_ref[...] = first
         for q in range(size // per):
             part = slice(q * per, (q + 1) * per)
             yt_ref[part, :] = diffusion(first, ct_ref[:, part])
             ym_ref[part, :] = diffusion(first, cm_ref[:, part])
+
+    for q in range(mask_ref.shape[1] // per):
+        part = slice(q * per, (q + 1) * per)
+        ice = mask_ref[:, part].astype(F32).astype(BF16)
+        ice = lax.dot_general(move_ref[...], ice, NT, preferred_element_type=F32)
+        rate_ref[part, :] = 0.7 - 0.4 * ice
+        both_ref[part, :] = 0.7 - 0.31 * ice
+
+    @pl.when(pl.program_id(0) == 0)
+    def _():
         head_rate_ref[...] = rate_ref[:size]
 
 
@@ -392,7 +397,7 @@
     arrived = lax.all_to_all(outgoing.reshape(ndev, cap * 2 * rows), AXES, split_axis=0, concat_axis=0, tiled=True)
     arrived = arrived.reshape(outgoing.shape)
 
-    block = TRIO * GROUP * crmx
+    block = PREP * crmx
     count = levels * crmx // block
     take = lambda offset: pl.BlockSpec((slots, block), lambda g: (0, g + offset))
     rates_spec = [pl.BlockSpec((block, slots), lambda g: (g, 0))] * 2
@@ -405,6 +410,7 @@
         in_specs=[take(0)] + [pl.BlockSpec((slots, size), lambda g, i=i: (0, i * offset)) for i in range(2)],
         out_specs=rates_spec + [VMEM] * 4,
         out_shape=[field] * 2 + [coef] * 3 + [sds((GROUP * crmx, GROUP * crmx), BF16)],
+        scratch_shapes=[pltpu.VMEM((GROUP * crmx, GROUP * crmx), BF16)],
         compiler_params=pltpu.CompilerParams(vmem_limit_bytes=53000 << 10),
         cost_estimate=pl.CostEstimate(flops=2 * slots * levels * crmx * GROUP * crmx, transcendentals=0, bytes_accessed=6 * slots * wide),
         name="prepare",

time: 51 us -> 50.3 us (0.986)
  waiting for transfers between devices: 3.01 us -> 3.84 us
  Pallas kernels: 22.8 us -> 22 us
  blocking collectives: 11 us -> 10.4 us
    all_to_all x1, waiting for transfers between devices: 3.01 us -> 3.84 us  [local(): lax.all_to_all(outgoing.reshape(ndev, cap * 2 * rows), AXES, split_axis=0...]
    pallas_call x1, Pallas kernels: 8.31 us -> 7.48 us  [local(): pl.pallas_call(functools.partial(prepare_kernel, crmx), grid=(count,), in...]
    all_to_all x1, blocking collectives: 11 us -> 10.4 us  [local(): lax.all_to_all(back.reshape(ndev, cap * rows), AXES, split_axis=0, concat...]
  transfers between devices with their start and end apart: 3 -> 3, of which waited for: 1 -> 1; matrix products, arithmetic and copies ran while one was open for 0% -> 0% of each run, Pallas kernels for 18% -> 16%
where the time goes in v9:
time: 50.3 us; the launch traced here: 50 us
  Pallas kernels  22 us (44%)
  starting transfers between devices  11.5 us (23%)
  blocking collectives  10.4 us (21%)
  waiting for transfers between devices  3.84 us (8%)
  local copies, waits for them, and re-layouts  2.22 us (4%)
    pallas_call x1, Pallas kernels, local(): pl.pallas_call(functools.partial(physics_kernel, levels, crmx, dense), in...  11.9 us
    all_to_all x1, blocking collectives, local(): lax.all_to_all(back.reshape(ndev, cap * rows), AXES, split_axis=0, concat...  10.4 us
    pallas_call x1, Pallas kernels, local(): pl.pallas_call(functools.partial(prepare_kernel, crmx), grid=(count,), in...  7.48 us
    ppermute x1, starting transfers between devices, local(): from_far = lax.ppermute(to_far, AXES, far)  6.47 us
    all_to_all x1, starting transfers between devices, local(): lax.all_to_all(outgoing.reshape(ndev, cap * 2 * rows), AXES, split_axis=0...  5.04 us
    all_to_all x1, waiting for transfers between devices, local(): lax.all_to_all(outgoing.reshape(ndev, cap * 2 * rows), AXES, split_axis=0...  3.84 us
    unnamed x6, local copies, waits for them, and re-layouts  2.22 us
  transfers between devices with their start and end apart: 3, of which 1 were waited for; matrix products, arithmetic and copies ran while one was open for 0% of the time, Pallas kernels for 16%

profile of v9, /device:TPU:0, one launch (start us, length us, event | category | flops | bytes accessed | tf_op | source)
XLA Modules:
  0.0 50.0 jit_solution(6146409950574691953)
XLA Ops:
  0.0 0.0 copy-start
  0.0 0.9 %copy-done = f32[2,72,128]{2,1,0:T(8,128)S(1)} copy-done((f32[2,72,128]{2,1,0:T(8,128)S(1)}, f32[2,72,128]{2,1,0:T(8,128)}, u32[]{:S(2)}) %copy-start) | copy-done | bytes 73752
  0.9 0.1 edges.1
  1.0 6.5 %collective-permute-start = (f32[8,144]{1,0:T(8,128)S(1)}, f32[8,144]{1,0:T(8,128)S(1)}, u32[]{:S(2)}, u32[]{:S(2)}) collective-permute-start(f32[8,144]{1,0:T(8,128)S(1)} %get-tuple-element.26), channel_id=1, source_target_pairs={{0,31},{1,2},{2,1},{3,4},{4,3},{5,6},{6,5},{7,8},{8,7},{9,10},{10,... | collective-permute-start | bytes 13832 | tf_op jit(solution)/shard_map/ppermute | solution.py:369
  7.4 0.0 collective-permute-start.1
  7.5 0.0 copy-start.1
  7.5 0.7 %copy-done.1 = s32[4,128]{1,0:T(4,128)S(1)} copy-done((s32[4,128]{1,0:T(4,128)S(1)}, s32[4,128]{1,0:T(4,128)}, u32[]{:S(2)}) %copy-start.1) | copy-done | bytes 2072
  8.1 0.0 copy-start.2
  8.1 0.7 %copy-done.2 = s32[128,1]{0,1:T(1,128)S(1)} copy-done((s32[128,1]{0,1:T(1,128)S(1)}, s32[128,1]{0,1:T(1,128)}, u32[]{:S(2)}) %copy-start.2) | copy-done | bytes 536
  8.8 0.6 %index.1 = (f32[576,128]{1,0:T(8,128)S(1)}, f32[144,128]{1,0:T(8,128)S(1)}, bf16[16,128]{1,0:T(8,128)(2,1)S(1)}, bf16[576,32]{1,0:T(8,128)(2,1)S(1)}, s32[3,128]{1,0:T(4,128)S(1)}) custom-call(f32[144,128]{1,0:T(8,128)S(1)} %get-tuple-element.21.state_ref, s32[4,128]{1,0:T(4,128)S(1)} %copy-done.1, s32[1,128]{1,0:T(1,128)S(1)} %bitcast.11), custom_call_target="tpu_custom_call" | custom-call | tf_op jit(solution)/shard_map/index/pallas_call | solution.py:374
  9.4 0.0 collective-permute-done.far_ref
  9.4 0.0 collective-permute-done.1.mate_ref
  9.4 1.0 %pack.1 = (f32[576,128]{1,0:T(8,128)}, f32[144,128]{1,0:T(8,128)S(1)}) custom-call(f32[576,128]{1,0:T(8,128)S(1)} %get-tuple-element.22.base_ref, f32[144,128]{1,0:T(8,128)S(1)} %get-tuple-element.23.part_ref, bf16[16,128]{1,0:T(8,128)(2,1)S(1)} %get-tuple-element.24.edge_ref, bf16[576,32]{1,0:T(8,128)(2,1)S(1)} %get-tuple-element.25.share_ref, ...), custom_call_target="tpu_custom_call" | custom-call | tf_op jit(solution)/shard_map/pack/pallas_call | solution.py:388
  10.4 5.0 %all-to-all-start = ((f32[32,1,2304]{2,1,0:T(1,128)}), f32[32,1,2304]{2,1,0:T(1,128)S(1)}, u32[]{:S(2)}, u32[]{:S(2)}) async-start(f32[32,1,2304]{2,1,0:T(1,128)} %bitcast.2), calls=%async_computation | async-start | bytes 589824 | tf_op jit(solution)/shard_map/all_to_all | solution.py:397
  15.5 7.5 %prepare.1 = (f32[4608,256]{1,0:T(8,128)}, f32[4608,256]{1,0:T(8,128)}, f32[512,256]{1,0:T(8,128)S(1)}, f32[512,256]{1,0:T(8,128)S(1)}, f32[512,256]{1,0:T(8,128)S(1)}, /*index=5*/bf16[256,256]{1,0:T(8,128)(2,1)S(1)}) custom-call(s32[256,4608]{1,0:T(8,128)} %mask_ref.1, bf16[256,9216]{1,0:T(8,128)(2,1)} %refs_4_.1, bf16[256,9216]{1,0:T(8,128)(2,1)} %refs_4_.1), custom_call_target="tpu_custom_call" | custom-call | flops 603979776 | bytes 14155776 | tf_op jit(solution)/shard_map/prepare/pallas_call | solution.py:407
  23.0 3.8 %all-to-all-done = f32[32,1,2304]{2,1,0:T(1,128)S(1)} async-done(((f32[32,1,2304]{2,1,0:T(1,128)}), f32[32,1,2304]{2,1,0:T(1,128)S(1)}, u32[]{:S(2)}, u32[]{:S(2)}) %all-to-all-start) | async-done | bytes 294944 | tf_op jit(solution)/shard_map/all_to_all | solution.py:397
  26.8 11.9 %physics.1 = f32[288,128]{1,0:T(8,128)S(1)} custom-call(f32[576,128]{1,0:T(8,128)S(1)} %bitcast.7, f32[512,256]{1,0:T(8,128)S(1)} %get-tuple-element.31.refs_0_, f32[512,256]{1,0:T(8,128)S(1)} %get-tuple-element.32.refs_1_, f32[512,256]{1,0:T(8,128)S(1)} %get-tuple-element.33.refs_2_, bf16[256,256]{1,0:T(8,128)(2,1)S(1)} %get-tuple-element.34.refs_3_, ...), custom_call_target="tpu_custom_call" | custom-call | tf_op jit(solution)/shard_map/physics/pallas_call | solution.py:419
  38.7 10.4 %all_to_all.18 = f32[32,1,1152]{2,1,0:T(1,128)S(1)} all-to-all(f32[32,1,1152]{2,1,0:T(1,128)S(1)} %bitcast.8), channel_id=1, replica_groups=mesh['sec'=4,'blk'=8] {'sec','blk'}, dimensions={0} | all-to-all | bytes 294912 | tf_op jit(solution)/shard_map/all_to_all | solution.py:436
  49.1 0.9 %finish.1 = f32[144,128]{1,0:T(8,128)} custom-call(f32[144,128]{1,0:T(8,128)S(1)} %get-tuple-element.28.dyn_ref, s32[3,128]{1,0:T(4,128)S(1)} %get-tuple-element.29.place_ref, f32[288,128]{1,0:T(8,128)S(1)} %bitcast.9), custom_call_target="tpu_custom_call" | custom-call | tf_op jit(solution)/shard_map/finish/pallas_call | solution.py:437
Async XLA Ops:
  0.0 0.9 %copy-start = (f32[2,72,128]{2,1,0:T(8,128)S(1)}, f32[2,72,128]{2,1,0:T(8,128)}, u32[]{:S(2)}) copy-start(f32[2,72,128]{2,1,0:T(8,128)} %param.5) | copy-start | bytes 221188
  1.0 8.4 %collective-permute-start = (f32[8,144]{1,0:T(8,128)S(1)}, f32[8,144]{1,0:T(8,128)S(1)}, u32[]{:S(2)}, u32[]{:S(2)}) collective-permute-start(f32[8,144]{1,0:T(8,128)S(1)} %get-tuple-element.26), channel_id=1, source_target_pairs={{0,31},{1,2},{2,1},{3,4},{4,3},{5,6},{6,5},{7,8},{8,7},{9,10},{10,... | collective-permute-start | bytes 13832 | tf_op jit(solution)/shard_map/ppermute | solution.py:369
  7.4 2.0 %collective-permute-start.1 = (f32[8,144]{1,0:T(8,128)S(1)}, f32[8,144]{1,0:T(8,128)S(1)}, u32[]{:S(2)}, u32[]{:S(2)}) collective-permute-start(f32[8,144]{1,0:T(8,128)S(1)} %get-tuple-element.27), channel_id=1, source_target_pairs={{0,1},{1,0},{2,3},{3,2},{4,5},{5,4},{6,7},{7,6},{8,9},{9,8},{10,11... | collective-permute-start | bytes 13832 | tf_op jit(solution)/shard_map/ppermute | solution.py:370
  7.5 0.7 %copy-start.1 = (s32[4,128]{1,0:T(4,128)S(1)}, s32[4,128]{1,0:T(4,128)}, u32[]{:S(2)}) copy-start(s32[4,128]{1,0:T(4,128)} %near_ref.1) | copy-start | bytes 6148
  8.1 0.7 %copy-start.2 = (s32[128,1]{0,1:T(1,128)S(1)}, s32[128,1]{0,1:T(1,128)}, u32[]{:S(2)}) copy-start(s32[128,1]{0,1:T(1,128)} %param.7) | copy-start | bytes 1540
  10.4 16.4 %all-to-all-start = ((f32[32,1,2304]{2,1,0:T(1,128)}), f32[32,1,2304]{2,1,0:T(1,128)S(1)}, u32[]{:S(2)}, u32[]{:S(2)}) async-start(f32[32,1,2304]{2,1,0:T(1,128)} %bitcast.2), calls=%async_computation | async-start | bytes 589824 | tf_op jit(solution)/shard_map/all_to_all | solution.py:397

commit v10 on v9

--- a/solution.py
+++ b/solution.py
@@ -237,7 +237,7 @@
                 cut = slice(q * part, (q + 1) * part)
                 ref[cut, :] = diffusion(first_ref[...], source[group - 1, :, cut])
 
-    for group in range(1, count):
+    for group in (1, 2):
         start(crm_copies(group))
         start(rate_copies(group))
     arrived = arrivals(dense, arrived_ref, slots, 4 * levels)
@@ -275,21 +275,28 @@
                 field = [a + b for a, b in zip(field[0::2], field[1::2])]
             sums_ref[half, pl.ds(pl.multiple_of((i * levels + level) * 8, 8), 8), :] = field[0]
 
-    def run(group, sources):
-        for inner in range(here):
+    def run(group, sources, levels_of_group):
+        for inner in levels_of_group:
             for half in range(halves):
                 unit(group, inner, half, sources)
 
     head[3][...] = 0.7 - 0.775 * (0.7 - head[2][...])
+    run(0, head, range(here // 2))
     wait(crm_copies(1))
     diffuse(1, 0)
-    run(0, head)
+    run(0, head, range(here // 2, here))
 
     @pl.loop(0, (count - 1) // 2)
     def _(trip):
         for k in range(2):
             group = 1 + 2 * trip + k
             ahead = jnp.minimum(group + 1, count - 1)
+
+            @pl.when(group + 2 < count)
+            def _():
+                start(crm_copies(group + 2))
+                start(rate_copies(group + 2))
+
             wait(rate_copies(group))
             if k == 0:
                 wait(crm_copies(ahead))
@@ -298,7 +305,7 @@
                 def _():
                     wait(crm_copies(group + 1))
             diffuse(ahead, 1 - k)
-            run(group, (*fields[k], coefs[0].at[group - 1], coefs[1].at[group - 1]))
+            run(group, (*fields[k], coefs[0].at[group - 1], coefs[1].at[group - 1]), range(here))
 
     total = 2 * levels
     for half in range(halves):

time: 50.3 us -> 50.8 us (level)
  no operation moved by 1% of the time
where the time goes in v10:
time: 50.8 us; the launch traced here: 50.5 us
  Pallas kernels  22.4 us (44%)
  starting transfers between devices  11.5 us (23%)
  blocking collectives  10.4 us (20%)
  waiting for transfers between devices  3.84 us (8%)
  local copies, waits for them, and re-layouts  2.22 us (4%)
    pallas_call x1, Pallas kernels, local(): pl.pallas_call(functools.partial(physics_kernel, levels, crmx, dense), in...  12.3 us
    all_to_all x1, blocking collectives, local(): lax.all_to_all(back.reshape(ndev, cap * rows), AXES, split_axis=0, concat...  10.4 us
    pallas_call x1, Pallas kernels, local(): pl.pallas_call(functools.partial(prepare_kernel, crmx), grid=(count,), in...  7.48 us
    ppermute x1, starting transfers between devices, local(): from_far = lax.ppermute(to_far, AXES, far)  6.47 us
    all_to_all x1, starting transfers between devices, local(): lax.all_to_all(outgoing.reshape(ndev, cap * 2 * rows), AXES, split_axis=0...  5.04 us
    all_to_all x1, waiting for transfers between devices, local(): lax.all_to_all(outgoing.reshape(ndev, cap * 2 * rows), AXES, split_axis=0...  3.84 us
    unnamed x6, local copies, waits for them, and re-layouts  2.22 us
  transfers between devices with their start and end apart: 3, of which 1 were waited for; matrix products, arithmetic and copies ran while one was open for 0% of the time, Pallas kernels for 16%

profile of v10, /device:TPU:0, one launch (start us, length us, event | category | flops | bytes accessed | tf_op | source)
XLA Modules:
  0.0 50.5 jit_solution(13176394660969514167)
XLA Ops:
  0.0 0.0 copy-start
  0.0 0.9 %copy-done = f32[2,72,128]{2,1,0:T(8,128)S(1)} copy-done((f32[2,72,128]{2,1,0:T(8,128)S(1)}, f32[2,72,128]{2,1,0:T(8,128)}, u32[]{:S(2)}) %copy-start) | copy-done | bytes 73752
  0.9 0.1 edges.1
  1.0 6.5 %collective-permute-start = (f32[8,144]{1,0:T(8,128)S(1)}, f32[8,144]{1,0:T(8,128)S(1)}, u32[]{:S(2)}, u32[]{:S(2)}) collective-permute-start(f32[8,144]{1,0:T(8,128)S(1)} %get-tuple-element.26), channel_id=1, source_target_pairs={{0,31},{1,2},{2,1},{3,4},{4,3},{5,6},{6,5},{7,8},{8,7},{9,10},{10,... | collective-permute-start | bytes 13832 | tf_op jit(solution)/shard_map/ppermute | solution.py:376
  7.4 0.0 collective-permute-start.1
  7.5 0.0 copy-start.1
  7.5 0.7 %copy-done.1 = s32[4,128]{1,0:T(4,128)S(1)} copy-done((s32[4,128]{1,0:T(4,128)S(1)}, s32[4,128]{1,0:T(4,128)}, u32[]{:S(2)}) %copy-start.1) | copy-done | bytes 2072
  8.1 0.0 copy-start.2
  8.1 0.7 %copy-done.2 = s32[128,1]{0,1:T(1,128)S(1)} copy-done((s32[128,1]{0,1:T(1,128)S(1)}, s32[128,1]{0,1:T(1,128)}, u32[]{:S(2)}) %copy-start.2) | copy-done | bytes 536
  8.8 0.6 %index.1 = (f32[576,128]{1,0:T(8,128)S(1)}, f32[144,128]{1,0:T(8,128)S(1)}, bf16[16,128]{1,0:T(8,128)(2,1)S(1)}, bf16[576,32]{1,0:T(8,128)(2,1)S(1)}, s32[3,128]{1,0:T(4,128)S(1)}) custom-call(f32[144,128]{1,0:T(8,128)S(1)} %get-tuple-element.21.state_ref, s32[4,128]{1,0:T(4,128)S(1)} %copy-done.1, s32[1,128]{1,0:T(1,128)S(1)} %bitcast.11), custom_call_target="tpu_custom_call" | custom-call | tf_op jit(solution)/shard_map/index/pallas_call | solution.py:381
  9.4 0.0 collective-permute-done.far_ref
  9.4 0.0 collective-permute-done.1.mate_ref
  9.4 1.0 %pack.1 = (f32[576,128]{1,0:T(8,128)}, f32[144,128]{1,0:T(8,128)S(1)}) custom-call(f32[576,128]{1,0:T(8,128)S(1)} %get-tuple-element.22.base_ref, f32[144,128]{1,0:T(8,128)S(1)} %get-tuple-element.23.part_ref, bf16[16,128]{1,0:T(8,128)(2,1)S(1)} %get-tuple-element.24.edge_ref, bf16[576,32]{1,0:T(8,128)(2,1)S(1)} %get-tuple-element.25.share_ref, ...), custom_call_target="tpu_custom_call" | custom-call | tf_op jit(solution)/shard_map/pack/pallas_call | solution.py:395
  10.4 5.0 %all-to-all-start = ((f32[32,1,2304]{2,1,0:T(1,128)}), f32[32,1,2304]{2,1,0:T(1,128)S(1)}, u32[]{:S(2)}, u32[]{:S(2)}) async-start(f32[32,1,2304]{2,1,0:T(1,128)} %bitcast.2), calls=%async_computation | async-start | bytes 589824 | tf_op jit(solution)/shard_map/all_to_all | solution.py:404
  15.5 7.5 %prepare.1 = (f32[4608,256]{1,0:T(8,128)}, f32[4608,256]{1,0:T(8,128)}, f32[512,256]{1,0:T(8,128)S(1)}, f32[512,256]{1,0:T(8,128)S(1)}, f32[512,256]{1,0:T(8,128)S(1)}, /*index=5*/bf16[256,256]{1,0:T(8,128)(2,1)S(1)}) custom-call(s32[256,4608]{1,0:T(8,128)} %mask_ref.1, bf16[256,9216]{1,0:T(8,128)(2,1)} %refs_4_.1, bf16[256,9216]{1,0:T(8,128)(2,1)} %refs_4_.1), custom_call_target="tpu_custom_call" | custom-call | flops 603979776 | bytes 14155776 | tf_op jit(solution)/shard_map/prepare/pallas_call | solution.py:414
  23.0 3.8 %all-to-all-done = f32[32,1,2304]{2,1,0:T(1,128)S(1)} async-done(((f32[32,1,2304]{2,1,0:T(1,128)}), f32[32,1,2304]{2,1,0:T(1,128)S(1)}, u32[]{:S(2)}, u32[]{:S(2)}) %all-to-all-start) | async-done | bytes 294944 | tf_op jit(solution)/shard_map/all_to_all | solution.py:404
  26.8 12.3 %physics.1 = f32[288,128]{1,0:T(8,128)S(1)} custom-call(f32[576,128]{1,0:T(8,128)S(1)} %bitcast.7, f32[512,256]{1,0:T(8,128)S(1)} %get-tuple-element.31.refs_0_, f32[512,256]{1,0:T(8,128)S(1)} %get-tuple-element.32.refs_1_, f32[512,256]{1,0:T(8,128)S(1)} %get-tuple-element.33.refs_2_, bf16[256,256]{1,0:T(8,128)(2,1)S(1)} %get-tuple-element.34.refs_3_, ...), custom_call_target="tpu_custom_call" | custom-call | tf_op jit(solution)/shard_map/physics/pallas_call | solution.py:426
  39.1 10.4 %all_to_all.18 = f32[32,1,1152]{2,1,0:T(1,128)S(1)} all-to-all(f32[32,1,1152]{2,1,0:T(1,128)S(1)} %bitcast.8), channel_id=1, replica_groups=mesh['sec'=4,'blk'=8] {'sec','blk'}, dimensions={0} | all-to-all | bytes 294912 | tf_op jit(solution)/shard_map/all_to_all | solution.py:443
  49.5 0.9 %finish.1 = f32[144,128]{1,0:T(8,128)} custom-call(f32[144,128]{1,0:T(8,128)S(1)} %get-tuple-element.28.dyn_ref, s32[3,128]{1,0:T(4,128)S(1)} %get-tuple-element.29.place_ref, f32[288,128]{1,0:T(8,128)S(1)} %bitcast.9), custom_call_target="tpu_custom_call" | custom-call | tf_op jit(solution)/shard_map/finish/pallas_call | solution.py:444
Async XLA Ops:
  0.0 0.9 %copy-start = (f32[2,72,128]{2,1,0:T(8,128)S(1)}, f32[2,72,128]{2,1,0:T(8,128)}, u32[]{:S(2)}) copy-start(f32[2,72,128]{2,1,0:T(8,128)} %param.5) | copy-start | bytes 221188
  1.0 8.4 %collective-permute-start = (f32[8,144]{1,0:T(8,128)S(1)}, f32[8,144]{1,0:T(8,128)S(1)}, u32[]{:S(2)}, u32[]{:S(2)}) collective-permute-start(f32[8,144]{1,0:T(8,128)S(1)} %get-tuple-element.26), channel_id=1, source_target_pairs={{0,31},{1,2},{2,1},{3,4},{4,3},{5,6},{6,5},{7,8},{8,7},{9,10},{10,... | collective-permute-start | bytes 13832 | tf_op jit(solution)/shard_map/ppermute | solution.py:376
  7.4 2.0 %collective-permute-start.1 = (f32[8,144]{1,0:T(8,128)S(1)}, f32[8,144]{1,0:T(8,128)S(1)}, u32[]{:S(2)}, u32[]{:S(2)}) collective-permute-start(f32[8,144]{1,0:T(8,128)S(1)} %get-tuple-element.27), channel_id=1, source_target_pairs={{0,1},{1,0},{2,3},{3,2},{4,5},{5,4},{6,7},{7,6},{8,9},{9,8},{10,11... | collective-permute-start | bytes 13832 | tf_op jit(solution)/shard_map/ppermute | solution.py:377
  7.5 0.7 %copy-start.1 = (s32[4,128]{1,0:T(4,128)S(1)}, s32[4,128]{1,0:T(4,128)}, u32[]{:S(2)}) copy-start(s32[4,128]{1,0:T(4,128)} %near_ref.1) | copy-start | bytes 6148
  8.1 0.7 %copy-start.2 = (s32[128,1]{0,1:T(1,128)S(1)}, s32[128,1]{0,1:T(1,128)}, u32[]{:S(2)}) copy-start(s32[128,1]{0,1:T(1,128)} %param.7) | copy-start | bytes 1540
  10.4 16.4 %all-to-all-start = ((f32[32,1,2304]{2,1,0:T(1,128)}), f32[32,1,2304]{2,1,0:T(1,128)S(1)}, u32[]{:S(2)}, u32[]{:S(2)}) async-start(f32[32,1,2304]{2,1,0:T(1,128)} %bitcast.2), calls=%async_computation | async-start | bytes 589824 | tf_op jit(solution)/shard_map/all_to_all | solution.py:404

commit v11 on v9

--- a/solution.py
+++ b/solution.py
@@ -275,15 +275,16 @@
                 field = [a + b for a, b in zip(field[0::2], field[1::2])]
             sums_ref[half, pl.ds(pl.multiple_of((i * levels + level) * 8, 8), 8), :] = field[0]
 
-    def run(group, sources):
-        for inner in range(here):
+    def run(group, sources, inners):
+        for inner in inners:
             for half in range(halves):
                 unit(group, inner, half, sources)
 
     head[3][...] = 0.7 - 0.775 * (0.7 - head[2][...])
+    run(0, head, range(here // 2))
     wait(crm_copies(1))
     diffuse(1, 0)
-    run(0, head)
+    run(0, head, range(here // 2, here))
 
     @pl.loop(0, (count - 1) // 2)
     def _(trip):
@@ -298,7 +299,7 @@
                 def _():
                     wait(crm_copies(group + 1))
             diffuse(ahead, 1 - k)
-            run(group, (*fields[k], coefs[0].at[group - 1], coefs[1].at[group - 1]))
+            run(group, (*fields[k], coefs[0].at[group - 1], coefs[1].at[group - 1]), range(here))
 
     total = 2 * levels
     for half in range(halves):

time: 50.3 us -> 49.9 us (level)
  no operation moved by 1% of the time
where the time goes in v11:
time: 49.9 us; the launch traced here: 49.6 us
  Pallas kernels  21.6 us (43%)
  starting transfers between devices  11.5 us (23%)
  blocking collectives  10.4 us (21%)
  waiting for transfers between devices  3.84 us (8%)
  local copies, waits for them, and re-layouts  2.22 us (4%)
    pallas_call x1, Pallas kernels, local(): pl.pallas_call(functools.partial(physics_kernel, levels, crmx, dense), in...  11.4 us
    all_to_all x1, blocking collectives, local(): lax.all_to_all(back.reshape(ndev, cap * rows), AXES, split_axis=0, concat...  10.4 us
    pallas_call x1, Pallas kernels, local(): pl.pallas_call(functools.partial(prepare_kernel, crmx), grid=(count,), in...  7.48 us
    ppermute x1, starting transfers between devices, local(): from_far = lax.ppermute(to_far, AXES, far)  6.47 us
    all_to_all x1, starting transfers between devices, local(): lax.all_to_all(outgoing.reshape(ndev, cap * 2 * rows), AXES, split_axis=0...  5.04 us
    all_to_all x1, waiting for transfers between devices, local(): lax.all_to_all(outgoing.reshape(ndev, cap * 2 * rows), AXES, split_axis=0...  3.84 us
    unnamed x6, local copies, waits for them, and re-layouts  2.22 us
  transfers between devices with their start and end apart: 3, of which 1 were waited for; matrix products, arithmetic and copies ran while one was open for 0% of the time, Pallas kernels for 16%

profile of v11, /device:TPU:0, one launch (start us, length us, event | category | flops | bytes accessed | tf_op | source)
XLA Modules:
  0.0 49.6 jit_solution(2913998104431704868)
XLA Ops:
  0.0 0.0 copy-start
  0.0 0.9 %copy-done = f32[2,72,128]{2,1,0:T(8,128)S(1)} copy-done((f32[2,72,128]{2,1,0:T(8,128)S(1)}, f32[2,72,128]{2,1,0:T(8,128)}, u32[]{:S(2)}) %copy-start) | copy-done | bytes 73752
  0.9 0.1 edges.1
  1.0 6.5 %collective-permute-start = (f32[8,144]{1,0:T(8,128)S(1)}, f32[8,144]{1,0:T(8,128)S(1)}, u32[]{:S(2)}, u32[]{:S(2)}) collective-permute-start(f32[8,144]{1,0:T(8,128)S(1)} %get-tuple-element.26), channel_id=1, source_target_pairs={{0,31},{1,2},{2,1},{3,4},{4,3},{5,6},{6,5},{7,8},{8,7},{9,10},{10,... | collective-permute-start | bytes 13832 | tf_op jit(solution)/shard_map/ppermute | solution.py:370
  7.4 0.0 collective-permute-start.1
  7.5 0.0 copy-start.1
  7.5 0.7 %copy-done.1 = s32[4,128]{1,0:T(4,128)S(1)} copy-done((s32[4,128]{1,0:T(4,128)S(1)}, s32[4,128]{1,0:T(4,128)}, u32[]{:S(2)}) %copy-start.1) | copy-done | bytes 2072
  8.1 0.0 copy-start.2
  8.1 0.7 %copy-done.2 = s32[128,1]{0,1:T(1,128)S(1)} copy-done((s32[128,1]{0,1:T(1,128)S(1)}, s32[128,1]{0,1:T(1,128)}, u32[]{:S(2)}) %copy-start.2) | copy-done | bytes 536
  8.8 0.6 %index.1 = (f32[576,128]{1,0:T(8,128)S(1)}, f32[144,128]{1,0:T(8,128)S(1)}, bf16[16,128]{1,0:T(8,128)(2,1)S(1)}, bf16[576,32]{1,0:T(8,128)(2,1)S(1)}, s32[3,128]{1,0:T(4,128)S(1)}) custom-call(f32[144,128]{1,0:T(8,128)S(1)} %get-tuple-element.21.state_ref, s32[4,128]{1,0:T(4,128)S(1)} %copy-done.1, s32[1,128]{1,0:T(1,128)S(1)} %bitcast.11), custom_call_target="tpu_custom_call" | custom-call | tf_op jit(solution)/shard_map/index/pallas_call | solution.py:375
  9.4 0.0 collective-permute-done.far_ref
  9.4 0.0 collective-permute-done.1.mate_ref
  9.4 1.0 %pack.1 = (f32[576,128]{1,0:T(8,128)}, f32[144,128]{1,0:T(8,128)S(1)}) custom-call(f32[576,128]{1,0:T(8,128)S(1)} %get-tuple-element.22.base_ref, f32[144,128]{1,0:T(8,128)S(1)} %get-tuple-element.23.part_ref, bf16[16,128]{1,0:T(8,128)(2,1)S(1)} %get-tuple-element.24.edge_ref, bf16[576,32]{1,0:T(8,128)(2,1)S(1)} %get-tuple-element.25.share_ref, ...), custom_call_target="tpu_custom_call" | custom-call | tf_op jit(solution)/shard_map/pack/pallas_call | solution.py:389
  10.4 5.0 %all-to-all-start = ((f32[32,1,2304]{2,1,0:T(1,128)}), f32[32,1,2304]{2,1,0:T(1,128)S(1)}, u32[]{:S(2)}, u32[]{:S(2)}) async-start(f32[32,1,2304]{2,1,0:T(1,128)} %bitcast.2), calls=%async_computation | async-start | bytes 589824 | tf_op jit(solution)/shard_map/all_to_all | solution.py:398
  15.5 7.5 %prepare.1 = (f32[4608,256]{1,0:T(8,128)}, f32[4608,256]{1,0:T(8,128)}, f32[512,256]{1,0:T(8,128)S(1)}, f32[512,256]{1,0:T(8,128)S(1)}, f32[512,256]{1,0:T(8,128)S(1)}, /*index=5*/bf16[256,256]{1,0:T(8,128)(2,1)S(1)}) custom-call(s32[256,4608]{1,0:T(8,128)} %mask_ref.1, bf16[256,9216]{1,0:T(8,128)(2,1)} %refs_4_.1, bf16[256,9216]{1,0:T(8,128)(2,1)} %refs_4_.1), custom_call_target="tpu_custom_call" | custom-call | flops 603979776 | bytes 14155776 | tf_op jit(solution)/shard_map/prepare/pallas_call | solution.py:408
  23.0 3.8 %all-to-all-done = f32[32,1,2304]{2,1,0:T(1,128)S(1)} async-done(((f32[32,1,2304]{2,1,0:T(1,128)}), f32[32,1,2304]{2,1,0:T(1,128)S(1)}, u32[]{:S(2)}, u32[]{:S(2)}) %all-to-all-start) | async-done | bytes 294944 | tf_op jit(solution)/shard_map/all_to_all | solution.py:398
  26.8 11.4 %physics.1 = f32[288,128]{1,0:T(8,128)S(1)} custom-call(f32[576,128]{1,0:T(8,128)S(1)} %bitcast.7, f32[512,256]{1,0:T(8,128)S(1)} %get-tuple-element.31.refs_0_, f32[512,256]{1,0:T(8,128)S(1)} %get-tuple-element.32.refs_1_, f32[512,256]{1,0:T(8,128)S(1)} %get-tuple-element.33.refs_2_, bf16[256,256]{1,0:T(8,128)(2,1)S(1)} %get-tuple-element.34.refs_3_, ...), custom_call_target="tpu_custom_call" | custom-call | tf_op jit(solution)/shard_map/physics/pallas_call | solution.py:420
  38.2 10.4 %all_to_all.18 = f32[32,1,1152]{2,1,0:T(1,128)S(1)} all-to-all(f32[32,1,1152]{2,1,0:T(1,128)S(1)} %bitcast.8), channel_id=1, replica_groups=mesh['sec'=4,'blk'=8] {'sec','blk'}, dimensions={0} | all-to-all | bytes 294912 | tf_op jit(solution)/shard_map/all_to_all | solution.py:437
  48.7 0.9 %finish.1 = f32[144,128]{1,0:T(8,128)} custom-call(f32[144,128]{1,0:T(8,128)S(1)} %get-tuple-element.28.dyn_ref, s32[3,128]{1,0:T(4,128)S(1)} %get-tuple-element.29.place_ref, f32[288,128]{1,0:T(8,128)S(1)} %bitcast.9), custom_call_target="tpu_custom_call" | custom-call | tf_op jit(solution)/shard_map/finish/pallas_call | solution.py:438
Async XLA Ops:
  0.0 0.9 %copy-start = (f32[2,72,128]{2,1,0:T(8,128)S(1)}, f32[2,72,128]{2,1,0:T(8,128)}, u32[]{:S(2)}) copy-start(f32[2,72,128]{2,1,0:T(8,128)} %param.5) | copy-start | bytes 221188
  1.0 8.4 %collective-permute-start = (f32[8,144]{1,0:T(8,128)S(1)}, f32[8,144]{1,0:T(8,128)S(1)}, u32[]{:S(2)}, u32[]{:S(2)}) collective-permute-start(f32[8,144]{1,0:T(8,128)S(1)} %get-tuple-element.26), channel_id=1, source_target_pairs={{0,31},{1,2},{2,1},{3,4},{4,3},{5,6},{6,5},{7,8},{8,7},{9,10},{10,... | collective-permute-start | bytes 13832 | tf_op jit(solution)/shard_map/ppermute | solution.py:370
  7.4 2.0 %collective-permute-start.1 = (f32[8,144]{1,0:T(8,128)S(1)}, f32[8,144]{1,0:T(8,128)S(1)}, u32[]{:S(2)}, u32[]{:S(2)}) collective-permute-start(f32[8,144]{1,0:T(8,128)S(1)} %get-tuple-element.27), channel_id=1, source_target_pairs={{0,1},{1,0},{2,3},{3,2},{4,5},{5,4},{6,7},{7,6},{8,9},{9,8},{10,11... | collective-permute-start | bytes 13832 | tf_op jit(solution)/shard_map/ppermute | solution.py:371
  7.5 0.7 %copy-start.1 = (s32[4,128]{1,0:T(4,128)S(1)}, s32[4,128]{1,0:T(4,128)}, u32[]{:S(2)}) copy-start(s32[4,128]{1,0:T(4,128)} %near_ref.1) | copy-start | bytes 6148
  8.1 0.7 %copy-start.2 = (s32[128,1]{0,1:T(1,128)S(1)}, s32[128,1]{0,1:T(1,128)}, u32[]{:S(2)}) copy-start(s32[128,1]{0,1:T(1,128)} %param.7) | copy-start | bytes 1540
  10.4 16.4 %all-to-all-start = ((f32[32,1,2304]{2,1,0:T(1,128)}), f32[32,1,2304]{2,1,0:T(1,128)S(1)}, u32[]{:S(2)}, u32[]{:S(2)}) async-start(f32[32,1,2304]{2,1,0:T(1,128)} %bitcast.2), calls=%async_computation | async-start | bytes 589824 | tf_op jit(solution)/shard_map/all_to_all | solution.py:398
